TPU v7x, 32 devices: a whole 2x2x4 slice. The times are simulated.
32 devices in a mesh: grp: 2 (over y), row: 4 (over z), col: 2 (over x), sub: 2 (over core).
Axes of the slice: x: 2, y: 2, z: 4, core: 2. Of those that a mesh axis runs over, the one named last changes fastest.
Arguments:
- left_features: bfloat16 [256, 256, 128], P(('grp', 'row'), ('col', 'sub')), parts along dimension 0, may hold values from -16 to 16
- right_features: bfloat16 [256, 256, 128], P(('grp', 'row'), ('col', 'sub')), parts along dimension 0, may hold values from -16 to 16
- left_image: float32 [3, 256, 256], P(None, ('grp', 'row'), ('col', 'sub')), parts along dimension 1, may hold values from -4 to 4
- query_key: bfloat16 [128, 128], replicated, may hold values from -0.5 to 0.5
- value_weight: bfloat16 [128, 128], replicated, may hold values from -0.5 to 0.5
- out_weight: bfloat16 [128, 128], replicated, may hold values from -0.5 to 0.5
- occlusion_weight: float32 [128], replicated, may hold values from -0.5 to 0.5
- first_conv: bfloat16 [9, 64, 5], replicated, may hold values from -0.875 to 0.875
- middle_conv: bfloat16 [3, 9, 64, 64], replicated, may hold values from -0.25 to 0.25
- last_conv: bfloat16 [9, 2, 64], replicated, may hold values from -0.25 to 0.25
Outputs:
- disparity_out: float32 [256, 256], P(('grp', 'row'), ('col', 'sub')), parts along dimension 0
- occlusion_out: float32 [256, 256], P(('grp', 'row'), ('col', 'sub')), parts along dimension 0
There are 2 independent parts, one for each index of `grp`. A program takes and returns all parts, laid end to end along the dimension named above; an argument that names none is the same for every part. Nothing has to cross between parts.
All inputs are finite; a program needn't handle non-finite values.
Results may differ from a plain program's by a relative error of at most 0.0033.
Values may be sent and summed in bfloat16 or wider, within the bound.
No kernel may reach another device: no remote copies, remote signals or barrier semaphores. Data moves between devices by JAX's collectives and lax.ppermute only.
A program may use at most 64 MiB of HBM per device.

v0:
```python
import jax
import jax.numpy as jnp
from jax import lax
from jax.sharding import PartitionSpec as P

C = 128
HEADS = 8
HEAD = 16


def with_halo(cells, sides, width):
    for axis, dim in sides:
        count = lax.axis_size(axis)
        ends = count - 1
        head = lax.slice_in_dim(cells, 0, width, axis=dim)
        tail = lax.slice_in_dim(cells, cells.shape[dim] - width, cells.shape[dim], axis=dim)
        cells = jnp.concatenate(
            [
                lax.ppermute(tail, axis, [(i, (i + 1) % count) for i in range(ends)]),
                cells,
                lax.ppermute(head, axis, [((i + 1) % count, i) for i in range(ends)]),
            ],
            axis=dim,
        )
    return cells


def conv_valid(source, weight):
    height = source.shape[1] - 2
    across = source.shape[2] - 2
    summed = jnp.zeros((weight.shape[1], height, across), jnp.float32)
    for offset in range(9):
        window = source[:, offset // 3 : offset // 3 + height, offset % 3 : offset % 3 + across]
        summed = summed + jnp.einsum(
            "oc,crw->orw", weight[offset], window, preferred_element_type=jnp.float32
        )
    return summed


def layer_same(source, weight):
    padded = with_halo(source, (("row", 1), (("col", "sub"), 2)), 1)
    return conv_valid(padded, weight)


def occlusion_logit(gathered, out_weight, occlusion_weight):
    attended = jnp.einsum("rwc,cd->rwd", gathered, out_weight, preferred_element_type=jnp.float32)
    centre = jnp.mean(attended, axis=-1, keepdims=True)
    spread = jnp.mean((attended - centre) ** 2, axis=-1, keepdims=True)
    normalized = (attended - centre) * lax.rsqrt(spread + 1e-05)
    return jnp.einsum("rwc,c->rw", normalized, occlusion_weight, precision=lax.Precision.HIGHEST)


def per_device(
    left_features,
    right_features,
    left_image,
    query_key,
    value_weight,
    out_weight,
    occlusion_weight,
    first_conv,
    middle_conv,
    last_conv,
):
    tile_rows = left_features.shape[0]
    tile_cols = left_features.shape[1]
    group_size = lax.axis_size(("col", "sub"))
    row_length = tile_cols * group_size
    scaling = HEAD ** (-0.5)
    positions = jnp.arange(row_length)
    allowed = positions[None, :] <= positions[:, None]
    places = positions.astype(jnp.float32)

    def attend(inputs):
        query_block, key_block, value_block = inputs
        scores = jnp.einsum(
            "bihd,bjhd->bhij", query_block, key_block, preferred_element_type=jnp.float32
        )
        scores = jnp.where(allowed[None, None], scores, -jnp.inf)
        largest = jnp.max(scores, axis=-1, keepdims=True)
        exponent = jnp.exp(scores - largest)
        totals = jnp.sum(exponent, axis=-1, keepdims=True)
        probabilities = (exponent / totals).astype(jnp.bfloat16)
        blended = jnp.einsum(
            "bhij,bjhd->bihd", probabilities, value_block, preferred_element_type=jnp.float32
        ).astype(jnp.bfloat16)
        weighted = jnp.einsum("bhij,j->bhi", exponent, places, precision=lax.Precision.HIGHEST)
        shifts = places[None, None, :] - weighted / totals[..., 0]
        return (blended, jnp.sum(shifts, axis=1))

    band_count = tile_rows // group_size
    full_left, full_right = (
        lax.all_to_all(left_features, ("col", "sub"), split_axis=0, concat_axis=1, tiled=True),
        lax.all_to_all(right_features, ("col", "sub"), split_axis=0, concat_axis=1, tiled=True),
    )
    queries = (
        jnp.einsum("rwc,cd->rwd", full_left, query_key, preferred_element_type=jnp.float32)
        * scaling
    ).astype(jnp.bfloat16)
    keys = jnp.einsum(
        "rwc,cd->rwd", full_right, query_key, preferred_element_type=jnp.float32
    ).astype(jnp.bfloat16)
    values = jnp.einsum(
        "rwc,cd->rwd", full_right, value_weight, preferred_element_type=jnp.float32
    ).astype(jnp.bfloat16)
    block_shape = (band_count, 1, row_length, HEADS, HEAD)
    blended, shift_sums = lax.map(
        attend,
        (queries.reshape(block_shape), keys.reshape(block_shape), values.reshape(block_shape)),
    )
    head_out = blended.reshape(band_count, row_length, C)
    band_disparity = shift_sums.reshape(band_count, row_length) * (8.0 / (HEADS * row_length))
    band_occlusion = occlusion_logit(head_out, out_weight, occlusion_weight)
    maps = lax.all_to_all(
        jnp.stack([band_disparity, band_occlusion]),
        ("col", "sub"),
        split_axis=2,
        concat_axis=1,
        tiled=True,
    )
    disparity = maps[0]
    occlusion = maps[1]
    stacked = jnp.concatenate([disparity[None], occlusion[None], left_image], axis=0).astype(
        jnp.bfloat16
    )
    layer_one = jax.nn.relu(layer_same(stacked, first_conv)).astype(jnp.bfloat16)
    layer_two = jax.nn.relu(layer_same(layer_one, middle_conv[0])).astype(jnp.bfloat16)
    layer_three = jax.nn.relu(
        layer_one.astype(jnp.float32) + layer_same(layer_two, middle_conv[1])
    ).astype(jnp.bfloat16)
    layer_four = jax.nn.relu(layer_same(layer_three, middle_conv[2])).astype(jnp.bfloat16)
    correction = layer_same(layer_four, last_conv)
    disparity_out = disparity + correction[0]
    occlusion_out = jax.nn.sigmoid(occlusion + correction[1])
    return (disparity_out, occlusion_out)


def solution(mesh):
    placed = (
        P(("grp", "row"), ("col", "sub"), None),
        P(("grp", "row"), ("col", "sub"), None),
        P(None, ("grp", "row"), ("col", "sub")),
        P(),
        P(),
        P(),
        P(),
        P(),
        P(),
        P(),
    )
    return jax.shard_map(
        per_device,
        mesh=mesh,
        in_specs=placed,
        out_specs=(P(("grp", "row"), ("col", "sub")), P(("grp", "row"), ("col", "sub"))),
        check_vma=False,
    )
```

profile of v0, /device:TPU:0, one launch (start us, length us, event | category | flops | bytes accessed | tf_op | source)
XLA Modules:
  0.0 166.5 jit_solution(7081243207091826723)
XLA Ops:
  0.6 4.2 %all-to-all-start = ((bf16[32,64,128]{2,1,0:T(8,128)(2,1)}), bf16[32,64,128]{2,1,0:T(8,128)(2,1)S(1)}, u32[]{:S(2)}, u32[]{:S(2)}) async-start(bf16[32,64,128]{2,1,0:T(8,128)(2,1)} %param.13), calls=%async_computation | async-start | bytes 1048576 | tf_op jit(solution)/shard_map/all_to_all | solution.py:94
  4.9 8.8 %all-to-all-done = bf16[32,64,128]{2,1,0:T(8,128)(2,1)S(1)} async-done(((bf16[32,64,128]{2,1,0:T(8,128)(2,1)}), bf16[32,64,128]{2,1,0:T(8,128)(2,1)S(1)}, u32[]{:S(2)}, u32[]{:S(2)}) %all-to-all-start) | async-done | bytes 524320 | tf_op jit(solution)/shard_map/all_to_all | solution.py:94
  13.7 3.5 %all-to-all-start.1 = ((bf16[32,64,128]{2,1,0:T(8,128)(2,1)}), bf16[32,64,128]{2,1,0:T(8,128)(2,1)S(1)}, u32[]{:S(2)}, u32[]{:S(2)}) async-start(bf16[32,64,128]{2,1,0:T(8,128)(2,1)} %param.12), calls=%async_computation.1 | async-start | bytes 1048576 | tf_op jit(solution)/shard_map/all_to_all | solution.py:93
  19.1 6.9 %all-to-all-done.1 = bf16[32,64,128]{2,1,0:T(8,128)(2,1)S(1)} async-done(((bf16[32,64,128]{2,1,0:T(8,128)(2,1)}), bf16[32,64,128]{2,1,0:T(8,128)(2,1)S(1)}, u32[]{:S(2)}, u32[]{:S(2)}) %all-to-all-start.1) | async-done | bytes 524320 | tf_op jit(solution)/shard_map/all_to_all | solution.py:93
  26.4 36.1 %while.14 = (s32[]{:T(128)}, bf16[8,1,256,8,16]{2,4,3,1,0:T(8,128)(2,1)}, f32[8,1,256]{2,0,1:T(8,128)S(1)}, bf16[8,1,256,8,16]{2,4,3,1,0:T(8,128)(2,1)}, bf16[8,...) while((s32[]{:T(128)}, ...), condition=%wide.region_4.5_spmd.clone.clone, body=%wide.region_0.4_spmd.clone.clone.sunk | while | flops 45713408 | bytes 9060441 | solution.py:107
  27.0 1.5 fusion.296
  28.9 2.0 %fusion.295 = bf16[8,1,256,8,16]{2,4,3,1,0:T(8,128)(2,1)} fusion(bf16[8,1,256,8,16]{2,4,3,1,0:T(8,128)(2,1)} %get-tuple-element.239, s32[]{:T(128)} %get-tuple-element.238, f32[8,256,256]{1,2,0:T(8,128)S(1)} %get-tuple-element.228, f32[8,256]{1,0:T(8,128)S(1)} %fusion.294, f32[8,256]{1,0:T(8,128)S(1)} %get-tuple-element.229, ...), kind=kOutput, calls=%fused_computation.9.clone.1 | convolution fusion | flops 18907136 | bytes 2311168 | tf_op jit(solution)/shard_map/while/body/eval_jaxpr/bhij,bjhd->bihd/dot_general | solution.py:84
  31.5 1.5 fusion.296
  33.4 2.0 %fusion.295 = bf16[8,1,256,8,16]{2,4,3,1,0:T(8,128)(2,1)} fusion(bf16[8,1,256,8,16]{2,4,3,1,0:T(8,128)(2,1)} %get-tuple-element.239, s32[]{:T(128)} %get-tuple-element.238, f32[8,256,256]{1,2,0:T(8,128)S(1)} %get-tuple-element.228, f32[8,256]{1,0:T(8,128)S(1)} %fusion.294, f32[8,256]{1,0:T(8,128)S(1)} %get-tuple-element.229, ...), kind=kOutput, calls=%fused_computation.9.clone.1 | convolution fusion | flops 18907136 | bytes 2311168 | tf_op jit(solution)/shard_map/while/body/eval_jaxpr/bhij,bjhd->bihd/dot_general | solution.py:84
  36.0 1.5 fusion.296
  37.9 2.0 %fusion.295 = bf16[8,1,256,8,16]{2,4,3,1,0:T(8,128)(2,1)} fusion(bf16[8,1,256,8,16]{2,4,3,1,0:T(8,128)(2,1)} %get-tuple-element.239, s32[]{:T(128)} %get-tuple-element.238, f32[8,256,256]{1,2,0:T(8,128)S(1)} %get-tuple-element.228, f32[8,256]{1,0:T(8,128)S(1)} %fusion.294, f32[8,256]{1,0:T(8,128)S(1)} %get-tuple-element.229, ...), kind=kOutput, calls=%fused_computation.9.clone.1 | convolution fusion | flops 18907136 | bytes 2311168 | tf_op jit(solution)/shard_map/while/body/eval_jaxpr/bhij,bjhd->bihd/dot_general | solution.py:84
  40.5 1.5 fusion.296
  42.4 2.0 %fusion.295 = bf16[8,1,256,8,16]{2,4,3,1,0:T(8,128)(2,1)} fusion(bf16[8,1,256,8,16]{2,4,3,1,0:T(8,128)(2,1)} %get-tuple-element.239, s32[]{:T(128)} %get-tuple-element.238, f32[8,256,256]{1,2,0:T(8,128)S(1)} %get-tuple-element.228, f32[8,256]{1,0:T(8,128)S(1)} %fusion.294, f32[8,256]{1,0:T(8,128)S(1)} %get-tuple-element.229, ...), kind=kOutput, calls=%fused_computation.9.clone.1 | convolution fusion | flops 18907136 | bytes 2311168 | tf_op jit(solution)/shard_map/while/body/eval_jaxpr/bhij,bjhd->bihd/dot_general | solution.py:84
  45.0 1.5 fusion.296
  46.9 2.0 %fusion.295 = bf16[8,1,256,8,16]{2,4,3,1,0:T(8,128)(2,1)} fusion(bf16[8,1,256,8,16]{2,4,3,1,0:T(8,128)(2,1)} %get-tuple-element.239, s32[]{:T(128)} %get-tuple-element.238, f32[8,256,256]{1,2,0:T(8,128)S(1)} %get-tuple-element.228, f32[8,256]{1,0:T(8,128)S(1)} %fusion.294, f32[8,256]{1,0:T(8,128)S(1)} %get-tuple-element.229, ...), kind=kOutput, calls=%fused_computation.9.clone.1 | convolution fusion | flops 18907136 | bytes 2311168 | tf_op jit(solution)/shard_map/while/body/eval_jaxpr/bhij,bjhd->bihd/dot_general | solution.py:84
  49.5 1.5 fusion.296
  51.4 2.0 %fusion.295 = bf16[8,1,256,8,16]{2,4,3,1,0:T(8,128)(2,1)} fusion(bf16[8,1,256,8,16]{2,4,3,1,0:T(8,128)(2,1)} %get-tuple-element.239, s32[]{:T(128)} %get-tuple-element.238, f32[8,256,256]{1,2,0:T(8,128)S(1)} %get-tuple-element.228, f32[8,256]{1,0:T(8,128)S(1)} %fusion.294, f32[8,256]{1,0:T(8,128)S(1)} %get-tuple-element.229, ...), kind=kOutput, calls=%fused_computation.9.clone.1 | convolution fusion | flops 18907136 | bytes 2311168 | tf_op jit(solution)/shard_map/while/body/eval_jaxpr/bhij,bjhd->bihd/dot_general | solution.py:84
  54.0 1.5 fusion.296
  55.9 2.0 %fusion.295 = bf16[8,1,256,8,16]{2,4,3,1,0:T(8,128)(2,1)} fusion(bf16[8,1,256,8,16]{2,4,3,1,0:T(8,128)(2,1)} %get-tuple-element.239, s32[]{:T(128)} %get-tuple-element.238, f32[8,256,256]{1,2,0:T(8,128)S(1)} %get-tuple-element.228, f32[8,256]{1,0:T(8,128)S(1)} %fusion.294, f32[8,256]{1,0:T(8,128)S(1)} %get-tuple-element.229, ...), kind=kOutput, calls=%fused_computation.9.clone.1 | convolution fusion | flops 18907136 | bytes 2311168 | tf_op jit(solution)/shard_map/while/body/eval_jaxpr/bhij,bjhd->bihd/dot_general | solution.py:84
  58.5 1.5 fusion.296
  60.4 2.0 %fusion.295 = bf16[8,1,256,8,16]{2,4,3,1,0:T(8,128)(2,1)} fusion(bf16[8,1,256,8,16]{2,4,3,1,0:T(8,128)(2,1)} %get-tuple-element.239, s32[]{:T(128)} %get-tuple-element.238, f32[8,256,256]{1,2,0:T(8,128)S(1)} %get-tuple-element.228, f32[8,256]{1,0:T(8,128)S(1)} %fusion.294, f32[8,256]{1,0:T(8,128)S(1)} %get-tuple-element.229, ...), kind=kOutput, calls=%fused_computation.9.clone.1 | convolution fusion | flops 18907136 | bytes 2311168 | tf_op jit(solution)/shard_map/while/body/eval_jaxpr/bhij,bjhd->bihd/dot_general | solution.py:84
  62.5 1.4 fusion.276
  66.0 3.3 %all-to-all-start.2 = ((f32[4,1,1024]{2,1,0:T(1,128)}), f32[4,1,1024]{2,1,0:T(1,128)S(1)}, u32[]{:S(2)}, u32[]{:S(2)}) async-start(f32[4,1,1024]{2,1,0:T(1,128)} %reshape.211), calls=%async_computation.2 | async-start | bytes 32768 | tf_op jit(solution)/shard_map/all_to_all | solution.py:114
  69.3 3.8 %all-to-all-done.2 = f32[4,1,1024]{2,1,0:T(1,128)S(1)} async-done(((f32[4,1,1024]{2,1,0:T(1,128)}), f32[4,1,1024]{2,1,0:T(1,128)S(1)}, u32[]{:S(2)}, u32[]{:S(2)}) %all-to-all-start.2) | async-done | bytes 16416 | tf_op jit(solution)/shard_map/all_to_all | solution.py:114
  74.9 4.2 %collective-permute-start = (bf16[5,1,64]{2,1,0:T(2,128)(2,1)S(1)}, bf16[5,1,64]{2,1,0:T(2,128)(2,1)S(1)}, u32[]{:S(2)}, u32[]{:S(2)}) collective-permute-start(bf16[5,1,64]{2,1,0:T(2,128)(2,1)S(1)} %get-tuple-element.177), channel_id=1, source_target_pairs={{0,4},{4,8},{8,12},{1,5},{5,9},{9,13},{2,6},{6,10},{10,14},{3,7},{... | collective-permute-start | bytes 1928 | tf_op jit(solution)/shard_map/ppermute | solution.py:19
  79.1 1.3 collective-permute-start.1
  80.4 4.2 %collective-permute-done.1 = bf16[5,1,64]{2,1,0:T(2,128)(2,1)S(1)} collective-permute-done((bf16[5,1,64]{2,1,0:T(2,128)(2,1)S(1)}, bf16[5,1,64]{2,1,0:T(2,128)(2,1)S(1)}, u32[]{:S(2)}, u32[]{:S(2)}) %collective-permute-start.1) | collective-permute-done | bytes 672 | tf_op jit(solution)/shard_map/ppermute | solution.py:21
  84.7 1.3 collective-permute-start.2
  87.7 1.7 %collective-permute-done.3 = bf16[5,34,1]{2,1,0:T(8,128)(2,1)S(1)} collective-permute-done((bf16[5,34,1]{2,1,0:T(8,128)(2,1)S(1)}, bf16[5,34,1]{2,1,0:T(8,128)(2,1)S(1)}, u32[]{:S(2)}, u32[]{:S(2)}) %collective-permute-start.3) | collective-permute-done | bytes 372 | tf_op jit(solution)/shard_map/ppermute | solution.py:21
  92.5 3.5 %collective-permute-start.4 = (bf16[64,1,64]{0,2,1:T(8,128)(2,1)S(1)}, bf16[64,1,64]{0,2,1:T(8,128)(2,1)S(1)}, u32[]{:S(2)}, u32[]{:S(2)}) collective-permute-start(bf16[64,1,64]{0,2,1:T(8,128)(2,1)S(1)} %get-tuple-element.163), channel_id=1, source_target_pairs={{0,4},{4,8},{8,12},{1,5},{5,9},{9,13},{2,6},{6,10},{10,14},{3,7},{... | collective-permute-start | bytes 24584 | tf_op jit(solution)/shard_map/ppermute | solution.py:19
  97.6 4.0 %collective-permute-done.5 = bf16[64,1,64]{0,2,1:T(8,128)(2,1)S(1)} collective-permute-done((bf16[64,1,64]{0,2,1:T(8,128)(2,1)S(1)}, bf16[64,1,64]{0,2,1:T(8,128)(2,1)S(1)}, u32[]{:S(2)}, u32[]{:S(2)}) %collective-permute-start.5) | collective-permute-done | bytes 8224 | tf_op jit(solution)/shard_map/ppermute | solution.py:21
  101.7 3.3 %collective-permute-start.6 = (bf16[64,34,1]{0,2,1:T(2,128)(2,1)S(1)}, bf16[64,34,1]{0,2,1:T(2,128)(2,1)S(1)}, u32[]{:S(2)}, u32[]{:S(2)}) collective-permute-start(bf16[64,34,1]{0,2,1:T(2,128)(2,1)S(1)} %get-tuple-element.155), channel_id=1, source_target_pairs={{0,1},{1,2},{2,3},{4,5},{5,6},{6,7},{8,9},{9,10},{10,11},{12,13},{... | collective-permute-start | bytes 13064 | tf_op jit(solution)/shard_map/ppermute | solution.py:19
  106.9 2.1 %collective-permute-done.7 = bf16[64,34,1]{0,2,1:T(2,128)(2,1)S(1)} collective-permute-done((bf16[64,34,1]{0,2,1:T(2,128)(2,1)S(1)}, bf16[64,34,1]{0,2,1:T(2,128)(2,1)S(1)}, u32[]{:S(2)}, u32[]{:S(2)}) %collective-permute-start.7) | collective-permute-done | bytes 4384 | tf_op jit(solution)/shard_map/ppermute | solution.py:21
  111.3 3.7 %collective-permute-start.8 = (bf16[64,1,64]{0,2,1:T(8,128)(2,1)S(1)}, bf16[64,1,64]{0,2,1:T(8,128)(2,1)S(1)}, u32[]{:S(2)}, u32[]{:S(2)}) collective-permute-start(bf16[64,1,64]{0,2,1:T(8,128)(2,1)S(1)} %get-tuple-element.161), channel_id=1, source_target_pairs={{0,4},{4,8},{8,12},{1,5},{5,9},{9,13},{2,6},{6,10},{10,14},{3,7},{... | collective-permute-start | bytes 24584 | tf_op jit(solution)/shard_map/ppermute | solution.py:19
  116.6 4.0 %collective-permute-done.9 = bf16[64,1,64]{0,2,1:T(8,128)(2,1)S(1)} collective-permute-done((bf16[64,1,64]{0,2,1:T(8,128)(2,1)S(1)}, bf16[64,1,64]{0,2,1:T(8,128)(2,1)S(1)}, u32[]{:S(2)}, u32[]{:S(2)}) %collective-permute-start.9) | collective-permute-done | bytes 8224 | tf_op jit(solution)/shard_map/ppermute | solution.py:21
  120.7 3.0 %collective-permute-start.10 = (bf16[64,34,1]{0,2,1:T(2,128)(2,1)S(1)}, bf16[64,34,1]{0,2,1:T(2,128)(2,1)S(1)}, u32[]{:S(2)}, u32[]{:S(2)}) collective-permute-start(bf16[64,34,1]{0,2,1:T(2,128)(2,1)S(1)} %get-tuple-element.151), channel_id=1, source_target_pairs={{0,1},{1,2},{2,3},{4,5},{5,6},{6,7},{8,9},{9,10},{10,11},{12,13},{... | collective-permute-start | bytes 13064 | tf_op jit(solution)/shard_map/ppermute | solution.py:19
  123.6 1.3 collective-permute-start.11
  125.6 2.1 %collective-permute-done.11 = bf16[64,34,1]{0,2,1:T(2,128)(2,1)S(1)} collective-permute-done((bf16[64,34,1]{0,2,1:T(2,128)(2,1)S(1)}, bf16[64,34,1]{0,2,1:T(2,128)(2,1)S(1)}, u32[]{:S(2)}, u32[]{:S(2)}) %collective-permute-start.11) | collective-permute-done | bytes 4384 | tf_op jit(solution)/shard_map/ppermute | solution.py:21
  130.1 1.9 %collective-permute-start.12 = (bf16[64,1,64]{0,2,1:T(8,128)(2,1)S(1)}, bf16[64,1,64]{0,2,1:T(8,128)(2,1)S(1)}, u32[]{:S(2)}, u32[]{:S(2)}) collective-permute-start(bf16[64,1,64]{0,2,1:T(8,128)(2,1)S(1)} %get-tuple-element.159), channel_id=1, source_target_pairs={{0,4},{4,8},{8,12},{1,5},{5,9},{9,13},{2,6},{6,10},{10,14},{3,7},{... | collective-permute-start | bytes 24584 | tf_op jit(solution)/shard_map/ppermute | solution.py:19
  132.1 1.3 collective-permute-start.13
  133.7 4.0 %collective-permute-done.13 = bf16[64,1,64]{0,2,1:T(8,128)(2,1)S(1)} collective-permute-done((bf16[64,1,64]{0,2,1:T(8,128)(2,1)S(1)}, bf16[64,1,64]{0,2,1:T(8,128)(2,1)S(1)}, u32[]{:S(2)}, u32[]{:S(2)}) %collective-permute-start.13) | collective-permute-done | bytes 8224 | tf_op jit(solution)/shard_map/ppermute | solution.py:21
  137.8 3.0 %collective-permute-start.14 = (bf16[64,34,1]{0,2,1:T(2,128)(2,1)S(1)}, bf16[64,34,1]{0,2,1:T(2,128)(2,1)S(1)}, u32[]{:S(2)}, u32[]{:S(2)}) collective-permute-start(bf16[64,34,1]{0,2,1:T(2,128)(2,1)S(1)} %get-tuple-element.147), channel_id=1, source_target_pairs={{0,1},{1,2},{2,3},{4,5},{5,6},{6,7},{8,9},{9,10},{10,11},{12,13},{... | collective-permute-start | bytes 13064 | tf_op jit(solution)/shard_map/ppermute | solution.py:19
  142.6 2.1 %collective-permute-done.15 = bf16[64,34,1]{0,2,1:T(2,128)(2,1)S(1)} collective-permute-done((bf16[64,34,1]{0,2,1:T(2,128)(2,1)S(1)}, bf16[64,34,1]{0,2,1:T(2,128)(2,1)S(1)}, u32[]{:S(2)}, u32[]{:S(2)}) %collective-permute-start.15) | collective-permute-done | bytes 4384 | tf_op jit(solution)/shard_map/ppermute | solution.py:21
  147.1 1.9 %collective-permute-start.16 = (bf16[64,1,64]{0,2,1:T(8,128)(2,1)S(1)}, bf16[64,1,64]{0,2,1:T(8,128)(2,1)S(1)}, u32[]{:S(2)}, u32[]{:S(2)}) collective-permute-start(bf16[64,1,64]{0,2,1:T(8,128)(2,1)S(1)} %get-tuple-element.157), channel_id=1, source_target_pairs={{0,4},{4,8},{8,12},{1,5},{5,9},{9,13},{2,6},{6,10},{10,14},{3,7},{... | collective-permute-start | bytes 24584 | tf_op jit(solution)/shard_map/ppermute | solution.py:19
  150.9 3.8 %collective-permute-done.17 = bf16[64,1,64]{0,2,1:T(8,128)(2,1)S(1)} collective-permute-done((bf16[64,1,64]{0,2,1:T(8,128)(2,1)S(1)}, bf16[64,1,64]{0,2,1:T(8,128)(2,1)S(1)}, u32[]{:S(2)}, u32[]{:S(2)}) %collective-permute-start.17) | collective-permute-done | bytes 8224 | tf_op jit(solution)/shard_map/ppermute | solution.py:21
  154.8 3.0 %collective-permute-start.18 = (bf16[64,34,1]{0,2,1:T(2,128)(2,1)S(1)}, bf16[64,34,1]{0,2,1:T(2,128)(2,1)S(1)}, u32[]{:S(2)}, u32[]{:S(2)}) collective-permute-start(bf16[64,34,1]{0,2,1:T(2,128)(2,1)S(1)} %get-tuple-element.143), channel_id=1, source_target_pairs={{0,1},{1,2},{2,3},{4,5},{5,6},{6,7},{8,9},{9,10},{10,11},{12,13},{... | collective-permute-start | bytes 13064 | tf_op jit(solution)/shard_map/ppermute | solution.py:19
  157.7 1.3 collective-permute-start.19
  160.0 1.7 %collective-permute-done.19 = bf16[64,34,1]{0,2,1:T(2,128)(2,1)S(1)} collective-permute-done((bf16[64,34,1]{0,2,1:T(2,128)(2,1)S(1)}, bf16[64,34,1]{0,2,1:T(2,128)(2,1)S(1)}, u32[]{:S(2)}, u32[]{:S(2)}) %collective-permute-start.19) | collective-permute-done | bytes 4384 | tf_op jit(solution)/shard_map/ppermute | solution.py:21
  (172 shorter events, 41.3 us)
Async XLA Ops:
  0.6 16.6 %copy-start = (bf16[128,128]{1,0:T(8,128)(2,1)S(1)}, bf16[128,128]{1,0:T(8,128)(2,1)}, u32[]{:S(2)}) copy-start(bf16[128,128]{1,0:T(8,128)(2,1)} %param.15) | copy-start | bytes 98308
  0.6 13.1 %all-to-all-start = ((bf16[32,64,128]{2,1,0:T(8,128)(2,1)}), bf16[32,64,128]{2,1,0:T(8,128)(2,1)S(1)}, u32[]{:S(2)}, u32[]{:S(2)}) async-start(bf16[32,64,128]{2,1,0:T(8,128)(2,1)} %param.13), calls=%async_computation | async-start | bytes 1048576 | tf_op jit(solution)/shard_map/all_to_all | solution.py:94
  13.7 12.3 %all-to-all-start.1 = ((bf16[32,64,128]{2,1,0:T(8,128)(2,1)}), bf16[32,64,128]{2,1,0:T(8,128)(2,1)S(1)}, u32[]{:S(2)}, u32[]{:S(2)}) async-start(bf16[32,64,128]{2,1,0:T(8,128)(2,1)} %param.12), calls=%async_computation.1 | async-start | bytes 1048576 | tf_op jit(solution)/shard_map/all_to_all | solution.py:93
  17.2 0.8 copy-start.3
  26.4 36.1 %copy-start.4 = (bf16[128,128]{1,0:T(8,128)(2,1)S(1)}, bf16[128,128]{1,0:T(8,128)(2,1)}, u32[]{:S(2)}) copy-start(bf16[128,128]{1,0:T(8,128)(2,1)} %param.17) | copy-start | bytes 98308
  62.5 1.6 copy-start.6
  63.9 5.3 %copy-start.2 = (f32[3,32,64]{2,1,0:T(8,128)S(1)}, f32[3,32,64]{2,1,0:T(8,128)}, u32[]{:S(2)}) copy-start(f32[3,32,64]{2,1,0:T(8,128)} %param.14) | copy-start | bytes 73732
  64.8 22.5 %copy-start.5 = (bf16[9,64,5]{1,2,0:T(8,128)(2,1)S(1)}, bf16[9,64,5]{1,2,0:T(8,128)(2,1)}, u32[]{:S(2)}) copy-start(bf16[9,64,5]{1,2,0:T(8,128)(2,1)} %param.19) | copy-start | bytes 17284
  66.0 7.1 %all-to-all-start.2 = ((f32[4,1,1024]{2,1,0:T(1,128)}), f32[4,1,1024]{2,1,0:T(1,128)S(1)}, u32[]{:S(2)}, u32[]{:S(2)}) async-start(f32[4,1,1024]{2,1,0:T(1,128)} %reshape.211), calls=%async_computation.2 | async-start | bytes 32768 | tf_op jit(solution)/shard_map/all_to_all | solution.py:114
  74.9 5.5 %collective-permute-start = (bf16[5,1,64]{2,1,0:T(2,128)(2,1)S(1)}, bf16[5,1,64]{2,1,0:T(2,128)(2,1)S(1)}, u32[]{:S(2)}, u32[]{:S(2)}) collective-permute-start(bf16[5,1,64]{2,1,0:T(2,128)(2,1)S(1)} %get-tuple-element.177), channel_id=1, source_target_pairs={{0,4},{4,8},{8,12},{1,5},{5,9},{9,13},{2,6},{6,10},{10,14},{3,7},{... | collective-permute-start | bytes 1928 | tf_op jit(solution)/shard_map/ppermute | solution.py:19
  79.1 5.5 %collective-permute-start.1 = (bf16[5,1,64]{2,1,0:T(2,128)(2,1)S(1)}, bf16[5,1,64]{2,1,0:T(2,128)(2,1)S(1)}, u32[]{:S(2)}, u32[]{:S(2)}) collective-permute-start(bf16[5,1,64]{2,1,0:T(2,128)(2,1)S(1)} %get-tuple-element.178), channel_id=1, source_target_pairs={{4,0},{8,4},{12,8},{5,1},{9,5},{13,9},{6,2},{10,6},{14,10},{7,3},{... | collective-permute-start | bytes 1928 | tf_op jit(solution)/shard_map/ppermute | solution.py:21
  84.7 3.0 %collective-permute-start.2 = (bf16[5,34,1]{2,1,0:T(8,128)(2,1)S(1)}, bf16[5,34,1]{2,1,0:T(8,128)(2,1)S(1)}, u32[]{:S(2)}, u32[]{:S(2)}) collective-permute-start(bf16[5,34,1]{2,1,0:T(8,128)(2,1)S(1)} %get-tuple-element.171), channel_id=1, source_target_pairs={{0,1},{1,2},{2,3},{4,5},{5,6},{6,7},{8,9},{9,10},{10,11},{12,13},{... | collective-permute-start | bytes 1028 | tf_op jit(solution)/shard_map/ppermute | solution.py:19
  86.0 3.4 %collective-permute-start.3 = (bf16[5,34,1]{2,1,0:T(8,128)(2,1)S(1)}, bf16[5,34,1]{2,1,0:T(8,128)(2,1)S(1)}, u32[]{:S(2)}, u32[]{:S(2)}) collective-permute-start(bf16[5,34,1]{2,1,0:T(8,128)(2,1)S(1)} %get-tuple-element.172), channel_id=1, source_target_pairs={{1,0},{2,1},{3,2},{5,4},{6,5},{7,6},{9,8},{10,9},{11,10},{13,12},{... | collective-permute-start | bytes 1028 | tf_op jit(solution)/shard_map/ppermute | solution.py:21
  92.1 5.2 %copy-start.1 = (bf16[3,9,64,64]{3,2,1,0:T(8,128)(2,1)S(1)}, bf16[3,9,64,64]{3,2,1,0:T(8,128)(2,1)}, u32[]{:S(2)}) copy-start(bf16[3,9,64,64]{3,2,1,0:T(8,128)(2,1)} %param.20) | copy-start | bytes 663556
  92.5 5.1 %collective-permute-start.4 = (bf16[64,1,64]{0,2,1:T(8,128)(2,1)S(1)}, bf16[64,1,64]{0,2,1:T(8,128)(2,1)S(1)}, u32[]{:S(2)}, u32[]{:S(2)}) collective-permute-start(bf16[64,1,64]{0,2,1:T(8,128)(2,1)S(1)} %get-tuple-element.163), channel_id=1, source_target_pairs={{0,4},{4,8},{8,12},{1,5},{5,9},{9,13},{2,6},{6,10},{10,14},{3,7},{... | collective-permute-start | bytes 24584 | tf_op jit(solution)/shard_map/ppermute | solution.py:19
  96.0 5.6 %collective-permute-start.5 = (bf16[64,1,64]{0,2,1:T(8,128)(2,1)S(1)}, bf16[64,1,64]{0,2,1:T(8,128)(2,1)S(1)}, u32[]{:S(2)}, u32[]{:S(2)}) collective-permute-start(bf16[64,1,64]{0,2,1:T(8,128)(2,1)S(1)} %get-tuple-element.164), channel_id=1, source_target_pairs={{4,0},{8,4},{12,8},{5,1},{9,5},{13,9},{6,2},{10,6},{14,10},{7,3},{... | collective-permute-start | bytes 24584 | tf_op jit(solution)/shard_map/ppermute | solution.py:21
  101.7 5.2 %collective-permute-start.6 = (bf16[64,34,1]{0,2,1:T(2,128)(2,1)S(1)}, bf16[64,34,1]{0,2,1:T(2,128)(2,1)S(1)}, u32[]{:S(2)}, u32[]{:S(2)}) collective-permute-start(bf16[64,34,1]{0,2,1:T(2,128)(2,1)S(1)} %get-tuple-element.155), channel_id=1, source_target_pairs={{0,1},{1,2},{2,3},{4,5},{5,6},{6,7},{8,9},{9,10},{10,11},{12,13},{... | collective-permute-start | bytes 13064 | tf_op jit(solution)/shard_map/ppermute | solution.py:19
  104.9 4.0 %collective-permute-start.7 = (bf16[64,34,1]{0,2,1:T(2,128)(2,1)S(1)}, bf16[64,34,1]{0,2,1:T(2,128)(2,1)S(1)}, u32[]{:S(2)}, u32[]{:S(2)}) collective-permute-start(bf16[64,34,1]{0,2,1:T(2,128)(2,1)S(1)} %get-tuple-element.156), channel_id=1, source_target_pairs={{1,0},{2,1},{3,2},{5,4},{6,5},{7,6},{9,8},{10,9},{11,10},{13,12},{... | collective-permute-start | bytes 13064 | tf_op jit(solution)/shard_map/ppermute | solution.py:21
  111.3 5.3 %collective-permute-start.8 = (bf16[64,1,64]{0,2,1:T(8,128)(2,1)S(1)}, bf16[64,1,64]{0,2,1:T(8,128)(2,1)S(1)}, u32[]{:S(2)}, u32[]{:S(2)}) collective-permute-start(bf16[64,1,64]{0,2,1:T(8,128)(2,1)S(1)} %get-tuple-element.161), channel_id=1, source_target_pairs={{0,4},{4,8},{8,12},{1,5},{5,9},{9,13},{2,6},{6,10},{10,14},{3,7},{... | collective-permute-start | bytes 24584 | tf_op jit(solution)/shard_map/ppermute | solution.py:19
  115.0 5.6 %collective-permute-start.9 = (bf16[64,1,64]{0,2,1:T(8,128)(2,1)S(1)}, bf16[64,1,64]{0,2,1:T(8,128)(2,1)S(1)}, u32[]{:S(2)}, u32[]{:S(2)}) collective-permute-start(bf16[64,1,64]{0,2,1:T(8,128)(2,1)S(1)} %get-tuple-element.162), channel_id=1, source_target_pairs={{4,0},{8,4},{12,8},{5,1},{9,5},{13,9},{6,2},{10,6},{14,10},{7,3},{... | collective-permute-start | bytes 24584 | tf_op jit(solution)/shard_map/ppermute | solution.py:21
  120.7 4.9 %collective-permute-start.10 = (bf16[64,34,1]{0,2,1:T(2,128)(2,1)S(1)}, bf16[64,34,1]{0,2,1:T(2,128)(2,1)S(1)}, u32[]{:S(2)}, u32[]{:S(2)}) collective-permute-start(bf16[64,34,1]{0,2,1:T(2,128)(2,1)S(1)} %get-tuple-element.151), channel_id=1, source_target_pairs={{0,1},{1,2},{2,3},{4,5},{5,6},{6,7},{8,9},{9,10},{10,11},{12,13},{... | collective-permute-start | bytes 13064 | tf_op jit(solution)/shard_map/ppermute | solution.py:19
  123.6 4.0 %collective-permute-start.11 = (bf16[64,34,1]{0,2,1:T(2,128)(2,1)S(1)}, bf16[64,34,1]{0,2,1:T(2,128)(2,1)S(1)}, u32[]{:S(2)}, u32[]{:S(2)}) collective-permute-start(bf16[64,34,1]{0,2,1:T(2,128)(2,1)S(1)} %get-tuple-element.152), channel_id=1, source_target_pairs={{1,0},{2,1},{3,2},{5,4},{6,5},{7,6},{9,8},{10,9},{11,10},{13,12},{... | collective-permute-start | bytes 13064 | tf_op jit(solution)/shard_map/ppermute | solution.py:21
  130.1 3.5 %collective-permute-start.12 = (bf16[64,1,64]{0,2,1:T(8,128)(2,1)S(1)}, bf16[64,1,64]{0,2,1:T(8,128)(2,1)S(1)}, u32[]{:S(2)}, u32[]{:S(2)}) collective-permute-start(bf16[64,1,64]{0,2,1:T(8,128)(2,1)S(1)} %get-tuple-element.159), channel_id=1, source_target_pairs={{0,4},{4,8},{8,12},{1,5},{5,9},{9,13},{2,6},{6,10},{10,14},{3,7},{... | collective-permute-start | bytes 24584 | tf_op jit(solution)/shard_map/ppermute | solution.py:19
  132.1 5.6 %collective-permute-start.13 = (bf16[64,1,64]{0,2,1:T(8,128)(2,1)S(1)}, bf16[64,1,64]{0,2,1:T(8,128)(2,1)S(1)}, u32[]{:S(2)}, u32[]{:S(2)}) collective-permute-start(bf16[64,1,64]{0,2,1:T(8,128)(2,1)S(1)} %get-tuple-element.160), channel_id=1, source_target_pairs={{4,0},{8,4},{12,8},{5,1},{9,5},{13,9},{6,2},{10,6},{14,10},{7,3},{... | collective-permute-start | bytes 24584 | tf_op jit(solution)/shard_map/ppermute | solution.py:21
  137.8 4.9 %collective-permute-start.14 = (bf16[64,34,1]{0,2,1:T(2,128)(2,1)S(1)}, bf16[64,34,1]{0,2,1:T(2,128)(2,1)S(1)}, u32[]{:S(2)}, u32[]{:S(2)}) collective-permute-start(bf16[64,34,1]{0,2,1:T(2,128)(2,1)S(1)} %get-tuple-element.147), channel_id=1, source_target_pairs={{0,1},{1,2},{2,3},{4,5},{5,6},{6,7},{8,9},{9,10},{10,11},{12,13},{... | collective-permute-start | bytes 13064 | tf_op jit(solution)/shard_map/ppermute | solution.py:19
  140.7 4.0 %collective-permute-start.15 = (bf16[64,34,1]{0,2,1:T(2,128)(2,1)S(1)}, bf16[64,34,1]{0,2,1:T(2,128)(2,1)S(1)}, u32[]{:S(2)}, u32[]{:S(2)}) collective-permute-start(bf16[64,34,1]{0,2,1:T(2,128)(2,1)S(1)} %get-tuple-element.148), channel_id=1, source_target_pairs={{1,0},{2,1},{3,2},{5,4},{6,5},{7,6},{9,8},{10,9},{11,10},{13,12},{... | collective-permute-start | bytes 13064 | tf_op jit(solution)/shard_map/ppermute | solution.py:21
  146.7 3.7 %copy-start.7 = (bf16[9,2,64]{2,1,0:T(2,128)(2,1)S(1)}, bf16[9,2,64]{2,1,0:T(2,128)(2,1)}, u32[]{:S(2)}) copy-start(bf16[9,2,64]{2,1,0:T(2,128)(2,1)} %param.21) | copy-start | bytes 6916
  147.1 3.7 %collective-permute-start.16 = (bf16[64,1,64]{0,2,1:T(8,128)(2,1)S(1)}, bf16[64,1,64]{0,2,1:T(8,128)(2,1)S(1)}, u32[]{:S(2)}, u32[]{:S(2)}) collective-permute-start(bf16[64,1,64]{0,2,1:T(8,128)(2,1)S(1)} %get-tuple-element.157), channel_id=1, source_target_pairs={{0,4},{4,8},{8,12},{1,5},{5,9},{9,13},{2,6},{6,10},{10,14},{3,7},{... | collective-permute-start | bytes 24584 | tf_op jit(solution)/shard_map/ppermute | solution.py:19
  149.1 5.6 %collective-permute-start.17 = (bf16[64,1,64]{0,2,1:T(8,128)(2,1)S(1)}, bf16[64,1,64]{0,2,1:T(8,128)(2,1)S(1)}, u32[]{:S(2)}, u32[]{:S(2)}) collective-permute-start(bf16[64,1,64]{0,2,1:T(8,128)(2,1)S(1)} %get-tuple-element.158), channel_id=1, source_target_pairs={{4,0},{8,4},{12,8},{5,1},{9,5},{13,9},{6,2},{10,6},{14,10},{7,3},{... | collective-permute-start | bytes 24584 | tf_op jit(solution)/shard_map/ppermute | solution.py:21
  154.8 5.3 %collective-permute-start.18 = (bf16[64,34,1]{0,2,1:T(2,128)(2,1)S(1)}, bf16[64,34,1]{0,2,1:T(2,128)(2,1)S(1)}, u32[]{:S(2)}, u32[]{:S(2)}) collective-permute-start(bf16[64,34,1]{0,2,1:T(2,128)(2,1)S(1)} %get-tuple-element.143), channel_id=1, source_target_pairs={{0,1},{1,2},{2,3},{4,5},{5,6},{6,7},{8,9},{9,10},{10,11},{12,13},{... | collective-permute-start | bytes 13064 | tf_op jit(solution)/shard_map/ppermute | solution.py:19
  157.7 4.0 %collective-permute-start.19 = (bf16[64,34,1]{0,2,1:T(2,128)(2,1)S(1)}, bf16[64,34,1]{0,2,1:T(2,128)(2,1)S(1)}, u32[]{:S(2)}, u32[]{:S(2)}) collective-permute-start(bf16[64,34,1]{0,2,1:T(2,128)(2,1)S(1)} %get-tuple-element.144), channel_id=1, source_target_pairs={{1,0},{2,1},{3,2},{5,4},{6,5},{7,6},{9,8},{10,9},{11,10},{13,12},{... | collective-permute-start | bytes 13064 | tf_op jit(solution)/shard_map/ppermute | solution.py:21
where the time goes:
time: 170 us; the launch traced here: 166 us
  matrix products  52.6 us (31%)
  starting transfers between devices  52.5 us (31%)
  waiting for transfers between devices  49.4 us (29%)
  other arithmetic  6.97 us (4%)
  local copies, waits for them, and re-layouts  3.3 us (2%)
    ppermute x10, waiting for transfers between devices, with_halo(): lax.ppermute(head, axis, [((i + 1) % count, i) for i in range(ends)])  29.8 us
    ppermute x10, starting transfers between devices, with_halo(): lax.ppermute(tail, axis, [(i, (i + 1) % count) for i in range(ends)])  28.6 us
    dot_general x45, matrix products, conv_valid(): jnp.einsum('oc,crw->orw', weight[offset], window, preferred_element_type=...  16.7 us
    dot_general x8, matrix products, attend(): jnp.einsum('bhij,bjhd->bihd', probabilities, value_block, preferred_eleme...  16.1 us
    ppermute x10, starting transfers between devices, with_halo(): lax.ppermute(head, axis, [((i + 1) % count, i) for i in range(ends)])  12.9 us
    dot_general x8, matrix products, attend(): jnp.einsum('bhij,j->bhi', exponent, places, precision=lax.Precision.HIGHEST)  11.8 us
    all_to_all x1, waiting for transfers between devices, per_device(): lax.all_to_all(right_features, ('col', 'sub'), split_axis=0, concat_axis=...  8.84 us
    all_to_all x1, waiting for transfers between devices, per_device(): lax.all_to_all(left_features, ('col', 'sub'), split_axis=0, concat_axis=1...  6.92 us
  transfers between devices with their start and end apart: 23, of which 13 were waited for; matrix products, arithmetic and copies ran while one was open for 4% of the time, Pallas kernels for 0%

commit v1 on v0

v1 whole, which is shorter than its diff:
```python
import functools

import jax
import jax.numpy as jnp
from jax import lax
from jax.experimental import pallas as pl
from jax.experimental.pallas import tpu as pltpu
from jax.sharding import PartitionSpec as P

C = 128
HEADS = 8
HEAD = 16
CONV = 64
RIM = 5
SLOTS = 8
BLOCK = 128
F32 = jnp.float32
BF16 = jnp.bfloat16
GROUP = ("col", "sub")
BANDS = ("row", "col", "sub")


def dot(a, b, dims):
    return lax.dot_general(a, b, (dims, ((), ())), preferred_element_type=F32)


def attention_row(left, right, qw, kw, vw, ow, occ):
    length = left.shape[0]
    blocks = length // BLOCK
    queries = (dot(qw, left, ((1,), (1,))) * (HEAD**-0.5)).astype(BF16)
    keys = dot(right, kw, ((1,), (0,))).astype(BF16)
    values = dot(vw, right, ((1,), (1,))).astype(BF16)

    channel = lax.broadcasted_iota(jnp.int32, (1, C), 1)
    scores = []
    for j in range(blocks):
        part = keys[BLOCK * j : BLOCK * (j + 1)]
        by_head = jnp.concatenate(
            [jnp.where(channel // HEAD == h, part, jnp.zeros_like(part)) for h in range(HEADS)],
            axis=0,
        )
        scores.append(dot(by_head, queries[:, BLOCK * j :], ((1,), (0,))))

    key_at = lax.broadcasted_iota(jnp.int32, (BLOCK, BLOCK), 0)
    query_at = lax.broadcasted_iota(jnp.int32, (BLOCK, BLOCK), 1)
    allowed = key_at <= query_at
    line = lax.broadcasted_iota(jnp.int32, (HEAD, length), 0)
    place = lax.broadcasted_iota(jnp.int32, (HEAD, length), 1)
    counts = jnp.where(
        line == 0,
        1,
        jnp.where(line == 1, place % BLOCK, jnp.where(line == 2, place - place % BLOCK, 0)),
    )
    counts = counts.astype(F32).astype(BF16)

    heads = [[] for _ in range(blocks)]
    means = [jnp.zeros((1, BLOCK), F32) for _ in range(blocks)]
    for h in range(HEADS):
        stacked = jnp.concatenate([values[HEAD * h : HEAD * (h + 1)], counts], axis=0)
        for i in range(blocks):
            parts = []
            for j in range(i + 1):
                piece = scores[j][
                    BLOCK * h : BLOCK * (h + 1), BLOCK * (i - j) : BLOCK * (i - j + 1)
                ]
                if j == i:
                    piece = jnp.where(allowed, piece, -jnp.inf)
                parts.append(piece)
            largest = functools.reduce(
                jnp.maximum, [jnp.max(p, axis=0, keepdims=True) for p in parts]
            )
            expon = jnp.concatenate(
                [jnp.exp(p - largest).astype(BF16) for p in parts], axis=0
            )
            sums = dot(stacked[:, : BLOCK * (i + 1)], expon, ((1,), (0,)))
            inverse = 1.0 / sums[HEAD : HEAD + 1]
            heads[i].append((sums[:HEAD] * inverse).astype(BF16))
            means[i] = means[i] + (sums[HEAD + 1 : HEAD + 2] + sums[HEAD + 2 : HEAD + 3]) * inverse

    head_out = jnp.concatenate([jnp.concatenate(b, axis=0) for b in heads], axis=1)
    mean = jnp.concatenate(means, axis=1)
    column = lax.broadcasted_iota(jnp.int32, (1, length), 1).astype(F32)
    disparity = (HEADS * column - mean) * (8.0 / (HEADS * length))
    attended = dot(ow, head_out, ((1,), (0,)))
    centred = attended - jnp.mean(attended, axis=0, keepdims=True)
    spread = jnp.mean(centred * centred, axis=0, keepdims=True)
    occlusion = jnp.sum(centred * occ, axis=0, keepdims=True) * lax.rsqrt(spread + 1e-05)
    return disparity, occlusion


def attention_kernel(group, at_ref, own_left, own_right, *refs):
    pieces = refs[: group - 1]
    qw, kw, vw, ow, occ, image, stacked_ref, maps_ref, left_s, right_s = refs[group - 1 :]
    tile = own_left.shape[1]
    me = at_ref[0]
    row = pl.program_id(0)
    for k in range(group):
        start = pl.multiple_of((me ^ k) * tile, tile)
        if k == 0:
            left_s[pl.ds(start, tile), :] = own_left[0]
            right_s[pl.ds(start, tile), :] = own_right[0]
        else:
            left_s[pl.ds(start, tile), :] = pieces[k - 1][0, 0]
            right_s[pl.ds(start, tile), :] = pieces[k - 1][1, 0]
    disparity, occlusion = attention_row(
        left_s[...], right_s[...], qw[...], kw[...], vw[...], ow[...], occ[...]
    )
    maps = jnp.concatenate([disparity, occlusion], axis=0)
    maps_ref[row] = maps
    full = jnp.concatenate([maps, jnp.zeros((SLOTS - 2, maps.shape[1]), F32)], axis=0)
    stacked_ref[row] = (full + image[row].astype(F32)).astype(BF16)


def attention(at, left, right, pieces, weights, image, rows, length):
    group = len(pieces) + 1
    tile = left.shape[1]
    own = pl.BlockSpec((1, tile, C), lambda r, at: (at[0] * rows + r, 0, 0))
    piece = pl.BlockSpec((2, 1, tile, C), lambda r, at: (0, r, 0, 0))
    whole = lambda a: pl.BlockSpec(a.shape, lambda r, at, n=a.ndim: (0,) * n)
    return pl.pallas_call(
        functools.partial(attention_kernel, group),
        name="attention",
        out_shape=(
            jax.ShapeDtypeStruct((rows, SLOTS, length), BF16),
            jax.ShapeDtypeStruct((rows, 2, length), F32),
        ),
        grid_spec=pltpu.PrefetchScalarGridSpec(
            num_scalar_prefetch=1,
            grid=(rows,),
            in_specs=[own, own]
            + [piece] * (group - 1)
            + [whole(w) for w in weights]
            + [whole(image)],
            out_specs=(
                pl.BlockSpec((rows, SLOTS, length), lambda r, at: (0, 0, 0)),
                pl.BlockSpec((rows, 2, length), lambda r, at: (0, 0, 0)),
            ),
            scratch_shapes=[pltpu.VMEM((length, C), BF16)] * 2,
        ),
        compiler_params=pltpu.CompilerParams(
            dimension_semantics=("arbitrary",), vmem_limit_bytes=32 << 20
        ),
    )(at, left, right, *pieces, *weights, image)


def spread_taps(x):
    length = x.shape[1]
    column = lax.broadcasted_iota(jnp.int32, (1, length), 1)
    before = jnp.where(column == 0, 0.0, pltpu.roll(x, 1, 1))
    after = jnp.where(column == length - 1, 0.0, pltpu.roll(x, length - 1, 1))
    return before, x, after


def conv_rows(source, weight, outs, count, finish):
    def at(q):
        p = dot(weight[...], source[q], ((1,), (0,)))
        return p[:outs], p[outs : 2 * outs], p[2 * outs :]

    top0, top1, _ = at(0)
    next0, next1, _ = at(1)
    del top1

    def body(r, carry):
        first, second = carry
        p0, p1, p2 = at(r + 2)
        finish(r, first + p2)
        return second + p1, p0

    lax.fori_loop(0, count, body, (top0 + next1, next0))


def conv_kernel(group, hops, at_ref, own, maps, *refs):
    others = refs[: 2 * hops]
    w1, w2, w3, w4, w5 = refs[2 * hops : 2 * hops + 5]
    outs = refs[2 * hops + 5 : 2 * hops + 5 + group]
    x0, x1, x2, x3, x4 = refs[2 * hops + 5 + group :]
    rows, _, length = own.shape
    me, place, last = at_ref[0], at_ref[1], at_ref[2]
    base = place * rows

    def put(q, block):
        before, same, after = spread_taps(block.astype(F32))
        zero = jnp.zeros_like(same)
        x0[q] = jnp.concatenate([before, same, after, zero], axis=0).astype(BF16)

    for q in range(rows):
        put(RIM + q, own[q])
    for d in range(1, hops + 1):
        flag = jnp.bitwise_and(place, d) != 0
        a, b = others[2 * d - 2], others[2 * d - 1]
        for q in range(rows):
            up = RIM - d * rows + q
            if up >= 0:
                put(up, jnp.where(flag, a[q], b[q]))
            down = RIM + d * rows + q
            if down < rows + 2 * RIM:
                put(down, jnp.where(flag, b[q], a[q]))

    def store(target, lead, residual=None):
        def finish(r, total):
            if residual is not None:
                total = total + residual[r + 2, CONV : 2 * CONV].astype(F32)
            g = base + r - lead
            inside = jnp.logical_and(g >= 0, g < last)
            y = jnp.where(inside, jnp.maximum(total, 0.0), 0.0)
            before, same, after = spread_taps(y)
            target[r, :CONV] = before.astype(BF16)
            target[r, CONV : 2 * CONV] = same.astype(BF16)
            target[r, 2 * CONV :] = after.astype(BF16)

        return finish

    conv_rows(x0, w1, CONV, rows + 8, store(x1, 4))
    conv_rows(x1, w2, CONV, rows + 6, store(x2, 3))
    conv_rows(x2, w3, CONV, rows + 4, store(x3, 2, x1))
    conv_rows(x3, w4, CONV, rows + 2, store(x4, 1))

    tile = length // group

    def last_row(r, total):
        m = maps[r]
        disparity = m[:1] + total[:1]
        occlusion = jax.nn.sigmoid(m[1:2] + total[1:2])
        both = jnp.concatenate([disparity, occlusion], axis=0)
        cut = [both[:, tile * c : tile * (c + 1)] for c in range(group)]
        for k in range(group):
            pick = cut[0]
            for c in range(1, group):
                pick = jnp.where((me ^ k) == c, cut[c], pick)
            outs[k][r] = pick

    conv_rows(x4, w5, SLOTS, rows, last_row)


def convolutions(at, own, maps, others, weights, group):
    rows, _, length = own.shape
    tile = length // group
    hops = len(others) // 2
    vmem = pl.BlockSpec(memory_space=pltpu.VMEM)
    depth = 3 * CONV
    return pl.pallas_call(
        functools.partial(conv_kernel, group, hops),
        name="convolutions",
        out_shape=[jax.ShapeDtypeStruct((rows, 2, tile), F32)] * group,
        in_specs=[pl.BlockSpec(memory_space=pltpu.SMEM)]
        + [vmem] * (2 + len(others) + len(weights)),
        out_specs=[vmem] * group,
        scratch_shapes=[
            pltpu.VMEM((rows + 10, 4 * SLOTS, length), BF16),
            pltpu.VMEM((rows + 8, depth, length), BF16),
            pltpu.VMEM((rows + 6, depth, length), BF16),
            pltpu.VMEM((rows + 4, depth, length), BF16),
            pltpu.VMEM((rows + 2, depth, length), BF16),
        ],
        compiler_params=pltpu.CompilerParams(vmem_limit_bytes=40 << 20),
    )(at, own, maps, *others, *weights)


def place_kernel(group, at_ref, *refs):
    pieces, (first, second) = refs[:group], refs[group:]
    rows = pieces[0].shape[0]
    me = at_ref[0]
    for k in range(group):
        start = (me ^ k) * rows
        for r in range(rows):
            first[pl.ds(start + r, 1), :] = pieces[k][r, 0:1]
            second[pl.ds(start + r, 1), :] = pieces[k][r, 1:2]


def place_rows(at, pieces):
    group = len(pieces)
    rows, _, tile = pieces[0].shape
    vmem = pl.BlockSpec(memory_space=pltpu.VMEM)
    return pl.pallas_call(
        functools.partial(place_kernel, group),
        name="place",
        out_shape=[jax.ShapeDtypeStruct((rows * group, tile), F32)] * 2,
        in_specs=[pl.BlockSpec(memory_space=pltpu.SMEM)] + [vmem] * group,
        out_specs=[vmem] * 2,
    )(at, *pieces)


def swap(x, k):
    count = lax.axis_size(GROUP)
    return lax.ppermute(x, GROUP, [(i, i ^ k) for i in range(count)])


def neighbours(x, d):
    count = lax.axis_size(BANDS)
    even = [(i, i ^ d) for i in range(count)]
    odd = [(i, ((i + d) ^ d) - d) for i in range(count)]
    odd = [(i, j) for i, j in odd if 0 <= j < count]
    return [lax.ppermute(x, BANDS, even), lax.ppermute(x, BANDS, odd)]


def stack_taps(weight, outs, channels):
    o, k = weight.shape[1:]
    w = jnp.pad(weight.reshape(3, 3, o, k), ((0, 0), (0, 0), (0, outs - o), (0, channels - k)))
    return w.transpose(0, 2, 1, 3).reshape(3 * outs, 3 * channels)


def per_device(
    left_features,
    right_features,
    left_image,
    query_key,
    value_weight,
    out_weight,
    occlusion_weight,
    first_conv,
    middle_conv,
    last_conv,
):
    height, tile, _ = left_features.shape
    group = lax.axis_size(GROUP)
    rows = height // group
    length = tile * group
    me = lax.axis_index(GROUP)
    place = lax.axis_index(BANDS)
    at = jnp.stack([me, place, jnp.int32(rows * lax.axis_size(BANDS))]).astype(jnp.int32)

    def mine(x, k, axis=0):
        return lax.dynamic_slice_in_dim(x, (me ^ k) * rows, rows, axis)

    sent = {
        k: jnp.stack([mine(left_features, k), mine(right_features, k)]) for k in range(1, group)
    }
    pieces = {k: swap(sent[k], k) for k in range(group - 1, 0, -1)}
    pieces = [pieces[k] for k in range(1, group)]

    image = left_image.astype(BF16).transpose(1, 0, 2)
    image = jnp.pad(image, ((0, 0), (2, SLOTS - 5), (0, 0)))
    strips = [mine(image, 0)] + [swap(mine(image, k), k) for k in range(1, group)]
    width = 1
    while width < group:
        high = (me & width) != 0
        strips = [
            jnp.where(
                high,
                jnp.concatenate([strips[n + 1], strips[n]], axis=2),
                jnp.concatenate([strips[n], strips[n + 1]], axis=2),
            )
            for n in range(0, len(strips), 2)
        ]
        width *= 2
    image = strips[0]

    weights = (
        query_key.T,
        query_key,
        value_weight.T,
        out_weight.T,
        occlusion_weight[:, None],
    )
    stacked, maps = attention(
        at, left_features, right_features, pieces, weights, image, rows, length
    )

    others = []
    for d in range(1, -(-RIM // rows) + 1):
        others += neighbours(stacked, d)
    first = jnp.pad(stack_taps(first_conv, CONV, SLOTS), ((0, 0), (0, SLOTS)))
    convs = (
        first,
        stack_taps(middle_conv[0], CONV, CONV),
        stack_taps(middle_conv[1], CONV, CONV),
        stack_taps(middle_conv[2], CONV, CONV),
        stack_taps(last_conv, SLOTS, CONV),
    )
    results = convolutions(at, stacked, maps, others, convs, group)
    results = [results[0]] + [swap(results[k], k) for k in range(1, group)]
    return tuple(place_rows(at, results))


def solution(mesh):
    tiles = P(("grp", "row"), ("col", "sub"))
    placed = (
        P(("grp", "row"), ("col", "sub"), None),
        P(("grp", "row"), ("col", "sub"), None),
        P(None, ("grp", "row"), ("col", "sub")),
    ) + (P(),) * 7
    return jax.shard_map(
        per_device, mesh=mesh, in_specs=placed, out_specs=(tiles, tiles), check_vma=False
    )
```

time: 170 us -> 60.9 us (0.36); the launches traced: 166 us -> 60.5 us
  matrix products: 52.6 us -> 0 us
  waiting for transfers between devices: 49.4 us -> 9.99 us
  starting transfers between devices: 52.5 us -> 13.3 us
  Pallas kernels: 0 us -> 28.2 us
  other arithmetic: 6.97 us -> 1.85 us
  local copies, waits for them, and re-layouts: 3.3 us -> 6.18 us
    dot_general x74 -> x0, matrix products: 52.6 us -> none  [the longest x45 16.7 us: conv_valid(): jnp.einsum('oc,crw->orw', weight[offset], window, preferred_element_type=...]
    ppermute x20 -> x11, starting transfers between devices: 41.5 us -> 13.3 us  [the longest x9 12.5 us: swap(): return lax.ppermute(x, GROUP, [(i, i ^ k) for i in range(count)])]
    pallas_call x0 -> x3, Pallas kernels: none -> 28.2 us  [the longest x1 17.8 us: convolutions(): pl.pallas_call(functools.partial(conv_kernel, group, hops), name='convolu...]
    ppermute x20 -> x11, waiting for transfers between devices: 29.8 us -> 9.99 us  [the longest x9 9.98 us: swap(): return lax.ppermute(x, GROUP, [(i, i ^ k) for i in range(count)])]
    all_to_all x3 -> x0, waiting for transfers between devices: 19.6 us -> none  [the longest x1 8.84 us: per_device(): lax.all_to_all(right_features, ('col', 'sub'), split_axis=0, concat_axis=...]
    all_to_all x3 -> x0, starting transfers between devices: 10.9 us -> none  [the longest x1 4.22 us: per_device(): lax.all_to_all(right_features, ('col', 'sub'), split_axis=0, concat_axis=...]
    reduce_sum x17 -> x0, other arithmetic: 3.32 us -> none  [the longest x8 3 us: attend(): totals = jnp.sum(exponent, axis=-1, keepdims=True)]
    unnamed x18 -> x33, local copies, waits for them, and re-layouts: 1.81 us -> 3.46 us
  transfers between devices with their start and end apart: 23 -> 11, of which waited for: 13 -> 4; matrix products, arithmetic and copies ran while one was open for 4% -> 6% of each run, Pallas kernels for 0% -> 0%
where the time goes in v1:
time: 60.9 us; the launch traced here: 60.5 us
  Pallas kernels  28.2 us (46%)
  starting transfers between devices  13.3 us (22%)
  waiting for transfers between devices  9.99 us (16%)
  local copies, waits for them, and re-layouts  6.18 us (10%)
  other arithmetic  1.85 us (3%)
  between operations  0.95 us (2%)
    pallas_call x1, Pallas kernels, convolutions(): pl.pallas_call(functools.partial(conv_kernel, group, hops), name='convolu...  17.8 us
    ppermute x9, starting transfers between devices, swap(): return lax.ppermute(x, GROUP, [(i, i ^ k) for i in range(count)])  12.5 us
    ppermute x9, waiting for transfers between devices, swap(): return lax.ppermute(x, GROUP, [(i, i ^ k) for i in range(count)])  9.98 us
    pallas_call x1, Pallas kernels, attention(): pl.pallas_call(functools.partial(attention_kernel, group), name='attentio...  9 us
    unnamed x33, local copies, waits for them, and re-layouts  3.46 us
    pallas_call x1, Pallas kernels, place_rows(): pl.pallas_call(functools.partial(place_kernel, group), name='place', out_...  1.44 us
    another operation x1, local copies, waits for them, and re-layouts, per_device(): jnp.stack([mine(left_features, k), mine(right_features, k)])  1.29 us
  transfers between devices with their start and end apart: 11, of which 4 were waited for; matrix products, arithmetic and copies ran while one was open for 6% of the time, Pallas kernels for 0%

profile of v1, /device:TPU:0, one launch (start us, length us, event | category | flops | bytes accessed | tf_op | source)
XLA Modules:
  0.0 60.5 jit_solution(7728835533945075170)
XLA Ops:
  0.7 1.3 %dynamic-slice_bitcast_fusion = (bf16[1,8,64,128]{3,2,1,0:T(8,128)(2,1)S(1)}, bf16[1,8,64,128]{3,2,1,0:T(8,128)(2,1)S(1)}, bf16[1,8,64,128]{3,2,1,0:T(8,128)(2,1...) fusion(bf16[32,64,128]{2,1,0:T(8,128)(2,1)} %own_right.1, ...), kind=kLoop, calls=%fused_computation.6 | loop fusion | bytes 1572876 | tf_op jit(solution)/shard_map/stack | solution.py:326
  2.0 2.4 %collective-permute-start.2 = (bf16[2,8,64,128]{3,2,1,0:T(8,128)(2,1)S(1)}, bf16[2,8,64,128]{3,2,1,0:T(8,128)(2,1)S(1)}, u32[]{:S(2)}, u32[]{:S(2)}) collective-permute-start(bf16[2,8,64,128]{3,2,1,0:T(8,128)(2,1)S(1)} %pad_maximum_fusion.2), channel_id=1, source_target_pairs={{0,3},{1,2},{2,1},{3,0},{4,7},{5,6},{6,5},{7,4},{8,11},{9,10},{10,... | collective-permute-start | bytes 786440 | tf_op jit(solution)/shard_map/ppermute | solution.py:285
  4.5 0.0 copy-start.5
  4.5 0.6 %collective-permute-start.1 = (bf16[2,8,64,128]{3,2,1,0:T(8,128)(2,1)S(1)}, bf16[2,8,64,128]{3,2,1,0:T(8,128)(2,1)S(1)}, u32[]{:S(2)}, u32[]{:S(2)}) collective-permute-start(bf16[2,8,64,128]{3,2,1,0:T(8,128)(2,1)S(1)} %pad_maximum_fusion.1), channel_id=1, source_target_pairs={{0,2},{1,3},{2,0},{3,1},{4,6},{5,7},{6,4},{7,5},{8,10},{9,11},{10,... | collective-permute-start | bytes 786440 | tf_op jit(solution)/shard_map/ppermute | solution.py:285
  5.1 0.7 %pad_maximum_fusion = bf16[2,8,64,128]{3,2,1,0:T(8,128)(2,1)} fusion(bf16[1,8,64,128]{3,2,1,0:T(8,128)(2,1)S(1)} %get-tuple-element.19, bf16[1,8,64,128]{3,2,1,0:T(8,128)(2,1)S(1)} %get-tuple-element.27), kind=kLoop, calls=%fused_computation | loop fusion | flops 131072 | bytes 524288 | tf_op jit(solution)/shard_map/stack | solution.py:326
  5.8 0.1 collective-permute-start
  6.0 0.0 copy-start.9
  6.0 0.0 copy-start.14
  6.0 0.0 copy-start.7
  6.1 1.5 %collective-permute-start.3 = (bf16[8,8,64]{2,1,0:T(8,128)(2,1)S(1)}, bf16[8,8,64]{2,1,0:T(8,128)(2,1)}, u32[]{:S(2)}, u32[]{:S(2)}) collective-permute-start(bf16[8,8,64]{2,1,0:T(8,128)(2,1)S(1)} %get-tuple-element.23), channel_id=1, source_target_pairs={{0,3},{1,2},{2,1},{3,0},{4,7},{5,6},{6,5},{7,4},{8,11},{9,10},{10,... | collective-permute-start | bytes 24584 | tf_op jit(solution)/shard_map/ppermute | solution.py:285
  7.6 0.6 collective-permute-start.4
  8.3 0.1 pad_add_fusion.at_ref
  8.3 0.1 copy.37.refs_7_
  8.5 0.0 copy-start.2
  8.5 0.1 copy.35
  8.6 0.7 %copy-done.2 = bf16[128,128]{1,0:T(8,128)(2,1)S(1)} copy-done((bf16[128,128]{1,0:T(8,128)(2,1)S(1)}, bf16[128,128]{1,0:T(8,128)(2,1)}, u32[]{:S(2)}) %copy-start.2) | copy-done | bytes 32792
  9.3 0.1 copy.33
  9.4 0.6 %copy-done.8 = bf16[128,128]{1,0:T(8,128)(2,1)S(1)} copy-done((bf16[128,128]{1,0:T(8,128)(2,1)S(1)}, bf16[128,128]{1,0:T(8,128)(2,1)}, u32[]{:S(2)}) %copy-start.8) | copy-done | bytes 32792
  10.0 0.1 copy.34
  10.1 0.6 copy-done.13
  10.7 6.4 %collective-permute-done.3 = bf16[8,8,64]{2,1,0:T(8,128)(2,1)} collective-permute-done((bf16[8,8,64]{2,1,0:T(8,128)(2,1)S(1)}, bf16[8,8,64]{2,1,0:T(8,128)(2,1)}, u32[]{:S(2)}, u32[]{:S(2)}) %collective-permute-start.3) | collective-permute-done | bytes 8224 | tf_op jit(solution)/shard_map/ppermute | solution.py:285
  17.1 0.3 collective-permute-start.5
  17.4 0.3 collective-permute-done.4
  17.7 0.9 %maximum_select_fusion.1 = bf16[8,8,128]{2,1,0:T(8,128)(2,1)S(1)} fusion(bf16[8,8,64]{2,1,0:T(8,128)(2,1)} %collective-permute-done.4, bf16[8,8,64]{2,1,0:T(8,128)(2,1)} %collective-permute-done.3, pred[]{:T(512)S(6)} %ne.7), kind=kLoop, calls=%fused_computation.20 | loop fusion | flops 73728 | bytes 32769 | tf_op jit(solution)/shard_map/jit(_where)/select_n | solution.py:338
  18.6 0.0 collective-permute-done.5
  18.6 0.1 maximum_select_fusion.2
  18.7 0.0 collective-permute-done.2.refs_2_
  18.7 0.0 collective-permute-done.1.refs_1_
  18.8 9.0 %attention.1 = (bf16[8,8,256]{2,1,0:T(8,128)(2,1)S(1)}, f32[8,2,256]{2,1,0:T(2,128)S(1)}) custom-call(s32[3]{0:T(128)S(1)} %pad_add_fusion.at_ref, bf16[32,64,128]{2,1,0:T(8,128)(2,1)S(1)} %copy-done, bf16[32,64,128]{2,1,0:T(8,128)(2,1)S(1)} %copy-done.1, bf16[2,8,64,128]{3,2,1,0:T(8,128)(2,1)S(1)} %collective-permute-done.refs_0_, ...), custom_call_target="tpu_custom_call" | custom-call | tf_op jit(solution)/shard_map/attention/pallas_call | solution.py:120
  27.8 0.1 collective-permute-start.6
  27.9 0.7 %collective-permute-start.7 = (bf16[8,8,256]{2,1,0:T(8,128)(2,1)S(1)}, bf16[8,8,256]{2,1,0:T(8,128)(2,1)S(1)}, u32[]{:S(2)}, u32[]{:S(2)}) collective-permute-start(bf16[8,8,256]{2,1,0:T(8,128)(2,1)S(1)} %get-tuple-element.8.own), channel_id=1, source_target_pairs={{1,2},{2,1},{3,4},{4,3},{5,6},{6,5},{7,8},{8,7},{9,10},{10,9},{11,... | collective-permute-start | bytes 98312 | tf_op jit(solution)/shard_map/ppermute | solution.py:293
  28.6 0.1 copy.50
  28.7 0.2 reshape.27.refs_3_
  28.9 0.1 copy.49
  29.0 0.2 reshape.28.refs_4_
  29.2 0.1 copy.48
  29.3 0.2 reshape.29.refs_5_
  29.5 0.1 reshape.26
  29.6 0.1 copy.39
  29.7 0.1 reshape.31.refs_6_
  29.8 17.8 %convolutions.1 = (f32[8,2,64]{2,1,0:T(2,128)S(1)}, f32[8,2,64]{2,1,0:T(2,128)S(1)}, f32[8,2,64]{2,1,0:T(2,128)S(1)}, f32[8,2,64]{2,1,0:T(2,128)S(1)}) custom-call(s32[3]{0:T(128)S(1)} %pad_add_fusion.at_ref, bf16[8,8,256]{2,1,0:T(8,128)(2,1)S(1)} %get-tuple-element.8.own, f32[8,2,256]{2,1,0:T(2,128)S(1)} %get-tuple-element.9.maps, ...), custom_call_target="tpu_custom_call" | custom-call | tf_op jit(solution)/shard_map/convolutions/pallas_call | solution.py:241
  47.6 0.6 %copy-done.3 = f32[8,2,64]{2,1,0:T(2,128)} copy-done((f32[8,2,64]{2,1,0:T(2,128)}, f32[8,2,64]{2,1,0:T(2,128)S(1)}, u32[]{:S(2)}) %copy-start.3) | copy-done | bytes 4120
  48.2 6.6 %collective-permute-start.10 = (f32[8,2,64]{2,1,0:T(2,128)S(1)}, f32[8,2,64]{2,1,0:T(2,128)S(1)}, u32[]{:S(2)}, u32[]{:S(2)}) collective-permute-start(f32[8,2,64]{2,1,0:T(2,128)S(1)} %get-tuple-element.13), channel_id=1, source_target_pairs={{0,3},{1,2},{2,1},{3,0},{4,7},{5,6},{6,5},{7,4},{8,11},{9,10},{10,... | collective-permute-start | bytes 12296 | tf_op jit(solution)/shard_map/ppermute | solution.py:285
  54.8 0.4 collective-permute-start.9
  55.2 1.0 %collective-permute-done.10.refs_3_ = f32[8,2,64]{2,1,0:T(2,128)S(1)} collective-permute-done((f32[8,2,64]{2,1,0:T(2,128)S(1)}, f32[8,2,64]{2,1,0:T(2,128)S(1)}, u32[]{:S(2)}, u32[]{:S(2)}) %collective-permute-start.10) | collective-permute-done | bytes 4128 | tf_op jit(solution)/shard_map/ppermute | solution.py:285
  56.2 2.3 %collective-permute-done.9.refs_2_ = f32[8,2,64]{2,1,0:T(2,128)S(1)} collective-permute-done((f32[8,2,64]{2,1,0:T(2,128)S(1)}, f32[8,2,64]{2,1,0:T(2,128)S(1)}, u32[]{:S(2)}, u32[]{:S(2)}) %collective-permute-start.9) | collective-permute-done | bytes 4128 | tf_op jit(solution)/shard_map/ppermute | solution.py:285
  58.5 0.6 copy-done.12
  59.1 1.4 %place.1 = (f32[32,64]{1,0:T(8,128)}, f32[32,64]{1,0:T(8,128)}) custom-call(s32[3]{0:T(128)} %copy-done.4, f32[8,2,64]{2,1,0:T(2,128)} %copy-done.3, f32[8,2,64]{2,1,0:T(2,128)} %copy-done.11, f32[8,2,64]{2,1,0:T(2,128)} %copy-done.12, f32[8,2,64]{2,1,0:T(2,128)} %copy-done.10), custom_call_target="tpu_custom_call" | custom-call | tf_op jit(solution)/shard_map/place/pallas_call | solution.py:274
  (37 shorter events, 0.3 us)
Async XLA Ops:
  2.0 16.7 %collective-permute-start.2 = (bf16[2,8,64,128]{3,2,1,0:T(8,128)(2,1)S(1)}, bf16[2,8,64,128]{3,2,1,0:T(8,128)(2,1)S(1)}, u32[]{:S(2)}, u32[]{:S(2)}) collective-permute-start(bf16[2,8,64,128]{3,2,1,0:T(8,128)(2,1)S(1)} %pad_maximum_fusion.2), channel_id=1, source_target_pairs={{0,3},{1,2},{2,1},{3,0},{4,7},{5,6},{6,5},{7,4},{8,11},{9,10},{10,... | collective-permute-start | bytes 786440 | tf_op jit(solution)/shard_map/ppermute | solution.py:285
  4.5 3.7 %copy-start.5 = (bf16[3,9,64,64]{3,2,1,0:T(8,128)(2,1)S(1)}, bf16[3,9,64,64]{3,2,1,0:T(8,128)(2,1)}, u32[]{:S(2)}) copy-start(bf16[3,9,64,64]{3,2,1,0:T(8,128)(2,1)} %param.18) | copy-start | bytes 663556
  4.5 14.3 %collective-permute-start.1 = (bf16[2,8,64,128]{3,2,1,0:T(8,128)(2,1)S(1)}, bf16[2,8,64,128]{3,2,1,0:T(8,128)(2,1)S(1)}, u32[]{:S(2)}, u32[]{:S(2)}) collective-permute-start(bf16[2,8,64,128]{3,2,1,0:T(8,128)(2,1)S(1)} %pad_maximum_fusion.1), channel_id=1, source_target_pairs={{0,2},{1,3},{2,0},{3,1},{4,6},{5,7},{6,4},{7,5},{8,10},{9,11},{10,... | collective-permute-start | bytes 786440 | tf_op jit(solution)/shard_map/ppermute | solution.py:285
  5.1 0.9 %copy-start.6 = (f32[3,32,64]{2,1,0:T(8,128)S(1)}, f32[3,32,64]{2,1,0:T(8,128)}, u32[]{:S(2)}) copy-start(f32[3,32,64]{2,1,0:T(8,128)} %param.12) | copy-start | bytes 73732
  5.8 12.9 %collective-permute-start = (bf16[2,8,64,128]{3,2,1,0:T(8,128)(2,1)}, bf16[2,8,64,128]{3,2,1,0:T(8,128)(2,1)S(1)}, u32[]{:S(2)}, u32[]{:S(2)}) collective-permute-start(bf16[2,8,64,128]{3,2,1,0:T(8,128)(2,1)} %pad_maximum_fusion), channel_id=1, source_target_pairs={{0,1},{1,0},{2,3},{3,2},{4,5},{5,4},{6,7},{7,6},{8,9},{9,8},{10,11... | collective-permute-start | bytes 786440 | tf_op jit(solution)/shard_map/ppermute | solution.py:285
  6.0 2.2 %copy-start.9 = (bf16[9,64,5]{1,2,0:T(8,128)(2,1)S(1)}, bf16[9,64,5]{1,2,0:T(8,128)(2,1)}, u32[]{:S(2)}) copy-start(bf16[9,64,5]{1,2,0:T(8,128)(2,1)} %param.17) | copy-start | bytes 17284
  6.0 2.3 %copy-start.14 = (f32[128]{0:T(128)S(1)}, f32[128]{0:T(128)}, u32[]{:S(2)}) copy-start(f32[128]{0:T(128)} %param.16) | copy-start | bytes 1540
  6.0 2.4 %copy-start.7 = (bf16[128,128]{1,0:T(8,128)(2,1)S(1)}, bf16[128,128]{1,0:T(8,128)(2,1)}, u32[]{:S(2)}) copy-start(bf16[128,128]{1,0:T(8,128)(2,1)} %param.15) | copy-start | bytes 98308
  6.1 11.0 %collective-permute-start.3 = (bf16[8,8,64]{2,1,0:T(8,128)(2,1)S(1)}, bf16[8,8,64]{2,1,0:T(8,128)(2,1)}, u32[]{:S(2)}, u32[]{:S(2)}) collective-permute-start(bf16[8,8,64]{2,1,0:T(8,128)(2,1)S(1)} %get-tuple-element.23), channel_id=1, source_target_pairs={{0,3},{1,2},{2,1},{3,0},{4,7},{5,6},{6,5},{7,4},{8,11},{9,10},{10,... | collective-permute-start | bytes 24584 | tf_op jit(solution)/shard_map/ppermute | solution.py:285
  7.6 10.1 %collective-permute-start.4 = (bf16[8,8,64]{2,1,0:T(8,128)(2,1)S(1)}, bf16[8,8,64]{2,1,0:T(8,128)(2,1)}, u32[]{:S(2)}, u32[]{:S(2)}) collective-permute-start(bf16[8,8,64]{2,1,0:T(8,128)(2,1)S(1)} %get-tuple-element.24), channel_id=1, source_target_pairs={{0,2},{1,3},{2,0},{3,1},{4,6},{5,7},{6,4},{7,5},{8,10},{9,11},{10,... | collective-permute-start | bytes 24584 | tf_op jit(solution)/shard_map/ppermute | solution.py:285
  8.2 10.6 %copy-start = (bf16[32,64,128]{2,1,0:T(8,128)(2,1)S(1)}, bf16[32,64,128]{2,1,0:T(8,128)(2,1)}, u32[]{:S(2)}) copy-start(bf16[32,64,128]{2,1,0:T(8,128)(2,1)} %own_left.1) | copy-start | bytes 1572868
  8.2 10.6 %copy-start.1 = (bf16[32,64,128]{2,1,0:T(8,128)(2,1)S(1)}, bf16[32,64,128]{2,1,0:T(8,128)(2,1)}, u32[]{:S(2)}) copy-start(bf16[32,64,128]{2,1,0:T(8,128)(2,1)} %own_right.1) | copy-start | bytes 1572868
  8.3 21.5 %copy-start.4 = (s32[3]{0:T(128)}, s32[3]{0:T(128)S(1)}, u32[]{:S(2)}) copy-start(s32[3]{0:T(128)S(1)} %pad_add_fusion.at_ref) | copy-start | bytes 40
  8.5 0.8 %copy-start.2 = (bf16[128,128]{1,0:T(8,128)(2,1)S(1)}, bf16[128,128]{1,0:T(8,128)(2,1)}, u32[]{:S(2)}) copy-start(bf16[128,128]{1,0:T(8,128)(2,1)} %refs_4_.1) | copy-start | bytes 98308
  9.3 0.8 %copy-start.8 = (bf16[128,128]{1,0:T(8,128)(2,1)S(1)}, bf16[128,128]{1,0:T(8,128)(2,1)}, u32[]{:S(2)}) copy-start(bf16[128,128]{1,0:T(8,128)(2,1)} %param.14) | copy-start | bytes 98308
  10.0 0.7 %copy-start.13 = (bf16[9,2,64]{2,1,0:T(2,128)(2,1)S(1)}, bf16[9,2,64]{2,1,0:T(2,128)(2,1)}, u32[]{:S(2)}) copy-start(bf16[9,2,64]{2,1,0:T(2,128)(2,1)} %param.19) | copy-start | bytes 6916
  17.1 1.5 %collective-permute-start.5 = (bf16[8,8,64]{2,1,0:T(8,128)(2,1)S(1)}, bf16[8,8,64]{2,1,0:T(8,128)(2,1)S(1)}, u32[]{:S(2)}, u32[]{:S(2)}) collective-permute-start(bf16[8,8,64]{2,1,0:T(8,128)(2,1)S(1)} %get-tuple-element.25), channel_id=1, source_target_pairs={{0,1},{1,0},{2,3},{3,2},{4,5},{5,4},{6,7},{7,6},{8,9},{9,8},{10,11... | collective-permute-start | bytes 24584 | tf_op jit(solution)/shard_map/ppermute | solution.py:285
  27.8 2.0 %collective-permute-start.6 = (bf16[8,8,256]{2,1,0:T(8,128)(2,1)S(1)}, bf16[8,8,256]{2,1,0:T(8,128)(2,1)S(1)}, u32[]{:S(2)}, u32[]{:S(2)}) collective-permute-start(bf16[8,8,256]{2,1,0:T(8,128)(2,1)S(1)} %get-tuple-element.8.own), channel_id=1, source_target_pairs={{0,1},{1,0},{2,3},{3,2},{4,5},{5,4},{6,7},{7,6},{8,9},{9,8},{10,11... | collective-permute-start | bytes 98312 | tf_op jit(solution)/shard_map/ppermute | solution.py:293
  27.9 1.9 %collective-permute-start.7 = (bf16[8,8,256]{2,1,0:T(8,128)(2,1)S(1)}, bf16[8,8,256]{2,1,0:T(8,128)(2,1)S(1)}, u32[]{:S(2)}, u32[]{:S(2)}) collective-permute-start(bf16[8,8,256]{2,1,0:T(8,128)(2,1)S(1)} %get-tuple-element.8.own), channel_id=1, source_target_pairs={{1,2},{2,1},{3,4},{4,3},{5,6},{6,5},{7,8},{8,7},{9,10},{10,9},{11,... | collective-permute-start | bytes 98312 | tf_op jit(solution)/shard_map/ppermute | solution.py:293
  47.6 0.6 %copy-start.3 = (f32[8,2,64]{2,1,0:T(2,128)}, f32[8,2,64]{2,1,0:T(2,128)S(1)}, u32[]{:S(2)}) copy-start(f32[8,2,64]{2,1,0:T(2,128)S(1)} %get-tuple-element.10.refs_0_) | copy-start | bytes 12292
  48.2 7.9 %collective-permute-start.10 = (f32[8,2,64]{2,1,0:T(2,128)S(1)}, f32[8,2,64]{2,1,0:T(2,128)S(1)}, u32[]{:S(2)}, u32[]{:S(2)}) collective-permute-start(f32[8,2,64]{2,1,0:T(2,128)S(1)} %get-tuple-element.13), channel_id=1, source_target_pairs={{0,3},{1,2},{2,1},{3,0},{4,7},{5,6},{6,5},{7,4},{8,11},{9,10},{10,... | collective-permute-start | bytes 12296 | tf_op jit(solution)/shard_map/ppermute | solution.py:285
  54.8 1.4 %collective-permute-start.8 = (f32[8,2,64]{2,1,0:T(2,128)S(1)}, f32[8,2,64]{2,1,0:T(2,128)S(1)}, u32[]{:S(2)}, u32[]{:S(2)}) collective-permute-start(f32[8,2,64]{2,1,0:T(2,128)S(1)} %get-tuple-element.11), channel_id=1, source_target_pairs={{0,1},{1,0},{2,3},{3,2},{4,5},{5,4},{6,7},{7,6},{8,9},{9,8},{10,11... | collective-permute-start | bytes 12296 | tf_op jit(solution)/shard_map/ppermute | solution.py:285
  54.8 3.7 %collective-permute-start.9 = (f32[8,2,64]{2,1,0:T(2,128)S(1)}, f32[8,2,64]{2,1,0:T(2,128)S(1)}, u32[]{:S(2)}, u32[]{:S(2)}) collective-permute-start(f32[8,2,64]{2,1,0:T(2,128)S(1)} %get-tuple-element.12), channel_id=1, source_target_pairs={{0,2},{1,3},{2,0},{3,1},{4,6},{5,7},{6,4},{7,5},{8,10},{9,11},{10,... | collective-permute-start | bytes 12296 | tf_op jit(solution)/shard_map/ppermute | solution.py:285
  56.2 2.3 %copy-start.10 = (f32[8,2,64]{2,1,0:T(2,128)}, f32[8,2,64]{2,1,0:T(2,128)S(1)}, u32[]{:S(2)}) copy-start(f32[8,2,64]{2,1,0:T(2,128)S(1)} %collective-permute-done.10.refs_3_) | copy-start | bytes 12292
  56.2 2.3 %copy-start.11 = (f32[8,2,64]{2,1,0:T(2,128)}, f32[8,2,64]{2,1,0:T(2,128)S(1)}, u32[]{:S(2)}) copy-start(f32[8,2,64]{2,1,0:T(2,128)S(1)} %collective-permute-done.8.refs_1_) | copy-start | bytes 12292
  58.5 0.6 copy-start.12

commit v2 on v1

--- a/solution.py
+++ b/solution.py
@@ -88,59 +88,169 @@
     return disparity, occlusion
 
 
-def attention_kernel(group, at_ref, own_left, own_right, *refs):
-    pieces = refs[: group - 1]
-    qw, kw, vw, ow, occ, image, stacked_ref, maps_ref, left_s, right_s = refs[group - 1 :]
-    tile = own_left.shape[1]
-    me = at_ref[0]
-    row = pl.program_id(0)
-    for k in range(group):
-        start = pl.multiple_of((me ^ k) * tile, tile)
-        if k == 0:
-            left_s[pl.ds(start, tile), :] = own_left[0]
-            right_s[pl.ds(start, tile), :] = own_right[0]
-        else:
-            left_s[pl.ds(start, tile), :] = pieces[k - 1][0, 0]
-            right_s[pl.ds(start, tile), :] = pieces[k - 1][1, 0]
-    disparity, occlusion = attention_row(
-        left_s[...], right_s[...], qw[...], kw[...], vw[...], ow[...], occ[...]
-    )
-    maps = jnp.concatenate([disparity, occlusion], axis=0)
-    maps_ref[row] = maps
-    full = jnp.concatenate([maps, jnp.zeros((SLOTS - 2, maps.shape[1]), F32)], axis=0)
-    stacked_ref[row] = (full + image[row].astype(F32)).astype(BF16)
-
-
-def attention(at, left, right, pieces, weights, image, rows, length):
-    group = len(pieces) + 1
-    tile = left.shape[1]
-    own = pl.BlockSpec((1, tile, C), lambda r, at: (at[0] * rows + r, 0, 0))
-    piece = pl.BlockSpec((2, 1, tile, C), lambda r, at: (0, r, 0, 0))
-    whole = lambda a: pl.BlockSpec(a.shape, lambda r, at, n=a.ndim: (0,) * n)
+def strip_lines(rows):
+    return -(-3 * rows // 16) * 16
+
+
+def line_plan(cuts, tile, rows):
+    sizes = [2 * c * tile + (strip_lines(rows) if n == 0 else 0) for n, c in enumerate(cuts)]
+    return [(sum(sizes[:n]), s) for n, s in enumerate(sizes)]
+
+
+def order(k, near):
+    chip, core = k // near, k % near
+    return chip * near + jnp.where(chip % 2 == 0, core, near - 1 - core)
+
+
+def place_of(member, band, group, near):
+    q = order(member, near)
+    return jnp.where(band % 2 == 0, q, group - 1 - q)
+
+
+def shared_place():
+    group, near = lax.axis_size(GROUP), lax.axis_size("sub")
+    me, band = lax.axis_index(GROUP), lax.axis_index("row")
+    return lambda k: place_of(me ^ k, band, group, near)
+
+
+def pack_kernel(partners, cuts, chunks, left, right, image, *refs):
+    outs, image_s, sems, image_sem = refs[-len(partners) - 3 : -3], *refs[-3:]
+    tile = image.shape[2]
+    rows = sum(cuts)
+    plan = line_plan(cuts, tile, rows)
+    share = shared_place()
+    lines = strip_lines(rows)
+    copies = []
+    if 0 in chunks:
+        colours = pltpu.make_async_copy(image, image_s, image_sem)
+        colours.start()
+    n = 0
+    for c in chunks:
+        for k, out in zip(partners, outs):
+            base = plan[c][0] - plan[chunks[0]][0]
+            start = pl.multiple_of((share(k) * rows + sum(cuts[:c])) * tile, tile)
+            for s, side in enumerate((left, right)):
+                copy = pltpu.make_async_copy(
+                    side.at[pl.ds(start, cuts[c] * tile), :],
+                    out.at[pl.ds(base + s * cuts[c] * tile, cuts[c] * tile), :],
+                    sems.at[n],
+                )
+                copy.start()
+                copies.append(copy)
+                n += 1
+    if 0 in chunks:
+        colours.wait()
+        for k, out in zip(partners, outs):
+            strip = [
+                image_s[ch, pl.ds(pl.multiple_of(share(k) * rows, rows), rows), :]
+                for ch in range(3)
+            ]
+            if lines > 3 * rows:
+                strip.append(jnp.zeros((lines - 3 * rows, tile), F32))
+            strip = jnp.concatenate(strip, axis=0)
+            strip = jnp.concatenate([strip, jnp.zeros((lines, C - tile), F32)], axis=1)
+            first = 2 * cuts[0] * tile
+            out[first : first + lines, :] = strip.astype(BF16)
+    for copy in copies:
+        copy.wait()
+
+
+def pack(left, right, image, partners, cuts, chunks, after=()):
+    height, tile, _ = left.shape
+    plan = line_plan(cuts, tile, sum(cuts))
+    size = sum(plan[c][1] for c in chunks)
+    vmem = pl.BlockSpec(memory_space=pltpu.VMEM)
+    hbm = pl.BlockSpec(memory_space=pltpu.HBM)
     return pl.pallas_call(
-        functools.partial(attention_kernel, group),
+        functools.partial(pack_kernel, partners, cuts, chunks),
+        name="pack",
+        out_shape=[jax.ShapeDtypeStruct((size, C), BF16)] * len(partners),
+        in_specs=[hbm] * 3 + [vmem] * len(after),
+        out_specs=[vmem] * len(partners),
+        scratch_shapes=[
+            pltpu.VMEM(image.shape, F32),
+            pltpu.SemaphoreType.DMA((2 * len(partners) * len(chunks),)),
+            pltpu.SemaphoreType.DMA,
+        ],
+        compiler_params=pltpu.CompilerParams(vmem_limit_bytes=16 << 20),
+    )(left.reshape(height * tile, C), right.reshape(height * tile, C), image, *after)
+
+
+def attention_kernel(group, near, cuts, chunk, *refs):
+    pieces, (qw, kw, vw, ow, occ) = refs[:group], refs[group : group + 5]
+    earlier, (stacked_ref, maps_ref, left_s, right_s) = refs[group + 5 : -4], refs[-4:]
+    count, length, _ = left_s.shape
+    tile = length // group
+    rows, offset = sum(cuts), sum(cuts[:chunk])
+    plan = line_plan(cuts, tile, rows)
+    me = lax.axis_index(GROUP)
+    base = [plan[chunk][0] if k < near else 0 for k in range(group)]
+    for n in range(count):
+        for k in range(group):
+            start = pl.multiple_of((me ^ k) * tile, tile)
+            line = base[k] + n * tile
+            left_s[n, pl.ds(start, tile), :] = pieces[k][line : line + tile]
+            line += count * tile
+            right_s[n, pl.ds(start, tile), :] = pieces[k][line : line + tile]
+    if chunk:
+        stacked_ref[...] = earlier[0][...]
+        maps_ref[...] = earlier[1][...]
+    else:
+        first = [b + 2 * count * tile for b in base]
+        strips = [
+            pieces[k][f : f + strip_lines(rows), :tile].astype(F32) for k, f in enumerate(first)
+        ]
+        width = 1
+        while width < group:
+            high = (me & width) != 0
+            strips = [
+                jnp.where(
+                    high,
+                    jnp.concatenate([strips[n + 1], strips[n]], axis=1),
+                    jnp.concatenate([strips[n], strips[n + 1]], axis=1),
+                )
+                for n in range(0, len(strips), 2)
+            ]
+            width *= 2
+        zero = jnp.zeros((1, length), F32)
+        for r in range(rows):
+            colours = [strips[0][ch * rows + r : ch * rows + r + 1] for ch in range(3)]
+            stacked_ref[r] = jnp.concatenate(
+                [zero, zero] + colours + [zero] * (SLOTS - 5), axis=0
+            ).astype(BF16)
+    slot = lax.broadcasted_iota(jnp.int32, (SLOTS, 1), 0)
+    for n in range(count):
+        r = offset + n
+        disparity, occlusion = attention_row(
+            left_s[n], right_s[n], qw[...], kw[...], vw[...], ow[...], occ[...]
+        )
+        maps_ref[r] = jnp.concatenate([disparity, occlusion], axis=0)
+        full = jnp.where(slot == 0, disparity, stacked_ref[r].astype(F32))
+        stacked_ref[r] = jnp.where(slot == 1, occlusion, full).astype(BF16)
+
+
+def attention(pieces, weights, earlier, near, cuts, length):
+    group = len(pieces)
+    chunk = 0 if not earlier else earlier[2]
+    rows, count = sum(cuts), cuts[chunk]
+    vmem = pl.BlockSpec(memory_space=pltpu.VMEM)
+    pairs = count * HEADS * length * length
+    results = pl.pallas_call(
+        functools.partial(attention_kernel, group, near, cuts, chunk),
         name="attention",
         out_shape=(
             jax.ShapeDtypeStruct((rows, SLOTS, length), BF16),
             jax.ShapeDtypeStruct((rows, 2, length), F32),
         ),
-        grid_spec=pltpu.PrefetchScalarGridSpec(
-            num_scalar_prefetch=1,
-            grid=(rows,),
-            in_specs=[own, own]
-            + [piece] * (group - 1)
-            + [whole(w) for w in weights]
-            + [whole(image)],
-            out_specs=(
-                pl.BlockSpec((rows, SLOTS, length), lambda r, at: (0, 0, 0)),
-                pl.BlockSpec((rows, 2, length), lambda r, at: (0, 0, 0)),
-            ),
-            scratch_shapes=[pltpu.VMEM((length, C), BF16)] * 2,
+        in_specs=[vmem] * (group + len(weights) + len(earlier[:2])),
+        out_specs=(vmem, vmem),
+        scratch_shapes=[pltpu.VMEM((count, length, C), BF16)] * 2,
+        compiler_params=pltpu.CompilerParams(vmem_limit_bytes=24 << 20),
+        cost_estimate=pl.CostEstimate(
+            flops=pairs * 4 * C, transcendentals=pairs, bytes_accessed=8 * count * length * C
         ),
-        compiler_params=pltpu.CompilerParams(
-            dimension_semantics=("arbitrary",), vmem_limit_bytes=32 << 20
-        ),
-    )(at, left, right, *pieces, *weights, image)
+    )(*pieces, *weights, *earlier[:2])
+    return (*results, chunk + 1)
 
 
 def spread_taps(x):
@@ -166,16 +276,20 @@
         finish(r, first + p2)
         return second + p1, p0
 
-    lax.fori_loop(0, count, body, (top0 + next1, next0))
-
-
-def conv_kernel(group, hops, at_ref, own, maps, *refs):
+    carry = (top0 + next1, next0)
+    for r in range(count):
+        carry = body(r, carry)
+
+
+def conv_kernel(group, hops, own, maps, *refs):
     others = refs[: 2 * hops]
     w1, w2, w3, w4, w5 = refs[2 * hops : 2 * hops + 5]
     outs = refs[2 * hops + 5 : 2 * hops + 5 + group]
     x0, x1, x2, x3, x4 = refs[2 * hops + 5 + group :]
     rows, _, length = own.shape
-    me, place, last = at_ref[0], at_ref[1], at_ref[2]
+    me = lax.axis_index(GROUP)
+    place = lax.axis_index("row") * group + shared_place()(0)
+    last = lax.axis_size(BANDS) * rows
     base = place * rows
 
     def put(q, block):
@@ -221,18 +335,22 @@
         m = maps[r]
         disparity = m[:1] + total[:1]
         occlusion = jax.nn.sigmoid(m[1:2] + total[1:2])
-        both = jnp.concatenate([disparity, occlusion], axis=0)
+        finals[0].append(disparity)
+        finals[1].append(occlusion)
+
+    finals = [], []
+    conv_rows(x4, w5, SLOTS, rows, last_row)
+    for n in range(2):
+        both = jnp.concatenate(finals[n], axis=0)
         cut = [both[:, tile * c : tile * (c + 1)] for c in range(group)]
         for k in range(group):
             pick = cut[0]
             for c in range(1, group):
                 pick = jnp.where((me ^ k) == c, cut[c], pick)
-            outs[k][r] = pick
-
-    conv_rows(x4, w5, SLOTS, rows, last_row)
-
-
-def convolutions(at, own, maps, others, weights, group):
+            outs[k][n] = pick
+
+
+def convolutions(own, maps, others, weights, group):
     rows, _, length = own.shape
     tile = length // group
     hops = len(others) // 2
@@ -241,9 +359,8 @@
     return pl.pallas_call(
         functools.partial(conv_kernel, group, hops),
         name="convolutions",
-        out_shape=[jax.ShapeDtypeStruct((rows, 2, tile), F32)] * group,
-        in_specs=[pl.BlockSpec(memory_space=pltpu.SMEM)]
-        + [vmem] * (2 + len(others) + len(weights)),
+        out_shape=[jax.ShapeDtypeStruct((2, rows, tile), F32)] * group,
+        in_specs=[vmem] * (2 + len(others) + len(weights)),
         out_specs=[vmem] * group,
         scratch_shapes=[
             pltpu.VMEM((rows + 10, 4 * SLOTS, length), BF16),
@@ -253,31 +370,31 @@
             pltpu.VMEM((rows + 2, depth, length), BF16),
         ],
         compiler_params=pltpu.CompilerParams(vmem_limit_bytes=40 << 20),
-    )(at, own, maps, *others, *weights)
-
-
-def place_kernel(group, at_ref, *refs):
-    pieces, (first, second) = refs[:group], refs[group:]
-    rows = pieces[0].shape[0]
-    me = at_ref[0]
+    )(own, maps, *others, *weights)
+
+
+def place_kernel(group, *refs):
+    pieces, outs = refs[:group], refs[group:]
+    rows = pieces[0].shape[1]
+    share = shared_place()
     for k in range(group):
-        start = (me ^ k) * rows
-        for r in range(rows):
-            first[pl.ds(start + r, 1), :] = pieces[k][r, 0:1]
-            second[pl.ds(start + r, 1), :] = pieces[k][r, 1:2]
-
-
-def place_rows(at, pieces):
+        start = pl.multiple_of(share(k) * rows, rows)
+        for n in range(2):
+            outs[n][pl.ds(start, rows), :] = pieces[k][n]
+
+
+def place_rows(pieces):
     group = len(pieces)
-    rows, _, tile = pieces[0].shape
+    _, rows, tile = pieces[0].shape
     vmem = pl.BlockSpec(memory_space=pltpu.VMEM)
     return pl.pallas_call(
         functools.partial(place_kernel, group),
         name="place",
         out_shape=[jax.ShapeDtypeStruct((rows * group, tile), F32)] * 2,
-        in_specs=[pl.BlockSpec(memory_space=pltpu.SMEM)] + [vmem] * group,
+        in_specs=[vmem] * group,
         out_specs=[vmem] * 2,
-    )(at, *pieces)
+        compiler_params=pltpu.CompilerParams(vmem_limit_bytes=4 << 20),
+    )(*pieces)
 
 
 def swap(x, k):
@@ -286,11 +403,24 @@
 
 
 def neighbours(x, d):
-    count = lax.axis_size(BANDS)
+    count, group, near = lax.axis_size(BANDS), lax.axis_size(GROUP), lax.axis_size("sub")
+
+    def device(place):
+        band, q = divmod(place, group)
+        chip, core = divmod(q if band % 2 == 0 else group - 1 - q, near)
+        return band * group + chip * near + (core if chip % 2 == 0 else near - 1 - core)
+
     even = [(i, i ^ d) for i in range(count)]
     odd = [(i, ((i + d) ^ d) - d) for i in range(count)]
-    odd = [(i, j) for i, j in odd if 0 <= j < count]
-    return [lax.ppermute(x, BANDS, even), lax.ppermute(x, BANDS, odd)]
+    return [
+        lax.ppermute(x, BANDS, [(device(i), device(j)) for i, j in pairs if 0 <= j < count])
+        for pairs in (even, odd)
+    ]
+
+
+def chunks_of(rows):
+    first = -(-5 * rows // 8)
+    return (first, rows - first)
 
 
 def stack_taps(weight, outs, channels):
@@ -315,35 +445,21 @@
     group = lax.axis_size(GROUP)
     rows = height // group
     length = tile * group
-    me = lax.axis_index(GROUP)
-    place = lax.axis_index(BANDS)
-    at = jnp.stack([me, place, jnp.int32(rows * lax.axis_size(BANDS))]).astype(jnp.int32)
-
-    def mine(x, k, axis=0):
-        return lax.dynamic_slice_in_dim(x, (me ^ k) * rows, rows, axis)
-
-    sent = {
-        k: jnp.stack([mine(left_features, k), mine(right_features, k)]) for k in range(1, group)
-    }
-    pieces = {k: swap(sent[k], k) for k in range(group - 1, 0, -1)}
-    pieces = [pieces[k] for k in range(1, group)]
-
-    image = left_image.astype(BF16).transpose(1, 0, 2)
-    image = jnp.pad(image, ((0, 0), (2, SLOTS - 5), (0, 0)))
-    strips = [mine(image, 0)] + [swap(mine(image, k), k) for k in range(1, group)]
-    width = 1
-    while width < group:
-        high = (me & width) != 0
-        strips = [
-            jnp.where(
-                high,
-                jnp.concatenate([strips[n + 1], strips[n]], axis=2),
-                jnp.concatenate([strips[n], strips[n + 1]], axis=2),
-            )
-            for n in range(0, len(strips), 2)
-        ]
-        width *= 2
-    image = strips[0]
+    near = lax.axis_size("sub")
+    cuts = chunks_of(rows)
+    features = (left_features, right_features, left_image)
+    chunks = tuple(range(len(cuts)))
+    distant = tuple(range(near, group))
+    close = pack(*features, tuple(range(near)), cuts, chunks)
+    packed = pack(*features, distant, cuts, (0,))
+    tables = (first_conv, middle_conv, last_conv, query_key, value_weight, out_weight)
+    close, packed, tables = lax.optimization_barrier((close, packed, tables))
+    first_conv, middle_conv, last_conv, query_key, value_weight, out_weight = tables
+    far = [[swap(x, k) for k, x in zip(distant, packed)][::1]]
+    close = [close[0]] + [swap(close[k], k) for k in range(1, near)]
+    for c in chunks[1:]:
+        packed = pack(*features, distant, cuts, (c,), (close[-1],))
+        far.append([swap(x, k) for k, x in zip(distant, packed)])
 
     weights = (
         query_key.T,
@@ -352,13 +468,6 @@
         out_weight.T,
         occlusion_weight[:, None],
     )
-    stacked, maps = attention(
-        at, left_features, right_features, pieces, weights, image, rows, length
-    )
-
-    others = []
-    for d in range(1, -(-RIM // rows) + 1):
-        others += neighbours(stacked, d)
     first = jnp.pad(stack_taps(first_conv, CONV, SLOTS), ((0, 0), (0, SLOTS)))
     convs = (
         first,
@@ -367,9 +476,18 @@
         stack_taps(middle_conv[2], CONV, CONV),
         stack_taps(last_conv, SLOTS, CONV),
     )
-    results = convolutions(at, stacked, maps, others, convs, group)
+    weights, convs = lax.optimization_barrier((weights, convs))
+    done = ()
+    for c in range(len(cuts)):
+        done = attention(close + far[c], weights, done, near, cuts, length)
+    stacked, maps, _ = done
+
+    others = []
+    for d in range(1, -(-RIM // rows) + 1):
+        others += neighbours(stacked, d)
+    results = convolutions(stacked, maps, others, convs, group)
     results = [results[0]] + [swap(results[k], k) for k in range(1, group)]
-    return tuple(place_rows(at, results))
+    return tuple(place_rows(results))
 
 
 def solution(mesh):

time: 60.9 us -> 38.8 us (0.64)
  Pallas kernels: 28.2 us -> 12.4 us
  waiting for transfers between devices: 9.99 us -> 6.39 us
  other arithmetic: 1.85 us -> 0 us
    pallas_call x1, Pallas kernels: 17.8 us -> 3.12 us  [convolutions(): pl.pallas_call(functools.partial(conv_kernel, group, hops), name='convolu...]
    ppermute x9 -> x8, waiting for transfers between devices: 9.98 us -> 6.18 us  [swap(): return lax.ppermute(x, GROUP, [(i, i ^ k) for i in range(count)])]
    another operation x1 -> x0, local copies, waits for them, and re-layouts: 1.29 us -> none  [per_device(): jnp.stack([mine(left_features, k), mine(right_features, k)])]
    select_n x3 -> x0, other arithmetic: 0.99 us -> none  [per_device(): jnp.where(high, jnp.concatenate([strips[n + 1], strips[n]], axis=2), jnp....]
    another operation x4 -> x0, other arithmetic: 0.86 us -> none  [the longest x3 0.78 us: per_device(): jnp.stack([mine(left_features, k), mine(right_features, k)])]
    pallas_call x1, Pallas kernels: 1.44 us -> 0.62 us  [place_rows(): pl.pallas_call(functools.partial(place_kernel, group), name='place', out_...]
    ppermute x9 -> x8, starting transfers between devices: 12.5 us -> 12 us  [swap(): return lax.ppermute(x, GROUP, [(i, i ^ k) for i in range(count)])]
    unnamed x33 -> x26, local copies, waits for them, and re-layouts: 3.46 us -> 3.96 us
  transfers between devices with their start and end apart: 11 -> 10, of which waited for: 4 -> 4; matrix products, arithmetic and copies ran while one was open for 6% -> 4% of each run, Pallas kernels for 0% -> 12%
where the time goes in v2:
time: 38.8 us; the launch traced here: 38.5 us
  starting transfers between devices  13.1 us (34%)
  Pallas kernels  12.4 us (32%)
  waiting for transfers between devices  6.39 us (16%)
  local copies, waits for them, and re-layouts  5.67 us (15%)
  between operations  0.9 us (2%)
    ppermute x8, starting transfers between devices, swap(): return lax.ppermute(x, GROUP, [(i, i ^ k) for i in range(count)])  12 us
    pallas_call x2, Pallas kernels, attention(): pl.pallas_call(functools.partial(attention_kernel, group, near, cuts, chu...  6.96 us
    ppermute x8, waiting for transfers between devices, swap(): return lax.ppermute(x, GROUP, [(i, i ^ k) for i in range(count)])  6.18 us
    unnamed x26, local copies, waits for them, and re-layouts  3.96 us
    pallas_call x1, Pallas kernels, convolutions(): pl.pallas_call(functools.partial(conv_kernel, group, hops), name='convolu...  3.12 us
    pallas_call x3, Pallas kernels, pack(): pl.pallas_call(functools.partial(pack_kernel, partners, cuts, chunks), na...  1.75 us
    ppermute x2, starting transfers between devices, neighbours(): lax.ppermute(x, BANDS, [(device(i), device(j)) for i, j in pairs if 0 <=...  1.06 us
    reshape x6, local copies, waits for them, and re-layouts, stack_taps(): return w.transpose(0, 2, 1, 3).reshape(3 * outs, 3 * channels)  0.8 us
  transfers between devices with their start and end apart: 10, of which 4 were waited for; matrix products, arithmetic and copies ran while one was open for 4% of the time, Pallas kernels for 12%

profile of v2, /device:TPU:0, one launch (start us, length us, event | category | flops | bytes accessed | tf_op | source)
XLA Modules:
  0.0 38.5 jit_solution(17531160596346822920)
XLA Ops:
  0.6 0.0 copy-start
  0.6 1.0 %copy-done = bf16[32,64,128]{2,1,0:T(8,128)(2,1)S(1)} copy-done((bf16[32,64,128]{2,1,0:T(8,128)(2,1)S(1)}, bf16[32,64,128]{2,1,0:T(8,128)(2,1)}, u32[]{:S(2)}) %copy-start) | copy-done | bytes 524312
  1.7 1.0 %copy-done.2 = bf16[32,64,128]{2,1,0:T(8,128)(2,1)S(1)} copy-done((bf16[32,64,128]{2,1,0:T(8,128)(2,1)S(1)}, bf16[32,64,128]{2,1,0:T(8,128)(2,1)}, u32[]{:S(2)}) %copy-start.2) | copy-done | bytes 524312
  2.7 0.8 %copy-done.4 = f32[3,32,64]{2,1,0:T(8,128)S(1)} copy-done((f32[3,32,64]{2,1,0:T(8,128)S(1)}, f32[3,32,64]{2,1,0:T(8,128)}, u32[]{:S(2)}) %copy-start.4) | copy-done | bytes 24600
  3.5 0.8 %pack.3 = (bf16[1056,128]{1,0:T(8,128)(2,1)S(1)}, bf16[1056,128]{1,0:T(8,128)(2,1)S(1)}) custom-call(bf16[2048,128]{1,0:T(8,128)(2,1)S(1)} %bitcast.26, bf16[2048,128]{1,0:T(8,128)(2,1)S(1)} %bitcast.29, f32[3,32,64]{2,1,0:T(8,128)S(1)} %copy-done.4), custom_call_target="tpu_custom_call" | custom-call | tf_op jit(solution)/shard_map/pack/pallas_call | solution.py:164
  4.4 0.0 copy-start.7
  4.4 0.6 %pack.4 = (bf16[672,128]{1,0:T(8,128)(2,1)S(1)}, bf16[672,128]{1,0:T(8,128)(2,1)S(1)}) custom-call(bf16[2048,128]{1,0:T(8,128)(2,1)S(1)} %bitcast.27, bf16[2048,128]{1,0:T(8,128)(2,1)S(1)} %bitcast.30, f32[3,32,64]{2,1,0:T(8,128)S(1)} %copy-done.4), custom_call_target="tpu_custom_call" | custom-call | tf_op jit(solution)/shard_map/pack/pallas_call | solution.py:164
  5.0 0.5 %collective-permute-start = (bf16[1056,128]{1,0:T(8,128)(2,1)S(1)}, bf16[1056,128]{1,0:T(8,128)(2,1)S(1)}, u32[]{:S(2)}, u32[]{:S(2)}) collective-permute-start(bf16[1056,128]{1,0:T(8,128)(2,1)S(1)} %get-tuple-element.41), channel_id=1, source_target_pairs={{0,1},{1,0},{2,3},{3,2},{4,5},{5,4},{6,7},{7,6},{8,9},{9,8},{10,11... | collective-permute-start | bytes 811016 | tf_op jit(solution)/shard_map/ppermute | solution.py:402
  5.5 2.6 %collective-permute-start.3 = (bf16[672,128]{1,0:T(8,128)(2,1)S(1)}, bf16[672,128]{1,0:T(8,128)(2,1)S(1)}, u32[]{:S(2)}, u32[]{:S(2)}) collective-permute-start(bf16[672,128]{1,0:T(8,128)(2,1)S(1)} %get-tuple-element.55), channel_id=1, source_target_pairs={{0,2},{1,3},{2,0},{3,1},{4,6},{5,7},{6,4},{7,5},{8,10},{9,11},{10,... | collective-permute-start | bytes 516104 | tf_op jit(solution)/shard_map/ppermute | solution.py:402
  8.0 0.1 collective-permute-start.4
  8.2 0.1 copy.38
  8.3 0.2 reshape.39.refs_3_
  8.5 0.1 copy.37
  8.6 0.2 reshape.40.refs_4_
  8.8 0.0 copy-start.10
  8.8 0.0 copy-start.11
  8.8 0.0 copy-start.8
  8.8 0.0 copy-start.9
  8.8 0.0 copy-start.3
  8.8 0.1 copy.36
  9.0 0.2 reshape.41.refs_5_
  9.1 0.4 copy-done.6
  9.5 0.1 copy.22
  9.7 0.1 reshape.38
  9.8 0.1 copy.26
  9.9 0.1 reshape.43.refs_6_
  10.0 0.1 copy.23
  10.1 0.1 copy.24
  10.3 0.0 copy-start.12
  10.3 0.6 %copy-done.12 = f32[128]{0:T(128)S(1)} copy-done((f32[128]{0:T(128)S(1)}, f32[128]{0:T(128)}, u32[]{:S(2)}) %copy-start.12) | copy-done | bytes 536
  10.9 0.1 copy.32.refs_8_
  11.1 0.0 copy-done.5
  11.1 0.3 pack.5
  11.4 1.8 %collective-permute-start.1 = (bf16[384,128]{1,0:T(8,128)(2,1)S(1)}, bf16[384,128]{1,0:T(8,128)(2,1)S(1)}, u32[]{:S(2)}, u32[]{:S(2)}) collective-permute-start(bf16[384,128]{1,0:T(8,128)(2,1)S(1)} %get-tuple-element.42), channel_id=1, source_target_pairs={{0,2},{1,3},{2,0},{3,1},{4,6},{5,7},{6,4},{7,5},{8,10},{9,11},{10,... | collective-permute-start | bytes 294920 | tf_op jit(solution)/shard_map/ppermute | solution.py:402
  13.2 0.0 collective-permute-start.2
  13.3 3.2 %collective-permute-done.4.refs_3_ = bf16[672,128]{1,0:T(8,128)(2,1)S(1)} collective-permute-done((bf16[672,128]{1,0:T(8,128)(2,1)S(1)}, bf16[672,128]{1,0:T(8,128)(2,1)S(1)}, u32[]{:S(2)}, u32[]{:S(2)}) %collective-permute-start.4) | collective-permute-done | bytes 172064 | tf_op jit(solution)/shard_map/ppermute | solution.py:402
  16.4 4.3 %attention.2 = (bf16[8,8,256]{2,1,0:T(8,128)(2,1)S(1)}, f32[8,2,256]{2,1,0:T(2,128)S(1)}) custom-call(bf16[1056,128]{1,0:T(8,128)(2,1)S(1)} %get-tuple-element.40.refs_0_, bf16[1056,128]{1,0:T(8,128)(2,1)S(1)} %collective-permute-done.refs_0_.refs_1_, bf16[672,128]{1,0:T(8,128)(2,1)S(1)} %collective-permute-done.3.refs_2_, ...), custom_call_target="tpu_custom_call" | custom-call | flops 1342177280 | bytes 1310720 | tf_op jit(solution)/shard_map/attention/pallas_call | solution.py:238
  20.8 2.7 %attention.3 = (bf16[8,8,256]{2,1,0:T(8,128)(2,1)S(1)}, f32[8,2,256]{2,1,0:T(2,128)S(1)}) custom-call(bf16[1056,128]{1,0:T(8,128)(2,1)S(1)} %get-tuple-element.40.refs_0_, bf16[1056,128]{1,0:T(8,128)(2,1)S(1)} %collective-permute-done.refs_0_.refs_1_, bf16[384,128]{1,0:T(8,128)(2,1)S(1)} %collective-permute-done.1.refs_2_, ...), custom_call_target="tpu_custom_call" | custom-call | flops 805306368 | bytes 786432 | tf_op jit(solution)/shard_map/attention/pallas_call | solution.py:238
  23.4 0.4 %collective-permute-start.5 = (bf16[8,8,256]{2,1,0:T(8,128)(2,1)S(1)}, bf16[8,8,256]{2,1,0:T(8,128)(2,1)S(1)}, u32[]{:S(2)}, u32[]{:S(2)}) collective-permute-start(bf16[8,8,256]{2,1,0:T(8,128)(2,1)S(1)} %get-tuple-element.59.own), channel_id=1, source_target_pairs={{0,1},{1,0},{3,2},{2,3},{6,7},{7,6},{5,4},{4,5},{8,9},{9,8},{11,10... | collective-permute-start | bytes 98312 | tf_op jit(solution)/shard_map/ppermute | solution.py:416
  23.8 0.7 %collective-permute-start.6 = (bf16[8,8,256]{2,1,0:T(8,128)(2,1)S(1)}, bf16[8,8,256]{2,1,0:T(8,128)(2,1)S(1)}, u32[]{:S(2)}, u32[]{:S(2)}) collective-permute-start(bf16[8,8,256]{2,1,0:T(8,128)(2,1)S(1)} %get-tuple-element.59.own), channel_id=1, source_target_pairs={{1,3},{3,1},{2,6},{6,2},{7,5},{5,7},{4,8},{8,4},{9,11},{11,9},{10,... | collective-permute-start | bytes 98312 | tf_op jit(solution)/shard_map/ppermute | solution.py:416
  24.5 0.2 collective-permute-done.5.refs_0_
  24.7 3.1 %convolutions.1 = (f32[2,8,64]{2,1,0:T(8,128)S(1)}, f32[2,8,64]{2,1,0:T(8,128)S(1)}, f32[2,8,64]{2,1,0:T(8,128)S(1)}, f32[2,8,64]{2,1,0:T(8,128)S(1)}) custom-call(bf16[8,8,256]{2,1,0:T(8,128)(2,1)S(1)} %get-tuple-element.59.own, f32[8,2,256]{2,1,0:T(2,128)S(1)} %get-tuple-element.60.maps, bf16[8,8,256]{2,1,0:T(8,128)(2,1)S(1)} %collective-permute-done.5.refs_0_, ...), custom_call_target="tpu_custom_call" | custom-call | tf_op jit(solution)/shard_map/convolutions/pallas_call | solution.py:359
  27.8 4.0 %collective-permute-start.7 = (f32[2,8,64]{2,1,0:T(8,128)S(1)}, f32[2,8,64]{2,1,0:T(8,128)S(1)}, u32[]{:S(2)}, u32[]{:S(2)}) collective-permute-start(f32[2,8,64]{2,1,0:T(8,128)S(1)} %get-tuple-element.67), channel_id=1, source_target_pairs={{0,1},{1,0},{2,3},{3,2},{4,5},{5,4},{6,7},{7,6},{8,9},{9,8},{10,11... | collective-permute-start | bytes 12296 | tf_op jit(solution)/shard_map/ppermute | solution.py:402
  31.8 2.9 %collective-permute-start.8 = (f32[2,8,64]{2,1,0:T(8,128)S(1)}, f32[2,8,64]{2,1,0:T(8,128)S(1)}, u32[]{:S(2)}, u32[]{:S(2)}) collective-permute-start(f32[2,8,64]{2,1,0:T(8,128)S(1)} %get-tuple-element.68), channel_id=1, source_target_pairs={{0,2},{1,3},{2,0},{3,1},{4,6},{5,7},{6,4},{7,5},{8,10},{9,11},{10,... | collective-permute-start | bytes 12296 | tf_op jit(solution)/shard_map/ppermute | solution.py:402
  34.8 0.1 collective-permute-start.9
  34.8 1.6 %collective-permute-done.8.refs_2_ = f32[2,8,64]{2,1,0:T(8,128)S(1)} collective-permute-done((f32[2,8,64]{2,1,0:T(8,128)S(1)}, f32[2,8,64]{2,1,0:T(8,128)S(1)}, u32[]{:S(2)}, u32[]{:S(2)}) %collective-permute-start.8) | collective-permute-done | bytes 4128 | tf_op jit(solution)/shard_map/ppermute | solution.py:402
  36.4 1.4 %collective-permute-done.9.refs_3_ = f32[2,8,64]{2,1,0:T(8,128)S(1)} collective-permute-done((f32[2,8,64]{2,1,0:T(8,128)S(1)}, f32[2,8,64]{2,1,0:T(8,128)S(1)}, u32[]{:S(2)}, u32[]{:S(2)}) %collective-permute-start.9) | collective-permute-done | bytes 4128 | tf_op jit(solution)/shard_map/ppermute | solution.py:402
  37.9 0.6 %place.1 = (f32[32,64]{1,0:T(8,128)}, f32[32,64]{1,0:T(8,128)}) custom-call(f32[2,8,64]{2,1,0:T(8,128)S(1)} %get-tuple-element.66.refs_0_, f32[2,8,64]{2,1,0:T(8,128)S(1)} %collective-permute-done.7.refs_1_, f32[2,8,64]{2,1,0:T(8,128)S(1)} %collective-permute-done.8.refs_2_, f32[2,8,64]{2,1,0:T(8,128)S(1)} %collective-permute-done.9.refs_3_), custom_call_target="tpu_custom_call" | custom-call | tf_op jit(solution)/shard_map/place/pallas_call | solution.py:390
  (24 shorter events, 0.1 us)
Async XLA Ops:
  0.6 1.0 %copy-start = (bf16[32,64,128]{2,1,0:T(8,128)(2,1)S(1)}, bf16[32,64,128]{2,1,0:T(8,128)(2,1)}, u32[]{:S(2)}) copy-start(bf16[32,64,128]{2,1,0:T(8,128)(2,1)} %param.10) | copy-start | bytes 1572868
  1.7 1.0 %copy-start.2 = (bf16[32,64,128]{2,1,0:T(8,128)(2,1)S(1)}, bf16[32,64,128]{2,1,0:T(8,128)(2,1)}, u32[]{:S(2)}) copy-start(bf16[32,64,128]{2,1,0:T(8,128)(2,1)} %param.11) | copy-start | bytes 1572868
  2.7 0.8 %copy-start.4 = (f32[3,32,64]{2,1,0:T(8,128)S(1)}, f32[3,32,64]{2,1,0:T(8,128)}, u32[]{:S(2)}) copy-start(f32[3,32,64]{2,1,0:T(8,128)} %image.5) | copy-start | bytes 73732
  4.4 3.8 %copy-start.7 = (bf16[3,9,64,64]{3,2,1,0:T(8,128)(2,1)S(1)}, bf16[3,9,64,64]{3,2,1,0:T(8,128)(2,1)}, u32[]{:S(2)}) copy-start(bf16[3,9,64,64]{3,2,1,0:T(8,128)(2,1)} %param.18) | copy-start | bytes 663556
  5.0 6.1 %collective-permute-start = (bf16[1056,128]{1,0:T(8,128)(2,1)S(1)}, bf16[1056,128]{1,0:T(8,128)(2,1)S(1)}, u32[]{:S(2)}, u32[]{:S(2)}) collective-permute-start(bf16[1056,128]{1,0:T(8,128)(2,1)S(1)} %get-tuple-element.41), channel_id=1, source_target_pairs={{0,1},{1,0},{2,3},{3,2},{4,5},{5,4},{6,7},{7,6},{8,9},{9,8},{10,11... | collective-permute-start | bytes 811016 | tf_op jit(solution)/shard_map/ppermute | solution.py:402
  5.5 7.8 %collective-permute-start.3 = (bf16[672,128]{1,0:T(8,128)(2,1)S(1)}, bf16[672,128]{1,0:T(8,128)(2,1)S(1)}, u32[]{:S(2)}, u32[]{:S(2)}) collective-permute-start(bf16[672,128]{1,0:T(8,128)(2,1)S(1)} %get-tuple-element.55), channel_id=1, source_target_pairs={{0,2},{1,3},{2,0},{3,1},{4,6},{5,7},{6,4},{7,5},{8,10},{9,11},{10,... | collective-permute-start | bytes 516104 | tf_op jit(solution)/shard_map/ppermute | solution.py:402
  8.0 8.4 %collective-permute-start.4 = (bf16[672,128]{1,0:T(8,128)(2,1)S(1)}, bf16[672,128]{1,0:T(8,128)(2,1)S(1)}, u32[]{:S(2)}, u32[]{:S(2)}) collective-permute-start(bf16[672,128]{1,0:T(8,128)(2,1)S(1)} %get-tuple-element.56), channel_id=1, source_target_pairs={{0,3},{1,2},{2,1},{3,0},{4,7},{5,6},{6,5},{7,4},{8,11},{9,10},{10,... | collective-permute-start | bytes 516104 | tf_op jit(solution)/shard_map/ppermute | solution.py:402
  8.8 0.8 %copy-start.6 = (bf16[128,128]{1,0:T(8,128)(2,1)S(1)}, bf16[128,128]{1,0:T(8,128)(2,1)}, u32[]{:S(2)}) copy-start(bf16[128,128]{1,0:T(8,128)(2,1)} %refs_5_.1) | copy-start | bytes 98308
  8.8 0.9 %copy-start.10 = (bf16[9,64,5]{1,2,0:T(8,128)(2,1)S(1)}, bf16[9,64,5]{1,2,0:T(8,128)(2,1)}, u32[]{:S(2)}) copy-start(bf16[9,64,5]{1,2,0:T(8,128)(2,1)} %param.17) | copy-start | bytes 17284
  8.8 1.1 %copy-start.11 = (bf16[9,2,64]{2,1,0:T(2,128)(2,1)S(1)}, bf16[9,2,64]{2,1,0:T(2,128)(2,1)}, u32[]{:S(2)}) copy-start(bf16[9,2,64]{2,1,0:T(2,128)(2,1)} %param.19) | copy-start | bytes 6916
  8.8 1.2 %copy-start.8 = (bf16[128,128]{1,0:T(8,128)(2,1)S(1)}, bf16[128,128]{1,0:T(8,128)(2,1)}, u32[]{:S(2)}) copy-start(bf16[128,128]{1,0:T(8,128)(2,1)} %param.14) | copy-start | bytes 98308
  8.8 1.3 %copy-start.9 = (bf16[128,128]{1,0:T(8,128)(2,1)S(1)}, bf16[128,128]{1,0:T(8,128)(2,1)}, u32[]{:S(2)}) copy-start(bf16[128,128]{1,0:T(8,128)(2,1)} %param.15) | copy-start | bytes 98308
  8.8 2.2 %copy-start.3 = (bf16[32,64,128]{2,1,0:T(8,128)(2,1)S(1)}, bf16[32,64,128]{2,1,0:T(8,128)(2,1)}, u32[]{:S(2)}) copy-start(bf16[32,64,128]{2,1,0:T(8,128)(2,1)} %param.11) | copy-start | bytes 1572868
  9.0 2.1 %copy-start.1 = (bf16[32,64,128]{2,1,0:T(8,128)(2,1)S(1)}, bf16[32,64,128]{2,1,0:T(8,128)(2,1)}, u32[]{:S(2)}) copy-start(bf16[32,64,128]{2,1,0:T(8,128)(2,1)} %param.10) | copy-start | bytes 1572868
  10.3 0.7 %copy-start.12 = (f32[128]{0:T(128)S(1)}, f32[128]{0:T(128)}, u32[]{:S(2)}) copy-start(f32[128]{0:T(128)} %param.16) | copy-start | bytes 1540
  10.3 0.8 %copy-start.5 = (f32[3,32,64]{2,1,0:T(8,128)S(1)}, f32[3,32,64]{2,1,0:T(8,128)}, u32[]{:S(2)}) copy-start(f32[3,32,64]{2,1,0:T(8,128)} %image.5) | copy-start | bytes 73732
  11.4 9.3 %collective-permute-start.1 = (bf16[384,128]{1,0:T(8,128)(2,1)S(1)}, bf16[384,128]{1,0:T(8,128)(2,1)S(1)}, u32[]{:S(2)}, u32[]{:S(2)}) collective-permute-start(bf16[384,128]{1,0:T(8,128)(2,1)S(1)} %get-tuple-element.42), channel_id=1, source_target_pairs={{0,2},{1,3},{2,0},{3,1},{4,6},{5,7},{6,4},{7,5},{8,10},{9,11},{10,... | collective-permute-start | bytes 294920 | tf_op jit(solution)/shard_map/ppermute | solution.py:402
  13.2 7.5 %collective-permute-start.2 = (bf16[384,128]{1,0:T(8,128)(2,1)S(1)}, bf16[384,128]{1,0:T(8,128)(2,1)S(1)}, u32[]{:S(2)}, u32[]{:S(2)}) collective-permute-start(bf16[384,128]{1,0:T(8,128)(2,1)S(1)} %get-tuple-element.43), channel_id=1, source_target_pairs={{0,3},{1,2},{2,1},{3,0},{4,7},{5,6},{6,5},{7,4},{8,11},{9,10},{10,... | collective-permute-start | bytes 294920 | tf_op jit(solution)/shard_map/ppermute | solution.py:402
  23.4 1.3 %collective-permute-start.5 = (bf16[8,8,256]{2,1,0:T(8,128)(2,1)S(1)}, bf16[8,8,256]{2,1,0:T(8,128)(2,1)S(1)}, u32[]{:S(2)}, u32[]{:S(2)}) collective-permute-start(bf16[8,8,256]{2,1,0:T(8,128)(2,1)S(1)} %get-tuple-element.59.own), channel_id=1, source_target_pairs={{0,1},{1,0},{3,2},{2,3},{6,7},{7,6},{5,4},{4,5},{8,9},{9,8},{11,10... | collective-permute-start | bytes 98312 | tf_op jit(solution)/shard_map/ppermute | solution.py:416
  23.8 0.9 %collective-permute-start.6 = (bf16[8,8,256]{2,1,0:T(8,128)(2,1)S(1)}, bf16[8,8,256]{2,1,0:T(8,128)(2,1)S(1)}, u32[]{:S(2)}, u32[]{:S(2)}) collective-permute-start(bf16[8,8,256]{2,1,0:T(8,128)(2,1)S(1)} %get-tuple-element.59.own), channel_id=1, source_target_pairs={{1,3},{3,1},{2,6},{6,2},{7,5},{5,7},{4,8},{8,4},{9,11},{11,9},{10,... | collective-permute-start | bytes 98312 | tf_op jit(solution)/shard_map/ppermute | solution.py:416
  27.8 7.0 %collective-permute-start.7 = (f32[2,8,64]{2,1,0:T(8,128)S(1)}, f32[2,8,64]{2,1,0:T(8,128)S(1)}, u32[]{:S(2)}, u32[]{:S(2)}) collective-permute-start(f32[2,8,64]{2,1,0:T(8,128)S(1)} %get-tuple-element.67), channel_id=1, source_target_pairs={{0,1},{1,0},{2,3},{3,2},{4,5},{5,4},{6,7},{7,6},{8,9},{9,8},{10,11... | collective-permute-start | bytes 12296 | tf_op jit(solution)/shard_map/ppermute | solution.py:402
  31.8 4.6 %collective-permute-start.8 = (f32[2,8,64]{2,1,0:T(8,128)S(1)}, f32[2,8,64]{2,1,0:T(8,128)S(1)}, u32[]{:S(2)}, u32[]{:S(2)}) collective-permute-start(f32[2,8,64]{2,1,0:T(8,128)S(1)} %get-tuple-element.68), channel_id=1, source_target_pairs={{0,2},{1,3},{2,0},{3,1},{4,6},{5,7},{6,4},{7,5},{8,10},{9,11},{10,... | collective-permute-start | bytes 12296 | tf_op jit(solution)/shard_map/ppermute | solution.py:402
  34.8 3.1 %collective-permute-start.9 = (f32[2,8,64]{2,1,0:T(8,128)S(1)}, f32[2,8,64]{2,1,0:T(8,128)S(1)}, u32[]{:S(2)}, u32[]{:S(2)}) collective-permute-start(f32[2,8,64]{2,1,0:T(8,128)S(1)} %get-tuple-element.69), channel_id=1, source_target_pairs={{0,3},{1,2},{2,1},{3,0},{4,7},{5,6},{6,5},{7,4},{8,11},{9,10},{10,... | collective-permute-start | bytes 12296 | tf_op jit(solution)/shard_map/ppermute | solution.py:402

commit v3 on v2

--- a/solution.py
+++ b/solution.py
@@ -24,22 +24,26 @@
     return lax.dot_general(a, b, (dims, ((), ())), preferred_element_type=F32)
 
 
+def score_blocks(queries, keys):
+    channel = lax.broadcasted_iota(jnp.int32, (1, C), 1)
+    found = []
+    for j in range(keys.shape[0] // BLOCK):
+        part = keys[BLOCK * j : BLOCK * (j + 1)]
+        by_head = [
+            jnp.where(channel // HEAD == h, part, jnp.zeros_like(part)) for h in range(HEADS)
+        ]
+        s = dot(jnp.concatenate(by_head, axis=0), queries[:, BLOCK * j :], ((1,), (0,)))
+        found.append([s[:, i : i + BLOCK] for i in range(0, s.shape[1], BLOCK)])
+    return found
+
+
 def attention_row(left, right, qw, kw, vw, ow, occ):
     length = left.shape[0]
     blocks = length // BLOCK
     queries = (dot(qw, left, ((1,), (1,))) * (HEAD**-0.5)).astype(BF16)
     keys = dot(right, kw, ((1,), (0,))).astype(BF16)
     values = dot(vw, right, ((1,), (1,))).astype(BF16)
-
-    channel = lax.broadcasted_iota(jnp.int32, (1, C), 1)
-    scores = []
-    for j in range(blocks):
-        part = keys[BLOCK * j : BLOCK * (j + 1)]
-        by_head = jnp.concatenate(
-            [jnp.where(channel // HEAD == h, part, jnp.zeros_like(part)) for h in range(HEADS)],
-            axis=0,
-        )
-        scores.append(dot(by_head, queries[:, BLOCK * j :], ((1,), (0,))))
+    scores = score_blocks(queries, keys)
 
     key_at = lax.broadcasted_iota(jnp.int32, (BLOCK, BLOCK), 0)
     query_at = lax.broadcasted_iota(jnp.int32, (BLOCK, BLOCK), 1)
@@ -55,27 +59,28 @@
 
     heads = [[] for _ in range(blocks)]
     means = [jnp.zeros((1, BLOCK), F32) for _ in range(blocks)]
-    for h in range(HEADS):
-        stacked = jnp.concatenate([values[HEAD * h : HEAD * (h + 1)], counts], axis=0)
+    for h in range(0, HEADS, 2):
+        stacked = jnp.concatenate([values[HEAD * h : HEAD * (h + 2)], counts], axis=0)
         for i in range(blocks):
-            parts = []
-            for j in range(i + 1):
-                piece = scores[j][
-                    BLOCK * h : BLOCK * (h + 1), BLOCK * (i - j) : BLOCK * (i - j + 1)
-                ]
-                if j == i:
-                    piece = jnp.where(allowed, piece, -jnp.inf)
-                parts.append(piece)
-            largest = functools.reduce(
-                jnp.maximum, [jnp.max(p, axis=0, keepdims=True) for p in parts]
+            expon = []
+            for g in (h, h + 1):
+                parts = [scores[j][i - j][BLOCK * g : BLOCK * (g + 1)] for j in range(i + 1)]
+                parts[i] = jnp.where(allowed, parts[i], -jnp.inf)
+                largest = functools.reduce(
+                    jnp.maximum, [jnp.max(p, axis=0, keepdims=True) for p in parts]
+                )
+                expon.append(
+                    jnp.concatenate([jnp.exp(p - largest).astype(BF16) for p in parts], axis=0)
+                )
+            sums = dot(
+                stacked[:, : BLOCK * (i + 1)], jnp.concatenate(expon, axis=1), ((1,), (0,))
             )
-            expon = jnp.concatenate(
-                [jnp.exp(p - largest).astype(BF16) for p in parts], axis=0
-            )
-            sums = dot(stacked[:, : BLOCK * (i + 1)], expon, ((1,), (0,)))
-            inverse = 1.0 / sums[HEAD : HEAD + 1]
-            heads[i].append((sums[:HEAD] * inverse).astype(BF16))
-            means[i] = means[i] + (sums[HEAD + 1 : HEAD + 2] + sums[HEAD + 2 : HEAD + 3]) * inverse
+            for g in range(2):
+                part = sums[:, BLOCK * g : BLOCK * (g + 1)]
+                inverse = 1.0 / part[2 * HEAD : 2 * HEAD + 1]
+                heads[i].append((part[HEAD * g : HEAD * (g + 1)] * inverse).astype(BF16))
+                total = part[2 * HEAD + 1 : 2 * HEAD + 2] + part[2 * HEAD + 2 : 2 * HEAD + 3]
+                means[i] = means[i] + total * inverse
 
     head_out = jnp.concatenate([jnp.concatenate(b, axis=0) for b in heads], axis=1)
     mean = jnp.concatenate(means, axis=1)
@@ -92,11 +97,6 @@
     return -(-3 * rows // 16) * 16
 
 
-def line_plan(cuts, tile, rows):
-    sizes = [2 * c * tile + (strip_lines(rows) if n == 0 else 0) for n, c in enumerate(cuts)]
-    return [(sum(sizes[:n]), s) for n, s in enumerate(sizes)]
-
-
 def order(k, near):
     chip, core = k // near, k % near
     return chip * near + jnp.where(chip % 2 == 0, core, near - 1 - core)
@@ -113,93 +113,150 @@
     return lambda k: place_of(me ^ k, band, group, near)
 
 
-def pack_kernel(partners, cuts, chunks, left, right, image, *refs):
-    outs, image_s, sems, image_sem = refs[-len(partners) - 3 : -3], *refs[-3:]
+def chunk_start(place, cuts, chunk):
+    start = sum(cuts[:chunk])
+    return jnp.where(place % 2 == 0, start, sum(cuts) - start - cuts[chunk])
+
+
+def pack_kernel(chunk, cuts, left, right, image, *refs):
+    group = lax.axis_size(GROUP)
+    outs, image_s, sems, image_sem = refs[-group - 3 : -3], *refs[-3:]
     tile = image.shape[2]
-    rows = sum(cuts)
-    plan = line_plan(cuts, tile, rows)
+    rows, lines = sum(cuts), cuts[chunk] * tile
     share = shared_place()
-    lines = strip_lines(rows)
     copies = []
-    if 0 in chunks:
+
+    def send(source, target):
+        copy = pltpu.make_async_copy(source, target, sems.at[len(copies)])
+        copy.start()
+        copies.append(copy)
+
+    if chunk == 0:
         colours = pltpu.make_async_copy(image, image_s, image_sem)
         colours.start()
-    n = 0
-    for c in chunks:
-        for k, out in zip(partners, outs):
-            base = plan[c][0] - plan[chunks[0]][0]
-            start = pl.multiple_of((share(k) * rows + sum(cuts[:c])) * tile, tile)
-            for s, side in enumerate((left, right)):
-                copy = pltpu.make_async_copy(
-                    side.at[pl.ds(start, cuts[c] * tile), :],
-                    out.at[pl.ds(base + s * cuts[c] * tile, cuts[c] * tile), :],
-                    sems.at[n],
-                )
-                copy.start()
-                copies.append(copy)
-                n += 1
-    if 0 in chunks:
+    for k in range(group):
+        first = share(k) * rows + chunk_start(share(k), cuts, chunk)
+        first = pl.multiple_of(first * tile, tile)
+        for s, side in enumerate((left, right)):
+            send(side.at[pl.ds(first, lines), :], outs[k].at[pl.ds(s * lines, lines), :])
+    if chunk == 0:
+        count = strip_lines(rows)
         colours.wait()
-        for k, out in zip(partners, outs):
-            strip = [
-                image_s[ch, pl.ds(pl.multiple_of(share(k) * rows, rows), rows), :]
-                for ch in range(3)
-            ]
-            if lines > 3 * rows:
-                strip.append(jnp.zeros((lines - 3 * rows, tile), F32))
+        for k in range(group):
+            start = pl.multiple_of(share(k) * rows, rows)
+            strip = [image_s[ch, pl.ds(start, rows), :] for ch in range(3)]
+            if count > 3 * rows:
+                strip.append(jnp.zeros((count - 3 * rows, tile), F32))
             strip = jnp.concatenate(strip, axis=0)
-            strip = jnp.concatenate([strip, jnp.zeros((lines, C - tile), F32)], axis=1)
-            first = 2 * cuts[0] * tile
-            out[first : first + lines, :] = strip.astype(BF16)
+            strip = jnp.concatenate([strip, jnp.zeros((count, C - tile), F32)], axis=1)
+            outs[k][2 * lines : 2 * lines + count, :] = strip.astype(BF16)
     for copy in copies:
         copy.wait()
 
 
-def pack(left, right, image, partners, cuts, chunks, after=()):
+def pack(left, right, image, chunk, cuts, after=()):
     height, tile, _ = left.shape
-    plan = line_plan(cuts, tile, sum(cuts))
-    size = sum(plan[c][1] for c in chunks)
+    group = lax.axis_size(GROUP)
+    count = strip_lines(sum(cuts))
+    size = 2 * cuts[chunk] * tile + (count if chunk == 0 else 0)
     vmem = pl.BlockSpec(memory_space=pltpu.VMEM)
     hbm = pl.BlockSpec(memory_space=pltpu.HBM)
     return pl.pallas_call(
-        functools.partial(pack_kernel, partners, cuts, chunks),
+        functools.partial(pack_kernel, chunk, cuts),
         name="pack",
-        out_shape=[jax.ShapeDtypeStruct((size, C), BF16)] * len(partners),
+        out_shape=[jax.ShapeDtypeStruct((size, C), BF16)] * group,
         in_specs=[hbm] * 3 + [vmem] * len(after),
-        out_specs=[vmem] * len(partners),
+        out_specs=[vmem] * group,
         scratch_shapes=[
             pltpu.VMEM(image.shape, F32),
-            pltpu.SemaphoreType.DMA((2 * len(partners) * len(chunks),)),
+            pltpu.SemaphoreType.DMA((2 * group,)),
             pltpu.SemaphoreType.DMA,
         ],
+        compiler_params=pltpu.CompilerParams(vmem_limit_bytes=(16 if after else 60) << 20),
+    )(left.reshape(height * tile, C), right.reshape(height * tile, C), image, *after)
+
+
+def weight_kernel(qk, value, out, occ, first, middle, last, *outs):
+    q_t, v_t, o_t, occ_t, w1, w2, w3, w4, w5 = outs
+
+    def flip(x):
+        return jnp.transpose(x.astype(F32)).astype(BF16)
+
+    q_t[...], v_t[...], o_t[...] = flip(qk[...]), flip(value[...]), flip(out[...])
+    occ_t[...] = jnp.transpose(jnp.broadcast_to(occ[...], (C, C)))[:, :1]
+    for a in range(3):
+        block = []
+        for b in range(3):
+            block.append(first[3 * a + b].astype(F32))
+            block.append(jnp.zeros((SLOTS - first.shape[1], CONV), F32))
+        block.append(jnp.zeros((C - 3 * SLOTS, CONV), F32))
+        block = jnp.concatenate(block, axis=0)
+        block = jnp.concatenate([block, jnp.zeros((C, C - CONV), F32)], axis=1)
+        w1[CONV * a : CONV * (a + 1), :] = jnp.transpose(block)[:CONV, : 4 * SLOTS].astype(BF16)
+        for n, w in enumerate((w2, w3, w4)):
+            taps = [middle[9 * n + 3 * a + b] for b in range(3)]
+            w[CONV * a : CONV * (a + 1), :] = jnp.concatenate(taps, axis=1)
+        taps = jnp.concatenate([last[3 * a + b].astype(F32) for b in range(3)], axis=1)
+        taps = jnp.concatenate([taps, jnp.zeros((SLOTS - 2, 3 * CONV), F32)], axis=0)
+        rest = taps if a == 0 else jnp.concatenate([rest, taps], axis=0)
+    w5[...] = rest.astype(BF16)
+
+
+def prepare_weights(qk, value, out, occ, first, middle, last):
+    vmem = pl.BlockSpec(memory_space=pltpu.VMEM)
+    square = jax.ShapeDtypeStruct((C, C), BF16)
+    deep = jax.ShapeDtypeStruct((3 * CONV, 3 * CONV), BF16)
+    results = pl.pallas_call(
+        weight_kernel,
+        name="weights",
+        out_shape=[
+            square,
+            square,
+            square,
+            jax.ShapeDtypeStruct((C, 1), F32),
+            jax.ShapeDtypeStruct((3 * CONV, 4 * SLOTS), BF16),
+            deep,
+            deep,
+            deep,
+            jax.ShapeDtypeStruct((3 * SLOTS, 3 * CONV), BF16),
+        ],
+        in_specs=[vmem] * 7,
+        out_specs=[vmem] * 9,
         compiler_params=pltpu.CompilerParams(vmem_limit_bytes=16 << 20),
-    )(left.reshape(height * tile, C), right.reshape(height * tile, C), image, *after)
-
-
-def attention_kernel(group, near, cuts, chunk, *refs):
+    )(
+        qk,
+        value,
+        out,
+        occ[None],
+        first.transpose(0, 2, 1),
+        middle.reshape(27, CONV, CONV),
+        last,
+    )
+    q_t, v_t, o_t, occ_t, *convs = results
+    return (q_t, qk, v_t, o_t, occ_t), tuple(convs)
+
+
+def attention_kernel(cuts, chunk, *refs):
+    group = lax.axis_size(GROUP)
     pieces, (qw, kw, vw, ow, occ) = refs[:group], refs[group : group + 5]
     earlier, (stacked_ref, maps_ref, left_s, right_s) = refs[group + 5 : -4], refs[-4:]
     count, length, _ = left_s.shape
     tile = length // group
-    rows, offset = sum(cuts), sum(cuts[:chunk])
-    plan = line_plan(cuts, tile, rows)
-    me = lax.axis_index(GROUP)
-    base = [plan[chunk][0] if k < near else 0 for k in range(group)]
+    rows = sum(cuts)
+    me, place = lax.axis_index(GROUP), shared_place()(0)
     for n in range(count):
         for k in range(group):
             start = pl.multiple_of((me ^ k) * tile, tile)
-            line = base[k] + n * tile
-            left_s[n, pl.ds(start, tile), :] = pieces[k][line : line + tile]
-            line += count * tile
+            left_s[n, pl.ds(start, tile), :] = pieces[k][n * tile : (n + 1) * tile]
+            line = (count + n) * tile
             right_s[n, pl.ds(start, tile), :] = pieces[k][line : line + tile]
+    slot = lax.broadcasted_iota(jnp.int32, (SLOTS, 1), 0)
     if chunk:
         stacked_ref[...] = earlier[0][...]
         maps_ref[...] = earlier[1][...]
     else:
-        first = [b + 2 * count * tile for b in base]
-        strips = [
-            pieces[k][f : f + strip_lines(rows), :tile].astype(F32) for k, f in enumerate(first)
-        ]
+        line = 2 * count * tile
+        strips = [p[line : line + strip_lines(rows), :tile].astype(F32) for p in pieces]
         width = 1
         while width < group:
             high = (me & width) != 0
@@ -218,39 +275,37 @@
             stacked_ref[r] = jnp.concatenate(
                 [zero, zero] + colours + [zero] * (SLOTS - 5), axis=0
             ).astype(BF16)
-    slot = lax.broadcasted_iota(jnp.int32, (SLOTS, 1), 0)
+        maps_ref[...] = jnp.zeros_like(maps_ref)
+    first = chunk_start(place, cuts, chunk)
     for n in range(count):
-        r = offset + n
         disparity, occlusion = attention_row(
             left_s[n], right_s[n], qw[...], kw[...], vw[...], ow[...], occ[...]
         )
+        r = first + n
         maps_ref[r] = jnp.concatenate([disparity, occlusion], axis=0)
         full = jnp.where(slot == 0, disparity, stacked_ref[r].astype(F32))
         stacked_ref[r] = jnp.where(slot == 1, occlusion, full).astype(BF16)
 
 
-def attention(pieces, weights, earlier, near, cuts, length):
-    group = len(pieces)
-    chunk = 0 if not earlier else earlier[2]
+def attention(pieces, weights, earlier, cuts, chunk, length):
     rows, count = sum(cuts), cuts[chunk]
     vmem = pl.BlockSpec(memory_space=pltpu.VMEM)
     pairs = count * HEADS * length * length
-    results = pl.pallas_call(
-        functools.partial(attention_kernel, group, near, cuts, chunk),
+    return pl.pallas_call(
+        functools.partial(attention_kernel, cuts, chunk),
         name="attention",
         out_shape=(
             jax.ShapeDtypeStruct((rows, SLOTS, length), BF16),
             jax.ShapeDtypeStruct((rows, 2, length), F32),
         ),
-        in_specs=[vmem] * (group + len(weights) + len(earlier[:2])),
+        in_specs=[vmem] * (len(pieces) + len(weights) + len(earlier)),
         out_specs=(vmem, vmem),
         scratch_shapes=[pltpu.VMEM((count, length, C), BF16)] * 2,
         compiler_params=pltpu.CompilerParams(vmem_limit_bytes=24 << 20),
         cost_estimate=pl.CostEstimate(
             flops=pairs * 4 * C, transcendentals=pairs, bytes_accessed=8 * count * length * C
         ),
-    )(*pieces, *weights, *earlier[:2])
-    return (*results, chunk + 1)
+    )(*pieces, *weights, *earlier)
 
 
 def spread_taps(x):
@@ -305,10 +360,12 @@
         for q in range(rows):
             up = RIM - d * rows + q
             if up >= 0:
-                put(up, jnp.where(flag, a[q], b[q]))
+                inside = base - d * rows >= 0
+                put(up, jnp.where(inside, jnp.where(flag, a[q], b[q]).astype(F32), 0.0))
             down = RIM + d * rows + q
             if down < rows + 2 * RIM:
-                put(down, jnp.where(flag, b[q], a[q]))
+                inside = base + d * rows < last
+                put(down, jnp.where(inside, jnp.where(flag, b[q], a[q]).astype(F32), 0.0))
 
     def store(target, lead, residual=None):
         def finish(r, total):
@@ -402,7 +459,7 @@
     return lax.ppermute(x, GROUP, [(i, i ^ k) for i in range(count)])
 
 
-def neighbours(x, d):
+def neighbours(x, d, odd):
     count, group, near = lax.axis_size(BANDS), lax.axis_size(GROUP), lax.axis_size("sub")
 
     def device(place):
@@ -410,23 +467,21 @@
         chip, core = divmod(q if band % 2 == 0 else group - 1 - q, near)
         return band * group + chip * near + (core if chip % 2 == 0 else near - 1 - core)
 
-    even = [(i, i ^ d) for i in range(count)]
-    odd = [(i, ((i + d) ^ d) - d) for i in range(count)]
-    return [
-        lax.ppermute(x, BANDS, [(device(i), device(j)) for i, j in pairs if 0 <= j < count])
-        for pairs in (even, odd)
-    ]
+    pairs = [(i, ((i + d) ^ d) - d if odd else i ^ d) for i in range(count)]
+    parts = lax.axis_size("grp")
+    targets = []
+    for part in range(parts):
+        for i, j in pairs:
+            at = part
+            if not 0 <= j < count:
+                at, j = (part ^ 1 if part ^ 1 < parts else part), i
+            targets.append((part * count + device(i), at * count + device(j)))
+    return lax.ppermute(x, ("grp",) + BANDS, targets)
 
 
 def chunks_of(rows):
     first = -(-5 * rows // 8)
     return (first, rows - first)
-
-
-def stack_taps(weight, outs, channels):
-    o, k = weight.shape[1:]
-    w = jnp.pad(weight.reshape(3, 3, o, k), ((0, 0), (0, 0), (0, outs - o), (0, channels - k)))
-    return w.transpose(0, 2, 1, 3).reshape(3 * outs, 3 * channels)
 
 
 def per_device(
@@ -445,46 +500,40 @@
     group = lax.axis_size(GROUP)
     rows = height // group
     length = tile * group
-    near = lax.axis_size("sub")
     cuts = chunks_of(rows)
     features = (left_features, right_features, left_image)
-    chunks = tuple(range(len(cuts)))
-    distant = tuple(range(near, group))
-    close = pack(*features, tuple(range(near)), cuts, chunks)
-    packed = pack(*features, distant, cuts, (0,))
-    tables = (first_conv, middle_conv, last_conv, query_key, value_weight, out_weight)
-    close, packed, tables = lax.optimization_barrier((close, packed, tables))
-    first_conv, middle_conv, last_conv, query_key, value_weight, out_weight = tables
-    far = [[swap(x, k) for k, x in zip(distant, packed)][::1]]
-    close = [close[0]] + [swap(close[k], k) for k in range(1, near)]
-    for c in chunks[1:]:
-        packed = pack(*features, distant, cuts, (c,), (close[-1],))
-        far.append([swap(x, k) for k, x in zip(distant, packed)])
-
-    weights = (
-        query_key.T,
+    packed = pack(*features, 0, cuts)
+    tables = (
         query_key,
-        value_weight.T,
-        out_weight.T,
-        occlusion_weight[:, None],
+        value_weight,
+        out_weight,
+        occlusion_weight,
+        first_conv,
+        middle_conv,
+        last_conv,
     )
-    first = jnp.pad(stack_taps(first_conv, CONV, SLOTS), ((0, 0), (0, SLOTS)))
-    convs = (
-        first,
-        stack_taps(middle_conv[0], CONV, CONV),
-        stack_taps(middle_conv[1], CONV, CONV),
-        stack_taps(middle_conv[2], CONV, CONV),
-        stack_taps(last_conv, SLOTS, CONV),
-    )
+    packed, tables = lax.optimization_barrier((packed, tables))
+    pieces = []
+    for c in range(len(cuts)):
+        if c:
+            packed = pack(*features, c, cuts, (pieces[-1][1],))
+        pieces.append([packed[0]] + [swap(packed[k], k) for k in range(1, group)])
+
+    weights, convs = prepare_weights(*tables)
     weights, convs = lax.optimization_barrier((weights, convs))
     done = ()
+    others = []
+    hops = -(-RIM // rows)
     for c in range(len(cuts)):
-        done = attention(close + far[c], weights, done, near, cuts, length)
-    stacked, maps, _ = done
-
-    others = []
-    for d in range(1, -(-RIM // rows) + 1):
-        others += neighbours(stacked, d)
+        done = attention(pieces[c], weights, done, cuts, c, length)
+        if hops == 1 and len(others) == 0 and sum(cuts[: c + 1]) >= RIM:
+            others = [neighbours(done[0], 1, True)]
+    stacked, maps = done
+    if hops == 1:
+        others = [neighbours(stacked, 1, False)] + others
+    else:
+        for d in range(1, hops + 1):
+            others += [neighbours(stacked, d, odd) for odd in (False, True)]
     results = convolutions(stacked, maps, others, convs, group)
     results = [results[0]] + [swap(results[k], k) for k in range(1, group)]
     return tuple(place_rows(results))

time: 38.8 us -> 34 us (0.88)
  local copies, waits for them, and re-layouts: 5.67 us -> 0.59 us
  starting transfers between devices: 13.1 us -> 9.52 us
  waiting for transfers between devices: 6.39 us -> 8.95 us
  Pallas kernels: 12.4 us -> 13.9 us
    ppermute x8 -> x9, starting transfers between devices: 12 us -> 7.46 us  [swap(): return lax.ppermute(x, GROUP, [(i, i ^ k) for i in range(count)])]
    unnamed x26 -> x22, local copies, waits for them, and re-layouts: 3.96 us -> 0.59 us
    ppermute x8 -> x9, waiting for transfers between devices: 6.18 us -> 8.09 us  [swap(): return lax.ppermute(x, GROUP, [(i, i ^ k) for i in range(count)])]
    pallas_call x5, Pallas kernels: 8.71 us -> 10.2 us  [the longest x2 7.09 us: attention(): pl.pallas_call(functools.partial(attention_kernel, cuts, chunk), name='at...]
    ppermute x2, starting transfers between devices: 1.06 us -> 2.07 us  [neighbours(): return lax.ppermute(x, ('grp',) + BANDS, targets)]
    reshape x8 -> x0, local copies, waits for them, and re-layouts: 0.81 us -> none  [the longest x6 0.8 us: stack_taps(): return w.transpose(0, 2, 1, 3).reshape(3 * outs, 3 * channels)]
    ppermute x2, waiting for transfers between devices: 0.21 us -> 0.86 us  [neighbours(): return lax.ppermute(x, ('grp',) + BANDS, targets)]
    optimization_barrier x4 -> x0, local copies, waits for them, and re-layouts: 0.44 us -> none  [the longest x3 0.33 us: per_device(): close, packed, tables = lax.optimization_barrier((close, packed, tables))]
  transfers between devices with their start and end apart: 10 -> 11, of which waited for: 4 -> 5; matrix products, arithmetic and copies ran while one was open for 4% -> 0% of each run, Pallas kernels for 12% -> 23%
where the time goes in v3:
time: 34 us; the launch traced here: 33.8 us
  Pallas kernels  13.9 us (41%)
  starting transfers between devices  9.52 us (28%)
  waiting for transfers between devices  8.95 us (26%)
  between operations  0.82 us (2%)
  local copies, waits for them, and re-layouts  0.59 us (2%)
    ppermute x9, waiting for transfers between devices, swap(): return lax.ppermute(x, GROUP, [(i, i ^ k) for i in range(count)])  8.09 us
    ppermute x9, starting transfers between devices, swap(): return lax.ppermute(x, GROUP, [(i, i ^ k) for i in range(count)])  7.46 us
    pallas_call x2, Pallas kernels, attention(): pl.pallas_call(functools.partial(attention_kernel, cuts, chunk), name='at...  7.09 us
    pallas_call x1, Pallas kernels, convolutions(): pl.pallas_call(functools.partial(conv_kernel, group, hops), name='convolu...  3.11 us
    pallas_call x2, Pallas kernels, pack(): pl.pallas_call(functools.partial(pack_kernel, chunk, cuts), name='pack',...  2.91 us
    ppermute x2, starting transfers between devices, neighbours(): return lax.ppermute(x, ('grp',) + BANDS, targets)  2.07 us
    ppermute x2, waiting for transfers between devices, neighbours(): return lax.ppermute(x, ('grp',) + BANDS, targets)  0.86 us
  transfers between devices with their start and end apart: 11, of which 5 were waited for; matrix products, arithmetic and copies ran while one was open for 0% of the time, Pallas kernels for 23%

profile of v3, /device:TPU:0, one launch (start us, length us, event | category | flops | bytes accessed | tf_op | source)
XLA Modules:
  0.0 33.8 jit_solution(16432752132306440805)
XLA Ops:
  0.6 0.0 copy-start.2
  0.6 0.0 copy-start.4
  0.7 0.0 copy-start.5
  0.7 0.0 copy-start.6
  0.7 0.0 copy-start.7
  0.7 0.0 copy-start.8
  0.7 0.0 copy-start.9
  0.7 0.0 copy-start.1
  0.7 2.3 %pack.2 = (bf16[672,128]{1,0:T(8,128)(2,1)}, bf16[672,128]{1,0:T(8,128)(2,1)}, bf16[672,128]{1,0:T(8,128)(2,1)}, bf16[672,128]{1,0:T(8,128)(2,1)}) custom-call(bf16[2048,128]{1,0:T(8,128)(2,1)} %bitcast.5, bf16[2048,128]{1,0:T(8,128)(2,1)} %bitcast.7, f32[3,32,64]{2,1,0:T(8,128)} %image.3), custom_call_target="tpu_custom_call" | custom-call | tf_op jit(solution)/shard_map/pack/pallas_call | solution.py:164
  3.0 0.0 copy-start
  3.0 0.5 %collective-permute-start = (bf16[672,128]{1,0:T(8,128)(2,1)}, bf16[672,128]{1,0:T(8,128)(2,1)S(1)}, u32[]{:S(2)}, u32[]{:S(2)}) collective-permute-start(bf16[672,128]{1,0:T(8,128)(2,1)} %get-tuple-element.52), channel_id=1, source_target_pairs={{0,1},{1,0},{2,3},{3,2},{4,5},{5,4},{6,7},{7,6},{8,9},{9,8},{10,11... | collective-permute-start | bytes 516104 | tf_op jit(solution)/shard_map/ppermute | solution.py:459
  3.5 2.6 %collective-permute-start.4 = (bf16[672,128]{1,0:T(8,128)(2,1)}, bf16[672,128]{1,0:T(8,128)(2,1)S(1)}, u32[]{:S(2)}, u32[]{:S(2)}) collective-permute-start(bf16[672,128]{1,0:T(8,128)(2,1)} %get-tuple-element.79), channel_id=1, source_target_pairs={{0,2},{1,3},{2,0},{3,1},{4,6},{5,7},{6,4},{7,5},{8,10},{9,11},{10,... | collective-permute-start | bytes 516104 | tf_op jit(solution)/shard_map/ppermute | solution.py:459
  6.1 0.1 collective-permute-start.5
  6.2 0.0 copy-done.2
  6.2 0.0 copy-done.4
  6.2 0.0 copy-done.5
  6.2 0.0 copy-done.6
  6.2 0.0 copy-done.7
  6.2 0.0 copy-done.8
  6.2 0.0 copy-done.9
  6.2 0.0 copy-start.3
  6.2 0.2 weights.1
  6.4 0.0 copy-start.10
  6.4 0.0 collective-permute-done.refs_0_.refs_1_
  6.5 0.5 %copy-done.3 = f32[3,32,64]{2,1,0:T(8,128)S(1)} copy-done((f32[3,32,64]{2,1,0:T(8,128)S(1)}, f32[3,32,64]{2,1,0:T(8,128)}, u32[]{:S(2)}) %copy-start.3) | copy-done | bytes 24600
  7.0 0.6 %pack.3 = (bf16[384,128]{1,0:T(8,128)(2,1)S(1)}, bf16[384,128]{1,0:T(8,128)(2,1)S(1)}, bf16[384,128]{1,0:T(8,128)(2,1)S(1)}, bf16[384,128]{1,0:T(8,128)(2,1)S(1)}) custom-call(bf16[2048,128]{1,0:T(8,128)(2,1)S(1)} %bitcast.6, bf16[2048,128]{1,0:T(8,128)(2,1)S(1)} %bitcast.8, f32[3,32,64]{2,1,0:T(8,128)S(1)} %copy-done.3, ...), custom_call_target="tpu_custom_call" | custom-call | tf_op jit(solution)/shard_map/pack/pallas_call | solution.py:164
  7.6 0.2 collective-permute-start.1
  7.8 1.9 %collective-permute-start.2 = (bf16[384,128]{1,0:T(8,128)(2,1)S(1)}, bf16[384,128]{1,0:T(8,128)(2,1)S(1)}, u32[]{:S(2)}, u32[]{:S(2)}) collective-permute-start(bf16[384,128]{1,0:T(8,128)(2,1)S(1)} %get-tuple-element.55), channel_id=1, source_target_pairs={{0,2},{1,3},{2,0},{3,1},{4,6},{5,7},{6,4},{7,5},{8,10},{9,11},{10,... | collective-permute-start | bytes 294920 | tf_op jit(solution)/shard_map/ppermute | solution.py:459
  9.8 0.0 collective-permute-start.3
  9.8 1.7 %collective-permute-done.4.refs_2_ = bf16[672,128]{1,0:T(8,128)(2,1)S(1)} collective-permute-done((bf16[672,128]{1,0:T(8,128)(2,1)}, bf16[672,128]{1,0:T(8,128)(2,1)S(1)}, u32[]{:S(2)}, u32[]{:S(2)}) %collective-permute-start.4) | collective-permute-done | bytes 172064 | tf_op jit(solution)/shard_map/ppermute | solution.py:459
  11.5 3.3 %collective-permute-done.5.refs_3_ = bf16[672,128]{1,0:T(8,128)(2,1)S(1)} collective-permute-done((bf16[672,128]{1,0:T(8,128)(2,1)}, bf16[672,128]{1,0:T(8,128)(2,1)S(1)}, u32[]{:S(2)}, u32[]{:S(2)}) %collective-permute-start.5) | collective-permute-done | bytes 172064 | tf_op jit(solution)/shard_map/ppermute | solution.py:459
  14.8 4.4 %attention.2 = (bf16[8,8,256]{2,1,0:T(8,128)(2,1)S(1)}, f32[8,2,256]{2,1,0:T(2,128)S(1)}) custom-call(bf16[672,128]{1,0:T(8,128)(2,1)S(1)} %copy-done.10, bf16[672,128]{1,0:T(8,128)(2,1)S(1)} %collective-permute-done.refs_0_.refs_1_, bf16[672,128]{1,0:T(8,128)(2,1)S(1)} %collective-permute-done.4.refs_2_, ...), custom_call_target="tpu_custom_call" | custom-call | flops 1342177280 | bytes 1310720 | tf_op jit(solution)/shard_map/attention/pallas_call | solution.py:294
  19.2 1.6 %collective-permute-start.7 = (bf16[8,8,256]{2,1,0:T(8,128)(2,1)S(1)}, bf16[8,8,256]{2,1,0:T(8,128)(2,1)S(1)}, u32[]{:S(2)}, u32[]{:S(2)}) collective-permute-start(bf16[8,8,256]{2,1,0:T(8,128)(2,1)S(1)} %get-tuple-element.81.refs_9_), channel_id=1, source_target_pairs={{0,16},{1,3},{3,1},{2,6},{6,2},{7,5},{5,7},{4,8},{8,4},{9,11},{11,... | collective-permute-start | bytes 98312 | tf_op jit(solution)/shard_map/ppermute | solution.py:479
  20.7 0.0 collective-permute-done.1.refs_1_
  20.8 0.0 collective-permute-done.2.refs_2_
  20.8 0.0 collective-permute-done.3.refs_3_
  20.8 2.7 %attention.3 = (bf16[8,8,256]{2,1,0:T(8,128)(2,1)S(1)}, f32[8,2,256]{2,1,0:T(2,128)S(1)}) custom-call(bf16[384,128]{1,0:T(8,128)(2,1)S(1)} %get-tuple-element.53.refs_0_, bf16[384,128]{1,0:T(8,128)(2,1)S(1)} %collective-permute-done.1.refs_1_, bf16[384,128]{1,0:T(8,128)(2,1)S(1)} %collective-permute-done.2.refs_2_, ...), custom_call_target="tpu_custom_call" | custom-call | flops 805306368 | bytes 786432 | tf_op jit(solution)/shard_map/attention/pallas_call | solution.py:294
  23.5 0.5 %collective-permute-start.6 = (bf16[8,8,256]{2,1,0:T(8,128)(2,1)S(1)}, bf16[8,8,256]{2,1,0:T(8,128)(2,1)S(1)}, u32[]{:S(2)}, u32[]{:S(2)}) collective-permute-start(bf16[8,8,256]{2,1,0:T(8,128)(2,1)S(1)} %get-tuple-element.83.own), channel_id=1, source_target_pairs={{0,1},{1,0},{3,2},{2,3},{6,7},{7,6},{5,4},{4,5},{8,9},{9,8},{11,10... | collective-permute-start | bytes 98312 | tf_op jit(solution)/shard_map/ppermute | solution.py:479
  24.0 0.0 collective-permute-done.7.refs_1_
  24.0 0.9 %collective-permute-done.6.refs_0_ = bf16[8,8,256]{2,1,0:T(8,128)(2,1)S(1)} collective-permute-done((bf16[8,8,256]{2,1,0:T(8,128)(2,1)S(1)}, bf16[8,8,256]{2,1,0:T(8,128)(2,1)S(1)}, u32[]{:S(2)}, u32[]{:S(2)}) %collective-permute-start.6) | collective-permute-done | bytes 32800 | tf_op jit(solution)/shard_map/ppermute | solution.py:479
  24.8 3.1 %convolutions.1 = (f32[2,8,64]{2,1,0:T(8,128)S(1)}, f32[2,8,64]{2,1,0:T(8,128)S(1)}, f32[2,8,64]{2,1,0:T(8,128)S(1)}, f32[2,8,64]{2,1,0:T(8,128)S(1)}) custom-call(bf16[8,8,256]{2,1,0:T(8,128)(2,1)S(1)} %get-tuple-element.83.own, f32[8,2,256]{2,1,0:T(2,128)S(1)} %get-tuple-element.84.maps, bf16[8,8,256]{2,1,0:T(8,128)(2,1)S(1)} %collective-permute-done.6.refs_0_, ...), custom_call_target="tpu_custom_call" | custom-call | tf_op jit(solution)/shard_map/convolutions/pallas_call | solution.py:416
  27.9 1.2 %collective-permute-start.10 = (f32[2,8,64]{2,1,0:T(8,128)S(1)}, f32[2,8,64]{2,1,0:T(8,128)S(1)}, u32[]{:S(2)}, u32[]{:S(2)}) collective-permute-start(f32[2,8,64]{2,1,0:T(8,128)S(1)} %get-tuple-element.93), channel_id=1, source_target_pairs={{0,3},{1,2},{2,1},{3,0},{4,7},{5,6},{6,5},{7,4},{8,11},{9,10},{10,... | collective-permute-start | bytes 12296 | tf_op jit(solution)/shard_map/ppermute | solution.py:459
  29.2 0.4 %collective-permute-start.8 = (f32[2,8,64]{2,1,0:T(8,128)S(1)}, f32[2,8,64]{2,1,0:T(8,128)S(1)}, u32[]{:S(2)}, u32[]{:S(2)}) collective-permute-start(f32[2,8,64]{2,1,0:T(8,128)S(1)} %get-tuple-element.91), channel_id=1, source_target_pairs={{0,1},{1,0},{2,3},{3,2},{4,5},{5,4},{6,7},{7,6},{8,9},{9,8},{10,11... | collective-permute-start | bytes 12296 | tf_op jit(solution)/shard_map/ppermute | solution.py:459
  29.5 0.6 %collective-permute-start.9 = (f32[2,8,64]{2,1,0:T(8,128)S(1)}, f32[2,8,64]{2,1,0:T(8,128)S(1)}, u32[]{:S(2)}, u32[]{:S(2)}) collective-permute-start(f32[2,8,64]{2,1,0:T(8,128)S(1)} %get-tuple-element.92), channel_id=1, source_target_pairs={{0,2},{1,3},{2,0},{3,1},{4,6},{5,7},{6,4},{7,5},{8,10},{9,11},{10,... | collective-permute-start | bytes 12296 | tf_op jit(solution)/shard_map/ppermute | solution.py:459
  30.1 0.9 %collective-permute-done.10.refs_3_ = f32[2,8,64]{2,1,0:T(8,128)S(1)} collective-permute-done((f32[2,8,64]{2,1,0:T(8,128)S(1)}, f32[2,8,64]{2,1,0:T(8,128)S(1)}, u32[]{:S(2)}, u32[]{:S(2)}) %collective-permute-start.10) | collective-permute-done | bytes 4128 | tf_op jit(solution)/shard_map/ppermute | solution.py:459
  31.0 0.0 collective-permute-done.8.refs_1_
  31.1 2.1 %collective-permute-done.9.refs_2_ = f32[2,8,64]{2,1,0:T(8,128)S(1)} collective-permute-done((f32[2,8,64]{2,1,0:T(8,128)S(1)}, f32[2,8,64]{2,1,0:T(8,128)S(1)}, u32[]{:S(2)}, u32[]{:S(2)}) %collective-permute-start.9) | collective-permute-done | bytes 4128 | tf_op jit(solution)/shard_map/ppermute | solution.py:459
  33.2 0.6 %place.1 = (f32[32,64]{1,0:T(8,128)}, f32[32,64]{1,0:T(8,128)}) custom-call(f32[2,8,64]{2,1,0:T(8,128)S(1)} %get-tuple-element.90.refs_0_, f32[2,8,64]{2,1,0:T(8,128)S(1)} %collective-permute-done.8.refs_1_, f32[2,8,64]{2,1,0:T(8,128)S(1)} %collective-permute-done.9.refs_2_, f32[2,8,64]{2,1,0:T(8,128)S(1)} %collective-permute-done.10.refs_3_), custom_call_target="tpu_custom_call" | custom-call | tf_op jit(solution)/shard_map/place/pallas_call | solution.py:447
  (3 shorter events, 0.0 us)
Async XLA Ops:
  0.6 5.5 %copy-start.2 = (bf16[3,9,64,64]{3,2,1,0:T(8,128)(2,1)S(1)}, bf16[3,9,64,64]{3,2,1,0:T(8,128)(2,1)}, u32[]{:S(2)}) copy-start(bf16[3,9,64,64]{3,2,1,0:T(8,128)(2,1)} %param.18) | copy-start | bytes 663556
  0.6 5.5 %copy-start.4 = (bf16[128,128]{1,0:T(8,128)(2,1)S(1)}, bf16[128,128]{1,0:T(8,128)(2,1)}, u32[]{:S(2)}) copy-start(bf16[128,128]{1,0:T(8,128)(2,1)} %value) | copy-start | bytes 98308
  0.7 5.5 %copy-start.5 = (bf16[128,128]{1,0:T(8,128)(2,1)S(1)}, bf16[128,128]{1,0:T(8,128)(2,1)}, u32[]{:S(2)}) copy-start(bf16[128,128]{1,0:T(8,128)(2,1)} %out) | copy-start | bytes 98308
  0.7 5.5 %copy-start.6 = (bf16[128,128]{1,0:T(8,128)(2,1)S(1)}, bf16[128,128]{1,0:T(8,128)(2,1)}, u32[]{:S(2)}) copy-start(bf16[128,128]{1,0:T(8,128)(2,1)} %refs_5_.1) | copy-start | bytes 98308
  0.7 5.5 %copy-start.7 = (bf16[9,64,5]{1,2,0:T(8,128)(2,1)S(1)}, bf16[9,64,5]{1,2,0:T(8,128)(2,1)}, u32[]{:S(2)}) copy-start(bf16[9,64,5]{1,2,0:T(8,128)(2,1)} %param.17) | copy-start | bytes 17284
  0.7 5.5 %copy-start.8 = (bf16[9,2,64]{2,1,0:T(2,128)(2,1)S(1)}, bf16[9,2,64]{2,1,0:T(2,128)(2,1)}, u32[]{:S(2)}) copy-start(bf16[9,2,64]{2,1,0:T(2,128)(2,1)} %last) | copy-start | bytes 6916
  0.7 5.5 %copy-start.9 = (f32[128]{0:T(128)S(1)}, f32[128]{0:T(128)}, u32[]{:S(2)}) copy-start(f32[128]{0:T(128)} %param.16) | copy-start | bytes 1540
  0.7 5.7 %copy-start.1 = (bf16[32,64,128]{2,1,0:T(8,128)(2,1)S(1)}, bf16[32,64,128]{2,1,0:T(8,128)(2,1)}, u32[]{:S(2)}) copy-start(bf16[32,64,128]{2,1,0:T(8,128)(2,1)} %param.11) | copy-start | bytes 1572868
  3.0 3.5 %copy-start = (bf16[32,64,128]{2,1,0:T(8,128)(2,1)S(1)}, bf16[32,64,128]{2,1,0:T(8,128)(2,1)}, u32[]{:S(2)}) copy-start(bf16[32,64,128]{2,1,0:T(8,128)(2,1)} %param.10) | copy-start | bytes 1572868
  3.0 3.4 %collective-permute-start = (bf16[672,128]{1,0:T(8,128)(2,1)}, bf16[672,128]{1,0:T(8,128)(2,1)S(1)}, u32[]{:S(2)}, u32[]{:S(2)}) collective-permute-start(bf16[672,128]{1,0:T(8,128)(2,1)} %get-tuple-element.52), channel_id=1, source_target_pairs={{0,1},{1,0},{2,3},{3,2},{4,5},{5,4},{6,7},{7,6},{8,9},{9,8},{10,11... | collective-permute-start | bytes 516104 | tf_op jit(solution)/shard_map/ppermute | solution.py:459
  3.5 8.0 %collective-permute-start.4 = (bf16[672,128]{1,0:T(8,128)(2,1)}, bf16[672,128]{1,0:T(8,128)(2,1)S(1)}, u32[]{:S(2)}, u32[]{:S(2)}) collective-permute-start(bf16[672,128]{1,0:T(8,128)(2,1)} %get-tuple-element.79), channel_id=1, source_target_pairs={{0,2},{1,3},{2,0},{3,1},{4,6},{5,7},{6,4},{7,5},{8,10},{9,11},{10,... | collective-permute-start | bytes 516104 | tf_op jit(solution)/shard_map/ppermute | solution.py:459
  6.1 8.7 %collective-permute-start.5 = (bf16[672,128]{1,0:T(8,128)(2,1)}, bf16[672,128]{1,0:T(8,128)(2,1)S(1)}, u32[]{:S(2)}, u32[]{:S(2)}) collective-permute-start(bf16[672,128]{1,0:T(8,128)(2,1)} %get-tuple-element.80), channel_id=1, source_target_pairs={{0,3},{1,2},{2,1},{3,0},{4,7},{5,6},{6,5},{7,4},{8,11},{9,10},{10,... | collective-permute-start | bytes 516104 | tf_op jit(solution)/shard_map/ppermute | solution.py:459
  6.2 0.8 %copy-start.3 = (f32[3,32,64]{2,1,0:T(8,128)S(1)}, f32[3,32,64]{2,1,0:T(8,128)}, u32[]{:S(2)}) copy-start(f32[3,32,64]{2,1,0:T(8,128)} %image.3) | copy-start | bytes 73732
  6.4 8.4 %copy-start.10 = (bf16[672,128]{1,0:T(8,128)(2,1)S(1)}, bf16[672,128]{1,0:T(8,128)(2,1)}, u32[]{:S(2)}) copy-start(bf16[672,128]{1,0:T(8,128)(2,1)} %get-tuple-element.78.refs_0_) | copy-start | bytes 516100
  7.6 13.1 %collective-permute-start.1 = (bf16[384,128]{1,0:T(8,128)(2,1)S(1)}, bf16[384,128]{1,0:T(8,128)(2,1)S(1)}, u32[]{:S(2)}, u32[]{:S(2)}) collective-permute-start(bf16[384,128]{1,0:T(8,128)(2,1)S(1)} %get-tuple-element.54), channel_id=1, source_target_pairs={{0,1},{1,0},{2,3},{3,2},{4,5},{5,4},{6,7},{7,6},{8,9},{9,8},{10,11... | collective-permute-start | bytes 294920 | tf_op jit(solution)/shard_map/ppermute | solution.py:459
  7.8 12.9 %collective-permute-start.2 = (bf16[384,128]{1,0:T(8,128)(2,1)S(1)}, bf16[384,128]{1,0:T(8,128)(2,1)S(1)}, u32[]{:S(2)}, u32[]{:S(2)}) collective-permute-start(bf16[384,128]{1,0:T(8,128)(2,1)S(1)} %get-tuple-element.55), channel_id=1, source_target_pairs={{0,2},{1,3},{2,0},{3,1},{4,6},{5,7},{6,4},{7,5},{8,10},{9,11},{10,... | collective-permute-start | bytes 294920 | tf_op jit(solution)/shard_map/ppermute | solution.py:459
  9.8 11.0 %collective-permute-start.3 = (bf16[384,128]{1,0:T(8,128)(2,1)S(1)}, bf16[384,128]{1,0:T(8,128)(2,1)S(1)}, u32[]{:S(2)}, u32[]{:S(2)}) collective-permute-start(bf16[384,128]{1,0:T(8,128)(2,1)S(1)} %get-tuple-element.56), channel_id=1, source_target_pairs={{0,3},{1,2},{2,1},{3,0},{4,7},{5,6},{6,5},{7,4},{8,11},{9,10},{10,... | collective-permute-start | bytes 294920 | tf_op jit(solution)/shard_map/ppermute | solution.py:459
  19.2 4.8 %collective-permute-start.7 = (bf16[8,8,256]{2,1,0:T(8,128)(2,1)S(1)}, bf16[8,8,256]{2,1,0:T(8,128)(2,1)S(1)}, u32[]{:S(2)}, u32[]{:S(2)}) collective-permute-start(bf16[8,8,256]{2,1,0:T(8,128)(2,1)S(1)} %get-tuple-element.81.refs_9_), channel_id=1, source_target_pairs={{0,16},{1,3},{3,1},{2,6},{6,2},{7,5},{5,7},{4,8},{8,4},{9,11},{11,... | collective-permute-start | bytes 98312 | tf_op jit(solution)/shard_map/ppermute | solution.py:479
  23.5 1.3 %collective-permute-start.6 = (bf16[8,8,256]{2,1,0:T(8,128)(2,1)S(1)}, bf16[8,8,256]{2,1,0:T(8,128)(2,1)S(1)}, u32[]{:S(2)}, u32[]{:S(2)}) collective-permute-start(bf16[8,8,256]{2,1,0:T(8,128)(2,1)S(1)} %get-tuple-element.83.own), channel_id=1, source_target_pairs={{0,1},{1,0},{3,2},{2,3},{6,7},{7,6},{5,4},{4,5},{8,9},{9,8},{11,10... | collective-permute-start | bytes 98312 | tf_op jit(solution)/shard_map/ppermute | solution.py:479
  27.9 3.1 %collective-permute-start.10 = (f32[2,8,64]{2,1,0:T(8,128)S(1)}, f32[2,8,64]{2,1,0:T(8,128)S(1)}, u32[]{:S(2)}, u32[]{:S(2)}) collective-permute-start(f32[2,8,64]{2,1,0:T(8,128)S(1)} %get-tuple-element.93), channel_id=1, source_target_pairs={{0,3},{1,2},{2,1},{3,0},{4,7},{5,6},{6,5},{7,4},{8,11},{9,10},{10,... | collective-permute-start | bytes 12296 | tf_op jit(solution)/shard_map/ppermute | solution.py:459
  29.2 1.9 %collective-permute-start.8 = (f32[2,8,64]{2,1,0:T(8,128)S(1)}, f32[2,8,64]{2,1,0:T(8,128)S(1)}, u32[]{:S(2)}, u32[]{:S(2)}) collective-permute-start(f32[2,8,64]{2,1,0:T(8,128)S(1)} %get-tuple-element.91), channel_id=1, source_target_pairs={{0,1},{1,0},{2,3},{3,2},{4,5},{5,4},{6,7},{7,6},{8,9},{9,8},{10,11... | collective-permute-start | bytes 12296 | tf_op jit(solution)/shard_map/ppermute | solution.py:459
  29.5 3.7 %collective-permute-start.9 = (f32[2,8,64]{2,1,0:T(8,128)S(1)}, f32[2,8,64]{2,1,0:T(8,128)S(1)}, u32[]{:S(2)}, u32[]{:S(2)}) collective-permute-start(f32[2,8,64]{2,1,0:T(8,128)S(1)} %get-tuple-element.92), channel_id=1, source_target_pairs={{0,2},{1,3},{2,0},{3,1},{4,6},{5,7},{6,4},{7,5},{8,10},{9,11},{10,... | collective-permute-start | bytes 12296 | tf_op jit(solution)/shard_map/ppermute | solution.py:459

commit v4 on v3

--- a/solution.py
+++ b/solution.py
@@ -480,8 +480,8 @@
 
 
 def chunks_of(rows):
-    first = -(-5 * rows // 8)
-    return (first, rows - first)
+    ends = 3 * rows // 8
+    return tuple(c for c in (ends, rows - 2 * ends, ends) if c)
 
 
 def per_device(

time: 34 us -> 31.5 us (0.926)
  waiting for transfers between devices: 8.95 us -> 3.25 us
  starting transfers between devices: 9.52 us -> 12.2 us
  Pallas kernels: 13.9 us -> 14.4 us
    ppermute x9 -> x12, waiting for transfers between devices: 8.09 us -> 2.06 us  [swap(): return lax.ppermute(x, GROUP, [(i, i ^ k) for i in range(count)])]
    ppermute x9 -> x12, starting transfers between devices: 7.46 us -> 10.5 us  [swap(): return lax.ppermute(x, GROUP, [(i, i ^ k) for i in range(count)])]
    ppermute x2, starting transfers between devices: 2.07 us -> 1.66 us  [neighbours(): return lax.ppermute(x, ('grp',) + BANDS, targets)]
    pallas_call x2 -> x3, Pallas kernels: 2.91 us -> 3.16 us  [pack(): pl.pallas_call(functools.partial(pack_kernel, chunk, cuts), name='pack',...]
    pallas_call x2 -> x3, Pallas kernels: 7.09 us -> 7.3 us  [attention(): pl.pallas_call(functools.partial(attention_kernel, cuts, chunk), name='at...]
  transfers between devices with their start and end apart: 11 -> 14, of which waited for: 5 -> 2; matrix products, arithmetic and copies ran while one was open for 0% -> 0% of each run, Pallas kernels for 23% -> 28%
where the time goes in v4:
time: 31.5 us; the launch traced here: 31.3 us
  Pallas kernels  14.4 us (46%)
  starting transfers between devices  12.2 us (39%)
  waiting for transfers between devices  3.25 us (10%)
  between operations  0.83 us (3%)
  local copies, waits for them, and re-layouts  0.68 us (2%)
    ppermute x12, starting transfers between devices, swap(): return lax.ppermute(x, GROUP, [(i, i ^ k) for i in range(count)])  10.5 us
    pallas_call x3, Pallas kernels, attention(): pl.pallas_call(functools.partial(attention_kernel, cuts, chunk), name='at...  7.3 us
    pallas_call x3, Pallas kernels, pack(): pl.pallas_call(functools.partial(pack_kernel, chunk, cuts), name='pack',...  3.16 us
    pallas_call x1, Pallas kernels, convolutions(): pl.pallas_call(functools.partial(conv_kernel, group, hops), name='convolu...  3.12 us
    ppermute x12, waiting for transfers between devices, swap(): return lax.ppermute(x, GROUP, [(i, i ^ k) for i in range(count)])  2.06 us
    ppermute x2, starting transfers between devices, neighbours(): return lax.ppermute(x, ('grp',) + BANDS, targets)  1.66 us
    ppermute x2, waiting for transfers between devices, neighbours(): return lax.ppermute(x, ('grp',) + BANDS, targets)  1.19 us
    unnamed x22, local copies, waits for them, and re-layouts  0.68 us
  transfers between devices with their start and end apart: 14, of which 2 were waited for; matrix products, arithmetic and copies ran while one was open for 0% of the time, Pallas kernels for 28%

profile of v4, /device:TPU:0, one launch (start us, length us, event | category | flops | bytes accessed | tf_op | source)
XLA Modules:
  0.0 31.3 jit_solution(15374955595177016653)
XLA Ops:
  0.6 0.0 copy-start
  0.7 2.0 %pack.3 = (bf16[416,128]{1,0:T(8,128)(2,1)}, bf16[416,128]{1,0:T(8,128)(2,1)}, bf16[416,128]{1,0:T(8,128)(2,1)}, bf16[416,128]{1,0:T(8,128)(2,1)}) custom-call(bf16[2048,128]{1,0:T(8,128)(2,1)} %bitcast.5, bf16[2048,128]{1,0:T(8,128)(2,1)} %bitcast.8, f32[3,32,64]{2,1,0:T(8,128)} %image.5), custom_call_target="tpu_custom_call" | custom-call | tf_op jit(solution)/shard_map/pack/pallas_call | solution.py:164
  2.6 0.0 copy-start.3
  2.6 0.0 copy-start.4
  2.6 0.0 copy-start.5
  2.7 0.0 copy-start.6
  2.7 0.5 %collective-permute-start = (bf16[416,128]{1,0:T(8,128)(2,1)}, bf16[416,128]{1,0:T(8,128)(2,1)S(1)}, u32[]{:S(2)}, u32[]{:S(2)}) collective-permute-start(bf16[416,128]{1,0:T(8,128)(2,1)} %get-tuple-element.58), channel_id=1, source_target_pairs={{0,1},{1,0},{2,3},{3,2},{4,5},{5,4},{6,7},{7,6},{8,9},{9,8},{10,11... | collective-permute-start | bytes 319496 | tf_op jit(solution)/shard_map/ppermute | solution.py:459
  3.2 2.6 %collective-permute-start.7 = (bf16[416,128]{1,0:T(8,128)(2,1)}, bf16[416,128]{1,0:T(8,128)(2,1)S(1)}, u32[]{:S(2)}, u32[]{:S(2)}) collective-permute-start(bf16[416,128]{1,0:T(8,128)(2,1)} %get-tuple-element.89), channel_id=1, source_target_pairs={{0,2},{1,3},{2,0},{3,1},{4,6},{5,7},{6,4},{7,5},{8,10},{9,11},{10,... | collective-permute-start | bytes 319496 | tf_op jit(solution)/shard_map/ppermute | solution.py:459
  5.8 0.1 collective-permute-start.8
  5.8 0.0 collective-permute-done.refs_0_.refs_1_
  5.8 0.0 copy-start.7
  5.9 0.5 %pack.4 = (bf16[256,128]{1,0:T(8,128)(2,1)S(1)}, bf16[256,128]{1,0:T(8,128)(2,1)S(1)}, bf16[256,128]{1,0:T(8,128)(2,1)S(1)}, bf16[256,128]{1,0:T(8,128)(2,1)S(1)}) custom-call(bf16[2048,128]{1,0:T(8,128)(2,1)S(1)} %bitcast.6, bf16[2048,128]{1,0:T(8,128)(2,1)S(1)} %bitcast.9, f32[3,32,64]{2,1,0:T(8,128)S(1)} %copy-done.2, ...), custom_call_target="tpu_custom_call" | custom-call | tf_op jit(solution)/shard_map/pack/pallas_call | solution.py:164
  6.4 0.0 copy-start.8
  6.4 0.2 collective-permute-start.1
  6.6 0.0 copy-done.4
  6.6 0.4 %copy-done.8 = bf16[9,2,64]{2,1,0:T(2,128)(2,1)S(1)} copy-done((bf16[9,2,64]{2,1,0:T(2,128)(2,1)S(1)}, bf16[9,2,64]{2,1,0:T(2,128)(2,1)}, u32[]{:S(2)}) %copy-start.8) | copy-done | bytes 2328
  7.1 0.2 copy-done.9
  7.2 0.2 weights.1
  7.4 2.0 %collective-permute-start.5 = (bf16[256,128]{1,0:T(8,128)(2,1)S(1)}, bf16[256,128]{1,0:T(8,128)(2,1)S(1)}, u32[]{:S(2)}, u32[]{:S(2)}) collective-permute-start(bf16[256,128]{1,0:T(8,128)(2,1)S(1)} %get-tuple-element.86), channel_id=1, source_target_pairs={{0,2},{1,3},{2,0},{3,1},{4,6},{5,7},{6,4},{7,5},{8,10},{9,11},{10,... | collective-permute-start | bytes 196616 | tf_op jit(solution)/shard_map/ppermute | solution.py:459
  9.4 0.0 collective-permute-start.6
  9.5 0.0 collective-permute-done.1.refs_0_.refs_1_
  9.5 0.7 %pack.5 = (bf16[384,128]{1,0:T(8,128)(2,1)S(1)}, bf16[384,128]{1,0:T(8,128)(2,1)S(1)}, bf16[384,128]{1,0:T(8,128)(2,1)S(1)}, bf16[384,128]{1,0:T(8,128)(2,1)S(1)}) custom-call(bf16[2048,128]{1,0:T(8,128)(2,1)S(1)} %bitcast.7, bf16[2048,128]{1,0:T(8,128)(2,1)S(1)} %bitcast.10, f32[3,32,64]{2,1,0:T(8,128)S(1)} %copy-done.2, ...), custom_call_target="tpu_custom_call" | custom-call | tf_op jit(solution)/shard_map/pack/pallas_call | solution.py:164
  10.2 0.2 collective-permute-start.2
  10.4 0.0 collective-permute-done.7.refs_2_
  10.4 1.9 %collective-permute-start.3 = (bf16[384,128]{1,0:T(8,128)(2,1)S(1)}, bf16[384,128]{1,0:T(8,128)(2,1)S(1)}, u32[]{:S(2)}, u32[]{:S(2)}) collective-permute-start(bf16[384,128]{1,0:T(8,128)(2,1)S(1)} %get-tuple-element.62), channel_id=1, source_target_pairs={{0,2},{1,3},{2,0},{3,1},{4,6},{5,7},{6,4},{7,5},{8,10},{9,11},{10,... | collective-permute-start | bytes 294920 | tf_op jit(solution)/shard_map/ppermute | solution.py:459
  12.3 0.0 collective-permute-done.8.refs_3_
  12.3 1.1 %collective-permute-start.4 = (bf16[384,128]{1,0:T(8,128)(2,1)S(1)}, bf16[384,128]{1,0:T(8,128)(2,1)S(1)}, u32[]{:S(2)}, u32[]{:S(2)}) collective-permute-start(bf16[384,128]{1,0:T(8,128)(2,1)S(1)} %get-tuple-element.63), channel_id=1, source_target_pairs={{0,3},{1,2},{2,1},{3,0},{4,7},{5,6},{6,5},{7,4},{8,11},{9,10},{10,... | collective-permute-start | bytes 294920 | tf_op jit(solution)/shard_map/ppermute | solution.py:459
  13.4 0.0 copy-done.10
  13.4 2.7 %attention.3 = (bf16[8,8,256]{2,1,0:T(8,128)(2,1)S(1)}, f32[8,2,256]{2,1,0:T(2,128)S(1)}) custom-call(bf16[416,128]{1,0:T(8,128)(2,1)S(1)} %copy-done.10, bf16[416,128]{1,0:T(8,128)(2,1)S(1)} %collective-permute-done.refs_0_.refs_1_, bf16[416,128]{1,0:T(8,128)(2,1)S(1)} %collective-permute-done.7.refs_2_, ...), custom_call_target="tpu_custom_call" | custom-call | flops 805306368 | bytes 786432 | tf_op jit(solution)/shard_map/attention/pallas_call | solution.py:294
  16.1 0.0 collective-permute-done.5.refs_2_
  16.2 0.0 collective-permute-done.6.refs_3_
  16.2 1.9 %attention.4 = (bf16[8,8,256]{2,1,0:T(8,128)(2,1)S(1)}, f32[8,2,256]{2,1,0:T(2,128)S(1)}) custom-call(bf16[256,128]{1,0:T(8,128)(2,1)S(1)} %get-tuple-element.85.refs_0_, bf16[256,128]{1,0:T(8,128)(2,1)S(1)} %collective-permute-done.1.refs_0_.refs_1_, bf16[256,128]{1,0:T(8,128)(2,1)S(1)} %collective-permute-done.5.refs_2_, ...), custom_call_target="tpu_custom_call" | custom-call | flops 536870912 | bytes 524288 | tf_op jit(solution)/shard_map/attention/pallas_call | solution.py:294
  18.0 1.6 %collective-permute-start.10 = (bf16[8,8,256]{2,1,0:T(8,128)(2,1)S(1)}, bf16[8,8,256]{2,1,0:T(8,128)(2,1)S(1)}, u32[]{:S(2)}, u32[]{:S(2)}) collective-permute-start(bf16[8,8,256]{2,1,0:T(8,128)(2,1)S(1)} %get-tuple-element.93.refs_9_), channel_id=1, source_target_pairs={{0,16},{1,3},{3,1},{2,6},{6,2},{7,5},{5,7},{4,8},{8,4},{9,11},{11,... | collective-permute-start | bytes 98312 | tf_op jit(solution)/shard_map/ppermute | solution.py:479
  19.6 0.0 collective-permute-done.2.refs_1_
  19.6 0.0 collective-permute-done.3.refs_2_
  19.6 0.0 collective-permute-done.4.refs_3_
  19.7 2.7 %attention.5 = (bf16[8,8,256]{2,1,0:T(8,128)(2,1)S(1)}, f32[8,2,256]{2,1,0:T(2,128)S(1)}) custom-call(bf16[384,128]{1,0:T(8,128)(2,1)S(1)} %get-tuple-element.60.refs_0_, bf16[384,128]{1,0:T(8,128)(2,1)S(1)} %collective-permute-done.2.refs_1_, bf16[384,128]{1,0:T(8,128)(2,1)S(1)} %collective-permute-done.3.refs_2_, ...), custom_call_target="tpu_custom_call" | custom-call | flops 805306368 | bytes 786432 | tf_op jit(solution)/shard_map/attention/pallas_call | solution.py:294
  22.4 0.1 collective-permute-start.9
  22.5 0.0 collective-permute-done.10.refs_1_
  22.5 1.2 %collective-permute-done.9.refs_0_ = bf16[8,8,256]{2,1,0:T(8,128)(2,1)S(1)} collective-permute-done((bf16[8,8,256]{2,1,0:T(8,128)(2,1)S(1)}, bf16[8,8,256]{2,1,0:T(8,128)(2,1)S(1)}, u32[]{:S(2)}, u32[]{:S(2)}) %collective-permute-start.9) | collective-permute-done | bytes 32800 | tf_op jit(solution)/shard_map/ppermute | solution.py:479
  23.7 3.1 %convolutions.1 = (f32[2,8,64]{2,1,0:T(8,128)S(1)}, f32[2,8,64]{2,1,0:T(8,128)S(1)}, f32[2,8,64]{2,1,0:T(8,128)S(1)}, f32[2,8,64]{2,1,0:T(8,128)S(1)}) custom-call(bf16[8,8,256]{2,1,0:T(8,128)(2,1)S(1)} %get-tuple-element.95.own, f32[8,2,256]{2,1,0:T(2,128)S(1)} %get-tuple-element.96.maps, bf16[8,8,256]{2,1,0:T(8,128)(2,1)S(1)} %collective-permute-done.9.refs_0_, ...), custom_call_target="tpu_custom_call" | custom-call | tf_op jit(solution)/shard_map/convolutions/pallas_call | solution.py:416
  26.8 0.2 collective-permute-start.11
  27.0 0.6 %collective-permute-start.12 = (f32[2,8,64]{2,1,0:T(8,128)S(1)}, f32[2,8,64]{2,1,0:T(8,128)S(1)}, u32[]{:S(2)}, u32[]{:S(2)}) collective-permute-start(f32[2,8,64]{2,1,0:T(8,128)S(1)} %get-tuple-element.104), channel_id=1, source_target_pairs={{0,2},{1,3},{2,0},{3,1},{4,6},{5,7},{6,4},{7,5},{8,10},{9,11},{10,... | collective-permute-start | bytes 12296 | tf_op jit(solution)/shard_map/ppermute | solution.py:459
  27.5 1.1 %collective-permute-start.13 = (f32[2,8,64]{2,1,0:T(8,128)S(1)}, f32[2,8,64]{2,1,0:T(8,128)S(1)}, u32[]{:S(2)}, u32[]{:S(2)}) collective-permute-start(f32[2,8,64]{2,1,0:T(8,128)S(1)} %get-tuple-element.105), channel_id=1, source_target_pairs={{0,3},{1,2},{2,1},{3,0},{4,7},{5,6},{6,5},{7,4},{8,11},{9,10},{10,... | collective-permute-start | bytes 12296 | tf_op jit(solution)/shard_map/ppermute | solution.py:459
  28.7 0.0 collective-permute-done.11.refs_1_
  28.7 2.0 %collective-permute-done.12.refs_2_ = f32[2,8,64]{2,1,0:T(8,128)S(1)} collective-permute-done((f32[2,8,64]{2,1,0:T(8,128)S(1)}, f32[2,8,64]{2,1,0:T(8,128)S(1)}, u32[]{:S(2)}, u32[]{:S(2)}) %collective-permute-start.12) | collective-permute-done | bytes 4128 | tf_op jit(solution)/shard_map/ppermute | solution.py:459
  30.7 0.0 collective-permute-done.13.refs_3_
  30.7 0.6 %place.1 = (f32[32,64]{1,0:T(8,128)}, f32[32,64]{1,0:T(8,128)}) custom-call(f32[2,8,64]{2,1,0:T(8,128)S(1)} %get-tuple-element.102.refs_0_, f32[2,8,64]{2,1,0:T(8,128)S(1)} %collective-permute-done.11.refs_1_, f32[2,8,64]{2,1,0:T(8,128)S(1)} %collective-permute-done.12.refs_2_, f32[2,8,64]{2,1,0:T(8,128)S(1)} %collective-permute-done.13.refs_3_), custom_call_target="tpu_custom_call" | custom-call | tf_op jit(solution)/shard_map/place/pallas_call | solution.py:447
  (11 shorter events, 0.0 us)
Async XLA Ops:
  0.6 5.2 %copy-start = (bf16[32,64,128]{2,1,0:T(8,128)(2,1)S(1)}, bf16[32,64,128]{2,1,0:T(8,128)(2,1)}, u32[]{:S(2)}) copy-start(bf16[32,64,128]{2,1,0:T(8,128)(2,1)} %param.10) | copy-start | bytes 1572868
  0.6 5.2 %copy-start.1 = (bf16[32,64,128]{2,1,0:T(8,128)(2,1)S(1)}, bf16[32,64,128]{2,1,0:T(8,128)(2,1)}, u32[]{:S(2)}) copy-start(bf16[32,64,128]{2,1,0:T(8,128)(2,1)} %param.11) | copy-start | bytes 1572868
  0.6 5.2 %copy-start.2 = (f32[3,32,64]{2,1,0:T(8,128)S(1)}, f32[3,32,64]{2,1,0:T(8,128)}, u32[]{:S(2)}) copy-start(f32[3,32,64]{2,1,0:T(8,128)} %image.5) | copy-start | bytes 73732
  2.6 4.0 %copy-start.3 = (bf16[3,9,64,64]{3,2,1,0:T(8,128)(2,1)S(1)}, bf16[3,9,64,64]{3,2,1,0:T(8,128)(2,1)}, u32[]{:S(2)}) copy-start(bf16[3,9,64,64]{3,2,1,0:T(8,128)(2,1)} %param.18) | copy-start | bytes 663556
  2.6 4.0 %copy-start.4 = (bf16[128,128]{1,0:T(8,128)(2,1)S(1)}, bf16[128,128]{1,0:T(8,128)(2,1)}, u32[]{:S(2)}) copy-start(bf16[128,128]{1,0:T(8,128)(2,1)} %value) | copy-start | bytes 98308
  2.6 4.0 %copy-start.5 = (bf16[128,128]{1,0:T(8,128)(2,1)S(1)}, bf16[128,128]{1,0:T(8,128)(2,1)}, u32[]{:S(2)}) copy-start(bf16[128,128]{1,0:T(8,128)(2,1)} %out) | copy-start | bytes 98308
  2.7 3.9 %copy-start.6 = (bf16[128,128]{1,0:T(8,128)(2,1)S(1)}, bf16[128,128]{1,0:T(8,128)(2,1)}, u32[]{:S(2)}) copy-start(bf16[128,128]{1,0:T(8,128)(2,1)} %refs_5_.2) | copy-start | bytes 98308
  2.7 3.2 %collective-permute-start = (bf16[416,128]{1,0:T(8,128)(2,1)}, bf16[416,128]{1,0:T(8,128)(2,1)S(1)}, u32[]{:S(2)}, u32[]{:S(2)}) collective-permute-start(bf16[416,128]{1,0:T(8,128)(2,1)} %get-tuple-element.58), channel_id=1, source_target_pairs={{0,1},{1,0},{2,3},{3,2},{4,5},{5,4},{6,7},{7,6},{8,9},{9,8},{10,11... | collective-permute-start | bytes 319496 | tf_op jit(solution)/shard_map/ppermute | solution.py:459
  3.2 7.2 %collective-permute-start.7 = (bf16[416,128]{1,0:T(8,128)(2,1)}, bf16[416,128]{1,0:T(8,128)(2,1)S(1)}, u32[]{:S(2)}, u32[]{:S(2)}) collective-permute-start(bf16[416,128]{1,0:T(8,128)(2,1)} %get-tuple-element.89), channel_id=1, source_target_pairs={{0,2},{1,3},{2,0},{3,1},{4,6},{5,7},{6,4},{7,5},{8,10},{9,11},{10,... | collective-permute-start | bytes 319496 | tf_op jit(solution)/shard_map/ppermute | solution.py:459
  5.8 6.6 %collective-permute-start.8 = (bf16[416,128]{1,0:T(8,128)(2,1)}, bf16[416,128]{1,0:T(8,128)(2,1)S(1)}, u32[]{:S(2)}, u32[]{:S(2)}) collective-permute-start(bf16[416,128]{1,0:T(8,128)(2,1)} %get-tuple-element.90), channel_id=1, source_target_pairs={{0,3},{1,2},{2,1},{3,0},{4,7},{5,6},{6,5},{7,4},{8,11},{9,10},{10,... | collective-permute-start | bytes 319496 | tf_op jit(solution)/shard_map/ppermute | solution.py:459
  5.8 0.8 %copy-start.7 = (bf16[9,64,5]{1,2,0:T(8,128)(2,1)S(1)}, bf16[9,64,5]{1,2,0:T(8,128)(2,1)}, u32[]{:S(2)}) copy-start(bf16[9,64,5]{1,2,0:T(8,128)(2,1)} %param.17) | copy-start | bytes 17284
  6.4 0.7 %copy-start.8 = (bf16[9,2,64]{2,1,0:T(2,128)(2,1)S(1)}, bf16[9,2,64]{2,1,0:T(2,128)(2,1)}, u32[]{:S(2)}) copy-start(bf16[9,2,64]{2,1,0:T(2,128)(2,1)} %last) | copy-start | bytes 6916
  6.4 3.1 %collective-permute-start.1 = (bf16[256,128]{1,0:T(8,128)(2,1)S(1)}, bf16[256,128]{1,0:T(8,128)(2,1)S(1)}, u32[]{:S(2)}, u32[]{:S(2)}) collective-permute-start(bf16[256,128]{1,0:T(8,128)(2,1)S(1)} %get-tuple-element.59), channel_id=1, source_target_pairs={{0,1},{1,0},{2,3},{3,2},{4,5},{5,4},{6,7},{7,6},{8,9},{9,8},{10,11... | collective-permute-start | bytes 196616 | tf_op jit(solution)/shard_map/ppermute | solution.py:459
  6.6 0.7 %copy-start.9 = (f32[128]{0:T(128)S(1)}, f32[128]{0:T(128)}, u32[]{:S(2)}) copy-start(f32[128]{0:T(128)} %param.16) | copy-start | bytes 1540
  7.4 8.7 %collective-permute-start.5 = (bf16[256,128]{1,0:T(8,128)(2,1)S(1)}, bf16[256,128]{1,0:T(8,128)(2,1)S(1)}, u32[]{:S(2)}, u32[]{:S(2)}) collective-permute-start(bf16[256,128]{1,0:T(8,128)(2,1)S(1)} %get-tuple-element.86), channel_id=1, source_target_pairs={{0,2},{1,3},{2,0},{3,1},{4,6},{5,7},{6,4},{7,5},{8,10},{9,11},{10,... | collective-permute-start | bytes 196616 | tf_op jit(solution)/shard_map/ppermute | solution.py:459
  9.4 4.0 %copy-start.10 = (bf16[416,128]{1,0:T(8,128)(2,1)S(1)}, bf16[416,128]{1,0:T(8,128)(2,1)}, u32[]{:S(2)}) copy-start(bf16[416,128]{1,0:T(8,128)(2,1)} %get-tuple-element.88.refs_0_) | copy-start | bytes 319492
  9.4 6.7 %collective-permute-start.6 = (bf16[256,128]{1,0:T(8,128)(2,1)S(1)}, bf16[256,128]{1,0:T(8,128)(2,1)S(1)}, u32[]{:S(2)}, u32[]{:S(2)}) collective-permute-start(bf16[256,128]{1,0:T(8,128)(2,1)S(1)} %get-tuple-element.87), channel_id=1, source_target_pairs={{0,3},{1,2},{2,1},{3,0},{4,7},{5,6},{6,5},{7,4},{8,11},{9,10},{10,... | collective-permute-start | bytes 196616 | tf_op jit(solution)/shard_map/ppermute | solution.py:459
  10.2 9.5 %collective-permute-start.2 = (bf16[384,128]{1,0:T(8,128)(2,1)S(1)}, bf16[384,128]{1,0:T(8,128)(2,1)S(1)}, u32[]{:S(2)}, u32[]{:S(2)}) collective-permute-start(bf16[384,128]{1,0:T(8,128)(2,1)S(1)} %get-tuple-element.61), channel_id=1, source_target_pairs={{0,1},{1,0},{2,3},{3,2},{4,5},{5,4},{6,7},{7,6},{8,9},{9,8},{10,11... | collective-permute-start | bytes 294920 | tf_op jit(solution)/shard_map/ppermute | solution.py:459
  10.4 9.3 %collective-permute-start.3 = (bf16[384,128]{1,0:T(8,128)(2,1)S(1)}, bf16[384,128]{1,0:T(8,128)(2,1)S(1)}, u32[]{:S(2)}, u32[]{:S(2)}) collective-permute-start(bf16[384,128]{1,0:T(8,128)(2,1)S(1)} %get-tuple-element.62), channel_id=1, source_target_pairs={{0,2},{1,3},{2,0},{3,1},{4,6},{5,7},{6,4},{7,5},{8,10},{9,11},{10,... | collective-permute-start | bytes 294920 | tf_op jit(solution)/shard_map/ppermute | solution.py:459
  12.3 7.3 %collective-permute-start.4 = (bf16[384,128]{1,0:T(8,128)(2,1)S(1)}, bf16[384,128]{1,0:T(8,128)(2,1)S(1)}, u32[]{:S(2)}, u32[]{:S(2)}) collective-permute-start(bf16[384,128]{1,0:T(8,128)(2,1)S(1)} %get-tuple-element.63), channel_id=1, source_target_pairs={{0,3},{1,2},{2,1},{3,0},{4,7},{5,6},{6,5},{7,4},{8,11},{9,10},{10,... | collective-permute-start | bytes 294920 | tf_op jit(solution)/shard_map/ppermute | solution.py:459
  18.0 4.4 %collective-permute-start.10 = (bf16[8,8,256]{2,1,0:T(8,128)(2,1)S(1)}, bf16[8,8,256]{2,1,0:T(8,128)(2,1)S(1)}, u32[]{:S(2)}, u32[]{:S(2)}) collective-permute-start(bf16[8,8,256]{2,1,0:T(8,128)(2,1)S(1)} %get-tuple-element.93.refs_9_), channel_id=1, source_target_pairs={{0,16},{1,3},{3,1},{2,6},{6,2},{7,5},{5,7},{4,8},{8,4},{9,11},{11,... | collective-permute-start | bytes 98312 | tf_op jit(solution)/shard_map/ppermute | solution.py:479
  22.4 1.3 %collective-permute-start.9 = (bf16[8,8,256]{2,1,0:T(8,128)(2,1)S(1)}, bf16[8,8,256]{2,1,0:T(8,128)(2,1)S(1)}, u32[]{:S(2)}, u32[]{:S(2)}) collective-permute-start(bf16[8,8,256]{2,1,0:T(8,128)(2,1)S(1)} %get-tuple-element.95.own), channel_id=1, source_target_pairs={{0,1},{1,0},{3,2},{2,3},{6,7},{7,6},{5,4},{4,5},{8,9},{9,8},{11,10... | collective-permute-start | bytes 98312 | tf_op jit(solution)/shard_map/ppermute | solution.py:479
  26.8 1.9 %collective-permute-start.11 = (f32[2,8,64]{2,1,0:T(8,128)S(1)}, f32[2,8,64]{2,1,0:T(8,128)S(1)}, u32[]{:S(2)}, u32[]{:S(2)}) collective-permute-start(f32[2,8,64]{2,1,0:T(8,128)S(1)} %get-tuple-element.103), channel_id=1, source_target_pairs={{0,1},{1,0},{2,3},{3,2},{4,5},{5,4},{6,7},{7,6},{8,9},{9,8},{10,11... | collective-permute-start | bytes 12296 | tf_op jit(solution)/shard_map/ppermute | solution.py:459
  27.0 3.7 %collective-permute-start.12 = (f32[2,8,64]{2,1,0:T(8,128)S(1)}, f32[2,8,64]{2,1,0:T(8,128)S(1)}, u32[]{:S(2)}, u32[]{:S(2)}) collective-permute-start(f32[2,8,64]{2,1,0:T(8,128)S(1)} %get-tuple-element.104), channel_id=1, source_target_pairs={{0,2},{1,3},{2,0},{3,1},{4,6},{5,7},{6,4},{7,5},{8,10},{9,11},{10,... | collective-permute-start | bytes 12296 | tf_op jit(solution)/shard_map/ppermute | solution.py:459
  27.5 3.2 %collective-permute-start.13 = (f32[2,8,64]{2,1,0:T(8,128)S(1)}, f32[2,8,64]{2,1,0:T(8,128)S(1)}, u32[]{:S(2)}, u32[]{:S(2)}) collective-permute-start(f32[2,8,64]{2,1,0:T(8,128)S(1)} %get-tuple-element.105), channel_id=1, source_target_pairs={{0,3},{1,2},{2,1},{3,0},{4,7},{5,6},{6,5},{7,4},{8,11},{9,10},{10,... | collective-permute-start | bytes 12296 | tf_op jit(solution)/shard_map/ppermute | solution.py:459

commit v5 on v4

--- a/solution.py
+++ b/solution.py
@@ -311,8 +311,9 @@
 def spread_taps(x):
     length = x.shape[1]
     column = lax.broadcasted_iota(jnp.int32, (1, length), 1)
-    before = jnp.where(column == 0, 0.0, pltpu.roll(x, 1, 1))
-    after = jnp.where(column == length - 1, 0.0, pltpu.roll(x, length - 1, 1))
+    zero = jnp.zeros_like(x)
+    before = jnp.where(column == 0, zero, pltpu.roll(x, 1, 1))
+    after = jnp.where(column == length - 1, zero, pltpu.roll(x, length - 1, 1))
     return before, x, after
 
 
@@ -374,10 +375,10 @@
             g = base + r - lead
             inside = jnp.logical_and(g >= 0, g < last)
             y = jnp.where(inside, jnp.maximum(total, 0.0), 0.0)
-            before, same, after = spread_taps(y)
-            target[r, :CONV] = before.astype(BF16)
-            target[r, CONV : 2 * CONV] = same.astype(BF16)
-            target[r, 2 * CONV :] = after.astype(BF16)
+            before, same, after = spread_taps(y.astype(BF16))
+            target[r, :CONV] = before
+            target[r, CONV : 2 * CONV] = same
+            target[r, 2 * CONV :] = after
 
         return finish
 

time: 31.5 us -> 31.5 us (level)
  no operation moved by 1% of the time
where the time goes in v5:
time: 31.5 us; the launch traced here: 31.3 us
  Pallas kernels  14.4 us (46%)
  starting transfers between devices  12.2 us (39%)
  waiting for transfers between devices  3.25 us (10%)
  between operations  0.83 us (3%)
  local copies, waits for them, and re-layouts  0.68 us (2%)
    ppermute x12, starting transfers between devices, swap(): return lax.ppermute(x, GROUP, [(i, i ^ k) for i in range(count)])  10.5 us
    pallas_call x3, Pallas kernels, attention(): pl.pallas_call(functools.partial(attention_kernel, cuts, chunk), name='at...  7.3 us
    pallas_call x3, Pallas kernels, pack(): pl.pallas_call(functools.partial(pack_kernel, chunk, cuts), name='pack',...  3.16 us
    pallas_call x1, Pallas kernels, convolutions(): pl.pallas_call(functools.partial(conv_kernel, group, hops), name='convolu...  3.08 us
    ppermute x12, waiting for transfers between devices, swap(): return lax.ppermute(x, GROUP, [(i, i ^ k) for i in range(count)])  2.07 us
    ppermute x2, starting transfers between devices, neighbours(): return lax.ppermute(x, ('grp',) + BANDS, targets)  1.66 us
    ppermute x2, waiting for transfers between devices, neighbours(): return lax.ppermute(x, ('grp',) + BANDS, targets)  1.19 us
    unnamed x22, local copies, waits for them, and re-layouts  0.68 us
  transfers between devices with their start and end apart: 14, of which 2 were waited for; matrix products, arithmetic and copies ran while one was open for 0% of the time, Pallas kernels for 28%

profile of v5, /device:TPU:0, one launch (start us, length us, event | category | flops | bytes accessed | tf_op | source)
XLA Modules:
  0.0 31.3 jit_solution(9878490045604381830)
XLA Ops:
  0.6 0.0 copy-start
  0.7 2.0 %pack.3 = (bf16[416,128]{1,0:T(8,128)(2,1)}, bf16[416,128]{1,0:T(8,128)(2,1)}, bf16[416,128]{1,0:T(8,128)(2,1)}, bf16[416,128]{1,0:T(8,128)(2,1)}) custom-call(bf16[2048,128]{1,0:T(8,128)(2,1)} %bitcast.5, bf16[2048,128]{1,0:T(8,128)(2,1)} %bitcast.8, f32[3,32,64]{2,1,0:T(8,128)} %image.5), custom_call_target="tpu_custom_call" | custom-call | tf_op jit(solution)/shard_map/pack/pallas_call | solution.py:164
  2.6 0.0 copy-start.3
  2.6 0.0 copy-start.4
  2.6 0.0 copy-start.5
  2.7 0.0 copy-start.6
  2.7 0.5 %collective-permute-start = (bf16[416,128]{1,0:T(8,128)(2,1)}, bf16[416,128]{1,0:T(8,128)(2,1)S(1)}, u32[]{:S(2)}, u32[]{:S(2)}) collective-permute-start(bf16[416,128]{1,0:T(8,128)(2,1)} %get-tuple-element.58), channel_id=1, source_target_pairs={{0,1},{1,0},{2,3},{3,2},{4,5},{5,4},{6,7},{7,6},{8,9},{9,8},{10,11... | collective-permute-start | bytes 319496 | tf_op jit(solution)/shard_map/ppermute | solution.py:460
  3.2 2.6 %collective-permute-start.7 = (bf16[416,128]{1,0:T(8,128)(2,1)}, bf16[416,128]{1,0:T(8,128)(2,1)S(1)}, u32[]{:S(2)}, u32[]{:S(2)}) collective-permute-start(bf16[416,128]{1,0:T(8,128)(2,1)} %get-tuple-element.89), channel_id=1, source_target_pairs={{0,2},{1,3},{2,0},{3,1},{4,6},{5,7},{6,4},{7,5},{8,10},{9,11},{10,... | collective-permute-start | bytes 319496 | tf_op jit(solution)/shard_map/ppermute | solution.py:460
  5.8 0.1 collective-permute-start.8
  5.8 0.0 collective-permute-done.refs_0_.refs_1_
  5.8 0.0 copy-done.1
  5.8 0.0 copy-start.7
  5.9 0.5 %pack.4 = (bf16[256,128]{1,0:T(8,128)(2,1)S(1)}, bf16[256,128]{1,0:T(8,128)(2,1)S(1)}, bf16[256,128]{1,0:T(8,128)(2,1)S(1)}, bf16[256,128]{1,0:T(8,128)(2,1)S(1)}) custom-call(bf16[2048,128]{1,0:T(8,128)(2,1)S(1)} %bitcast.6, bf16[2048,128]{1,0:T(8,128)(2,1)S(1)} %bitcast.9, f32[3,32,64]{2,1,0:T(8,128)S(1)} %copy-done.2, ...), custom_call_target="tpu_custom_call" | custom-call | tf_op jit(solution)/shard_map/pack/pallas_call | solution.py:164
  6.4 0.0 copy-start.8
  6.4 0.2 collective-permute-start.1
  6.6 0.0 copy-done.3
  6.6 0.4 %copy-done.8 = bf16[9,2,64]{2,1,0:T(2,128)(2,1)S(1)} copy-done((bf16[9,2,64]{2,1,0:T(2,128)(2,1)S(1)}, bf16[9,2,64]{2,1,0:T(2,128)(2,1)}, u32[]{:S(2)}) %copy-start.8) | copy-done | bytes 2328
  7.1 0.2 copy-done.9
  7.2 0.2 weights.1
  7.4 2.0 %collective-permute-start.5 = (bf16[256,128]{1,0:T(8,128)(2,1)S(1)}, bf16[256,128]{1,0:T(8,128)(2,1)S(1)}, u32[]{:S(2)}, u32[]{:S(2)}) collective-permute-start(bf16[256,128]{1,0:T(8,128)(2,1)S(1)} %get-tuple-element.86), channel_id=1, source_target_pairs={{0,2},{1,3},{2,0},{3,1},{4,6},{5,7},{6,4},{7,5},{8,10},{9,11},{10,... | collective-permute-start | bytes 196616 | tf_op jit(solution)/shard_map/ppermute | solution.py:460
  9.4 0.0 collective-permute-start.6
  9.5 0.0 collective-permute-done.1.refs_0_.refs_1_
  9.5 0.7 %pack.5 = (bf16[384,128]{1,0:T(8,128)(2,1)S(1)}, bf16[384,128]{1,0:T(8,128)(2,1)S(1)}, bf16[384,128]{1,0:T(8,128)(2,1)S(1)}, bf16[384,128]{1,0:T(8,128)(2,1)S(1)}) custom-call(bf16[2048,128]{1,0:T(8,128)(2,1)S(1)} %bitcast.7, bf16[2048,128]{1,0:T(8,128)(2,1)S(1)} %bitcast.10, f32[3,32,64]{2,1,0:T(8,128)S(1)} %copy-done.2, ...), custom_call_target="tpu_custom_call" | custom-call | tf_op jit(solution)/shard_map/pack/pallas_call | solution.py:164
  10.2 0.2 collective-permute-start.2
  10.4 0.0 collective-permute-done.7.refs_2_
  10.4 1.9 %collective-permute-start.3 = (bf16[384,128]{1,0:T(8,128)(2,1)S(1)}, bf16[384,128]{1,0:T(8,128)(2,1)S(1)}, u32[]{:S(2)}, u32[]{:S(2)}) collective-permute-start(bf16[384,128]{1,0:T(8,128)(2,1)S(1)} %get-tuple-element.62), channel_id=1, source_target_pairs={{0,2},{1,3},{2,0},{3,1},{4,6},{5,7},{6,4},{7,5},{8,10},{9,11},{10,... | collective-permute-start | bytes 294920 | tf_op jit(solution)/shard_map/ppermute | solution.py:460
  12.3 0.0 collective-permute-done.8.refs_3_
  12.3 1.1 %collective-permute-start.4 = (bf16[384,128]{1,0:T(8,128)(2,1)S(1)}, bf16[384,128]{1,0:T(8,128)(2,1)S(1)}, u32[]{:S(2)}, u32[]{:S(2)}) collective-permute-start(bf16[384,128]{1,0:T(8,128)(2,1)S(1)} %get-tuple-element.63), channel_id=1, source_target_pairs={{0,3},{1,2},{2,1},{3,0},{4,7},{5,6},{6,5},{7,4},{8,11},{9,10},{10,... | collective-permute-start | bytes 294920 | tf_op jit(solution)/shard_map/ppermute | solution.py:460
  13.4 2.7 %attention.3 = (bf16[8,8,256]{2,1,0:T(8,128)(2,1)S(1)}, f32[8,2,256]{2,1,0:T(2,128)S(1)}) custom-call(bf16[416,128]{1,0:T(8,128)(2,1)S(1)} %copy-done.10, bf16[416,128]{1,0:T(8,128)(2,1)S(1)} %collective-permute-done.refs_0_.refs_1_, bf16[416,128]{1,0:T(8,128)(2,1)S(1)} %collective-permute-done.7.refs_2_, ...), custom_call_target="tpu_custom_call" | custom-call | flops 805306368 | bytes 786432 | tf_op jit(solution)/shard_map/attention/pallas_call | solution.py:294
  16.1 0.0 collective-permute-done.5.refs_2_
  16.2 0.0 collective-permute-done.6.refs_3_
  16.2 1.9 %attention.4 = (bf16[8,8,256]{2,1,0:T(8,128)(2,1)S(1)}, f32[8,2,256]{2,1,0:T(2,128)S(1)}) custom-call(bf16[256,128]{1,0:T(8,128)(2,1)S(1)} %get-tuple-element.85.refs_0_, bf16[256,128]{1,0:T(8,128)(2,1)S(1)} %collective-permute-done.1.refs_0_.refs_1_, bf16[256,128]{1,0:T(8,128)(2,1)S(1)} %collective-permute-done.5.refs_2_, ...), custom_call_target="tpu_custom_call" | custom-call | flops 536870912 | bytes 524288 | tf_op jit(solution)/shard_map/attention/pallas_call | solution.py:294
  18.0 1.6 %collective-permute-start.10 = (bf16[8,8,256]{2,1,0:T(8,128)(2,1)S(1)}, bf16[8,8,256]{2,1,0:T(8,128)(2,1)S(1)}, u32[]{:S(2)}, u32[]{:S(2)}) collective-permute-start(bf16[8,8,256]{2,1,0:T(8,128)(2,1)S(1)} %get-tuple-element.93.refs_9_), channel_id=1, source_target_pairs={{0,16},{1,3},{3,1},{2,6},{6,2},{7,5},{5,7},{4,8},{8,4},{9,11},{11,... | collective-permute-start | bytes 98312 | tf_op jit(solution)/shard_map/ppermute | solution.py:480
  19.6 0.0 collective-permute-done.2.refs_1_
  19.6 0.0 collective-permute-done.3.refs_2_
  19.6 0.0 collective-permute-done.4.refs_3_
  19.7 2.7 %attention.5 = (bf16[8,8,256]{2,1,0:T(8,128)(2,1)S(1)}, f32[8,2,256]{2,1,0:T(2,128)S(1)}) custom-call(bf16[384,128]{1,0:T(8,128)(2,1)S(1)} %get-tuple-element.60.refs_0_, bf16[384,128]{1,0:T(8,128)(2,1)S(1)} %collective-permute-done.2.refs_1_, bf16[384,128]{1,0:T(8,128)(2,1)S(1)} %collective-permute-done.3.refs_2_, ...), custom_call_target="tpu_custom_call" | custom-call | flops 805306368 | bytes 786432 | tf_op jit(solution)/shard_map/attention/pallas_call | solution.py:294
  22.4 0.1 collective-permute-start.9
  22.5 0.0 collective-permute-done.10.refs_1_
  22.5 1.2 %collective-permute-done.9.refs_0_ = bf16[8,8,256]{2,1,0:T(8,128)(2,1)S(1)} collective-permute-done((bf16[8,8,256]{2,1,0:T(8,128)(2,1)S(1)}, bf16[8,8,256]{2,1,0:T(8,128)(2,1)S(1)}, u32[]{:S(2)}, u32[]{:S(2)}) %collective-permute-start.9) | collective-permute-done | bytes 32800 | tf_op jit(solution)/shard_map/ppermute | solution.py:480
  23.7 3.1 %convolutions.1 = (f32[2,8,64]{2,1,0:T(8,128)S(1)}, f32[2,8,64]{2,1,0:T(8,128)S(1)}, f32[2,8,64]{2,1,0:T(8,128)S(1)}, f32[2,8,64]{2,1,0:T(8,128)S(1)}) custom-call(bf16[8,8,256]{2,1,0:T(8,128)(2,1)S(1)} %get-tuple-element.95.own, f32[8,2,256]{2,1,0:T(2,128)S(1)} %get-tuple-element.96.maps, bf16[8,8,256]{2,1,0:T(8,128)(2,1)S(1)} %collective-permute-done.9.refs_0_, ...), custom_call_target="tpu_custom_call" | custom-call | tf_op jit(solution)/shard_map/convolutions/pallas_call | solution.py:417
  26.7 0.2 collective-permute-start.11
  26.9 0.6 %collective-permute-start.12 = (f32[2,8,64]{2,1,0:T(8,128)S(1)}, f32[2,8,64]{2,1,0:T(8,128)S(1)}, u32[]{:S(2)}, u32[]{:S(2)}) collective-permute-start(f32[2,8,64]{2,1,0:T(8,128)S(1)} %get-tuple-element.104), channel_id=1, source_target_pairs={{0,2},{1,3},{2,0},{3,1},{4,6},{5,7},{6,4},{7,5},{8,10},{9,11},{10,... | collective-permute-start | bytes 12296 | tf_op jit(solution)/shard_map/ppermute | solution.py:460
  27.5 1.1 %collective-permute-start.13 = (f32[2,8,64]{2,1,0:T(8,128)S(1)}, f32[2,8,64]{2,1,0:T(8,128)S(1)}, u32[]{:S(2)}, u32[]{:S(2)}) collective-permute-start(f32[2,8,64]{2,1,0:T(8,128)S(1)} %get-tuple-element.105), channel_id=1, source_target_pairs={{0,3},{1,2},{2,1},{3,0},{4,7},{5,6},{6,5},{7,4},{8,11},{9,10},{10,... | collective-permute-start | bytes 12296 | tf_op jit(solution)/shard_map/ppermute | solution.py:460
  28.6 0.0 collective-permute-done.11.refs_1_
  28.6 2.0 %collective-permute-done.12.refs_2_ = f32[2,8,64]{2,1,0:T(8,128)S(1)} collective-permute-done((f32[2,8,64]{2,1,0:T(8,128)S(1)}, f32[2,8,64]{2,1,0:T(8,128)S(1)}, u32[]{:S(2)}, u32[]{:S(2)}) %collective-permute-start.12) | collective-permute-done | bytes 4128 | tf_op jit(solution)/shard_map/ppermute | solution.py:460
  30.7 0.0 collective-permute-done.13.refs_3_
  30.7 0.6 %place.1 = (f32[32,64]{1,0:T(8,128)}, f32[32,64]{1,0:T(8,128)}) custom-call(f32[2,8,64]{2,1,0:T(8,128)S(1)} %get-tuple-element.102.refs_0_, f32[2,8,64]{2,1,0:T(8,128)S(1)} %collective-permute-done.11.refs_1_, f32[2,8,64]{2,1,0:T(8,128)S(1)} %collective-permute-done.12.refs_2_, f32[2,8,64]{2,1,0:T(8,128)S(1)} %collective-permute-done.13.refs_3_), custom_call_target="tpu_custom_call" | custom-call | tf_op jit(solution)/shard_map/place/pallas_call | solution.py:448
  (11 shorter events, 0.0 us)
Async XLA Ops:
  0.6 5.2 %copy-start = (bf16[32,64,128]{2,1,0:T(8,128)(2,1)S(1)}, bf16[32,64,128]{2,1,0:T(8,128)(2,1)}, u32[]{:S(2)}) copy-start(bf16[32,64,128]{2,1,0:T(8,128)(2,1)} %param.10) | copy-start | bytes 1572868
  0.6 5.2 %copy-start.1 = (bf16[32,64,128]{2,1,0:T(8,128)(2,1)S(1)}, bf16[32,64,128]{2,1,0:T(8,128)(2,1)}, u32[]{:S(2)}) copy-start(bf16[32,64,128]{2,1,0:T(8,128)(2,1)} %param.11) | copy-start | bytes 1572868
  0.6 5.2 %copy-start.2 = (f32[3,32,64]{2,1,0:T(8,128)S(1)}, f32[3,32,64]{2,1,0:T(8,128)}, u32[]{:S(2)}) copy-start(f32[3,32,64]{2,1,0:T(8,128)} %image.5) | copy-start | bytes 73732
  2.6 4.0 %copy-start.3 = (bf16[3,9,64,64]{3,2,1,0:T(8,128)(2,1)S(1)}, bf16[3,9,64,64]{3,2,1,0:T(8,128)(2,1)}, u32[]{:S(2)}) copy-start(bf16[3,9,64,64]{3,2,1,0:T(8,128)(2,1)} %param.18) | copy-start | bytes 663556
  2.6 4.0 %copy-start.4 = (bf16[128,128]{1,0:T(8,128)(2,1)S(1)}, bf16[128,128]{1,0:T(8,128)(2,1)}, u32[]{:S(2)}) copy-start(bf16[128,128]{1,0:T(8,128)(2,1)} %value) | copy-start | bytes 98308
  2.6 4.0 %copy-start.5 = (bf16[128,128]{1,0:T(8,128)(2,1)S(1)}, bf16[128,128]{1,0:T(8,128)(2,1)}, u32[]{:S(2)}) copy-start(bf16[128,128]{1,0:T(8,128)(2,1)} %out) | copy-start | bytes 98308
  2.7 3.9 %copy-start.6 = (bf16[128,128]{1,0:T(8,128)(2,1)S(1)}, bf16[128,128]{1,0:T(8,128)(2,1)}, u32[]{:S(2)}) copy-start(bf16[128,128]{1,0:T(8,128)(2,1)} %refs_5_.2) | copy-start | bytes 98308
  2.7 3.2 %collective-permute-start = (bf16[416,128]{1,0:T(8,128)(2,1)}, bf16[416,128]{1,0:T(8,128)(2,1)S(1)}, u32[]{:S(2)}, u32[]{:S(2)}) collective-permute-start(bf16[416,128]{1,0:T(8,128)(2,1)} %get-tuple-element.58), channel_id=1, source_target_pairs={{0,1},{1,0},{2,3},{3,2},{4,5},{5,4},{6,7},{7,6},{8,9},{9,8},{10,11... | collective-permute-start | bytes 319496 | tf_op jit(solution)/shard_map/ppermute | solution.py:460
  3.2 7.2 %collective-permute-start.7 = (bf16[416,128]{1,0:T(8,128)(2,1)}, bf16[416,128]{1,0:T(8,128)(2,1)S(1)}, u32[]{:S(2)}, u32[]{:S(2)}) collective-permute-start(bf16[416,128]{1,0:T(8,128)(2,1)} %get-tuple-element.89), channel_id=1, source_target_pairs={{0,2},{1,3},{2,0},{3,1},{4,6},{5,7},{6,4},{7,5},{8,10},{9,11},{10,... | collective-permute-start | bytes 319496 | tf_op jit(solution)/shard_map/ppermute | solution.py:460
  5.8 6.6 %collective-permute-start.8 = (bf16[416,128]{1,0:T(8,128)(2,1)}, bf16[416,128]{1,0:T(8,128)(2,1)S(1)}, u32[]{:S(2)}, u32[]{:S(2)}) collective-permute-start(bf16[416,128]{1,0:T(8,128)(2,1)} %get-tuple-element.90), channel_id=1, source_target_pairs={{0,3},{1,2},{2,1},{3,0},{4,7},{5,6},{6,5},{7,4},{8,11},{9,10},{10,... | collective-permute-start | bytes 319496 | tf_op jit(solution)/shard_map/ppermute | solution.py:460
  5.8 0.8 %copy-start.7 = (bf16[9,64,5]{1,2,0:T(8,128)(2,1)S(1)}, bf16[9,64,5]{1,2,0:T(8,128)(2,1)}, u32[]{:S(2)}) copy-start(bf16[9,64,5]{1,2,0:T(8,128)(2,1)} %param.17) | copy-start | bytes 17284
  6.4 0.7 %copy-start.8 = (bf16[9,2,64]{2,1,0:T(2,128)(2,1)S(1)}, bf16[9,2,64]{2,1,0:T(2,128)(2,1)}, u32[]{:S(2)}) copy-start(bf16[9,2,64]{2,1,0:T(2,128)(2,1)} %last) | copy-start | bytes 6916
  6.4 3.1 %collective-permute-start.1 = (bf16[256,128]{1,0:T(8,128)(2,1)S(1)}, bf16[256,128]{1,0:T(8,128)(2,1)S(1)}, u32[]{:S(2)}, u32[]{:S(2)}) collective-permute-start(bf16[256,128]{1,0:T(8,128)(2,1)S(1)} %get-tuple-element.59), channel_id=1, source_target_pairs={{0,1},{1,0},{2,3},{3,2},{4,5},{5,4},{6,7},{7,6},{8,9},{9,8},{10,11... | collective-permute-start | bytes 196616 | tf_op jit(solution)/shard_map/ppermute | solution.py:460
  6.6 0.7 %copy-start.9 = (f32[128]{0:T(128)S(1)}, f32[128]{0:T(128)}, u32[]{:S(2)}) copy-start(f32[128]{0:T(128)} %param.16) | copy-start | bytes 1540
  7.4 8.7 %collective-permute-start.5 = (bf16[256,128]{1,0:T(8,128)(2,1)S(1)}, bf16[256,128]{1,0:T(8,128)(2,1)S(1)}, u32[]{:S(2)}, u32[]{:S(2)}) collective-permute-start(bf16[256,128]{1,0:T(8,128)(2,1)S(1)} %get-tuple-element.86), channel_id=1, source_target_pairs={{0,2},{1,3},{2,0},{3,1},{4,6},{5,7},{6,4},{7,5},{8,10},{9,11},{10,... | collective-permute-start | bytes 196616 | tf_op jit(solution)/shard_map/ppermute | solution.py:460
  9.4 4.0 %copy-start.10 = (bf16[416,128]{1,0:T(8,128)(2,1)S(1)}, bf16[416,128]{1,0:T(8,128)(2,1)}, u32[]{:S(2)}) copy-start(bf16[416,128]{1,0:T(8,128)(2,1)} %get-tuple-element.88.refs_0_) | copy-start | bytes 319492
  9.4 6.7 %collective-permute-start.6 = (bf16[256,128]{1,0:T(8,128)(2,1)S(1)}, bf16[256,128]{1,0:T(8,128)(2,1)S(1)}, u32[]{:S(2)}, u32[]{:S(2)}) collective-permute-start(bf16[256,128]{1,0:T(8,128)(2,1)S(1)} %get-tuple-element.87), channel_id=1, source_target_pairs={{0,3},{1,2},{2,1},{3,0},{4,7},{5,6},{6,5},{7,4},{8,11},{9,10},{10,... | collective-permute-start | bytes 196616 | tf_op jit(solution)/shard_map/ppermute | solution.py:460
  10.2 9.5 %collective-permute-start.2 = (bf16[384,128]{1,0:T(8,128)(2,1)S(1)}, bf16[384,128]{1,0:T(8,128)(2,1)S(1)}, u32[]{:S(2)}, u32[]{:S(2)}) collective-permute-start(bf16[384,128]{1,0:T(8,128)(2,1)S(1)} %get-tuple-element.61), channel_id=1, source_target_pairs={{0,1},{1,0},{2,3},{3,2},{4,5},{5,4},{6,7},{7,6},{8,9},{9,8},{10,11... | collective-permute-start | bytes 294920 | tf_op jit(solution)/shard_map/ppermute | solution.py:460
  10.4 9.3 %collective-permute-start.3 = (bf16[384,128]{1,0:T(8,128)(2,1)S(1)}, bf16[384,128]{1,0:T(8,128)(2,1)S(1)}, u32[]{:S(2)}, u32[]{:S(2)}) collective-permute-start(bf16[384,128]{1,0:T(8,128)(2,1)S(1)} %get-tuple-element.62), channel_id=1, source_target_pairs={{0,2},{1,3},{2,0},{3,1},{4,6},{5,7},{6,4},{7,5},{8,10},{9,11},{10,... | collective-permute-start | bytes 294920 | tf_op jit(solution)/shard_map/ppermute | solution.py:460
  12.3 7.3 %collective-permute-start.4 = (bf16[384,128]{1,0:T(8,128)(2,1)S(1)}, bf16[384,128]{1,0:T(8,128)(2,1)S(1)}, u32[]{:S(2)}, u32[]{:S(2)}) collective-permute-start(bf16[384,128]{1,0:T(8,128)(2,1)S(1)} %get-tuple-element.63), channel_id=1, source_target_pairs={{0,3},{1,2},{2,1},{3,0},{4,7},{5,6},{6,5},{7,4},{8,11},{9,10},{10,... | collective-permute-start | bytes 294920 | tf_op jit(solution)/shard_map/ppermute | solution.py:460
  18.0 4.4 %collective-permute-start.10 = (bf16[8,8,256]{2,1,0:T(8,128)(2,1)S(1)}, bf16[8,8,256]{2,1,0:T(8,128)(2,1)S(1)}, u32[]{:S(2)}, u32[]{:S(2)}) collective-permute-start(bf16[8,8,256]{2,1,0:T(8,128)(2,1)S(1)} %get-tuple-element.93.refs_9_), channel_id=1, source_target_pairs={{0,16},{1,3},{3,1},{2,6},{6,2},{7,5},{5,7},{4,8},{8,4},{9,11},{11,... | collective-permute-start | bytes 98312 | tf_op jit(solution)/shard_map/ppermute | solution.py:480
  22.4 1.3 %collective-permute-start.9 = (bf16[8,8,256]{2,1,0:T(8,128)(2,1)S(1)}, bf16[8,8,256]{2,1,0:T(8,128)(2,1)S(1)}, u32[]{:S(2)}, u32[]{:S(2)}) collective-permute-start(bf16[8,8,256]{2,1,0:T(8,128)(2,1)S(1)} %get-tuple-element.95.own), channel_id=1, source_target_pairs={{0,1},{1,0},{3,2},{2,3},{6,7},{7,6},{5,4},{4,5},{8,9},{9,8},{11,10... | collective-permute-start | bytes 98312 | tf_op jit(solution)/shard_map/ppermute | solution.py:480
  26.7 1.9 %collective-permute-start.11 = (f32[2,8,64]{2,1,0:T(8,128)S(1)}, f32[2,8,64]{2,1,0:T(8,128)S(1)}, u32[]{:S(2)}, u32[]{:S(2)}) collective-permute-start(f32[2,8,64]{2,1,0:T(8,128)S(1)} %get-tuple-element.103), channel_id=1, source_target_pairs={{0,1},{1,0},{2,3},{3,2},{4,5},{5,4},{6,7},{7,6},{8,9},{9,8},{10,11... | collective-permute-start | bytes 12296 | tf_op jit(solution)/shard_map/ppermute | solution.py:460
  26.9 3.7 %collective-permute-start.12 = (f32[2,8,64]{2,1,0:T(8,128)S(1)}, f32[2,8,64]{2,1,0:T(8,128)S(1)}, u32[]{:S(2)}, u32[]{:S(2)}) collective-permute-start(f32[2,8,64]{2,1,0:T(8,128)S(1)} %get-tuple-element.104), channel_id=1, source_target_pairs={{0,2},{1,3},{2,0},{3,1},{4,6},{5,7},{6,4},{7,5},{8,10},{9,11},{10,... | collective-permute-start | bytes 12296 | tf_op jit(solution)/shard_map/ppermute | solution.py:460
  27.5 3.2 %collective-permute-start.13 = (f32[2,8,64]{2,1,0:T(8,128)S(1)}, f32[2,8,64]{2,1,0:T(8,128)S(1)}, u32[]{:S(2)}, u32[]{:S(2)}) collective-permute-start(f32[2,8,64]{2,1,0:T(8,128)S(1)} %get-tuple-element.105), channel_id=1, source_target_pairs={{0,3},{1,2},{2,1},{3,0},{4,7},{5,6},{6,5},{7,4},{8,11},{9,10},{10,... | collective-permute-start | bytes 12296 | tf_op jit(solution)/shard_map/ppermute | solution.py:460
